TPU v7x, 32 devices: a whole 2x2x4 slice. The times are simulated.
32 devices in a mesh: energy: 8 (over y, x, core), space: 4 (over z).
Axes of the slice: x: 2, y: 2, z: 4, core: 2. Of those that a mesh axis runs over, the one named last changes fastest.
Arguments:
- green0: float32 [16, 8, 2, 128, 128], P('energy', 'space'), may hold values from -6 to 6
- grad_h: float32 [8, 8, 128, 128], P('space'), may hold values from -0.5 to 0.5
- neighbours: int32 [8, 8], P('space'), may hold values from 0 to 7, as said below
- shifts: int32 [4], replicated, may hold values from -2 to 2, as said below
- coupling: float32 [4], replicated, may hold values from 0.0002 to 0.0006
Outputs:
- green: float32 [16, 8, 2, 128, 128], P('energy', 'space')
Inputs may be any that keep to these rules, and one draw needn't show every extreme that they name: |neighbours[a, k] - a| <= 2; entry 0 of atom a is max(a - 2, 0) and entry 1 is min(a + 2, 7). The values 2 and -2 each stand at some position of shifts.
All inputs are finite; a program needn't handle non-finite values.
Results may differ from a plain program's by a relative error of at most 0.0001.
Values sent between devices are 32-bit elements; how exact they have to be, the bound alone decides.
No kernel may reach another device: no remote copies, remote signals or barrier semaphores. Data moves between devices by JAX's collectives and lax.ppermute only.
A program may use at most 64 MiB of HBM per device.

v0:
```python
import jax
import jax.numpy as jnp
from jax import lax
from jax.sharding import PartitionSpec as P

SHIFTS = 4
REACH = 2
ITERS = 2


def with_halo(cells, sides, width):
    for axis, dim in sides:
        count = lax.axis_size(axis)
        ends = count - 1
        head = lax.slice_in_dim(cells, 0, width, axis=dim)
        tail = lax.slice_in_dim(cells, cells.shape[dim] - width, cells.shape[dim], axis=dim)
        cells = jnp.concatenate(
            [
                lax.ppermute(tail, axis, [(i, (i + 1) % count) for i in range(ends)]),
                cells,
                lax.ppermute(head, axis, [((i + 1) % count, i) for i in range(ends)]),
            ],
            axis=dim,
        )
    return cells


def complex_mul(left, right):
    highest = lax.Precision.HIGHEST
    lre, lim = (left[:, :, 0], left[:, :, 1])
    rre, rim = (right[:, :, 0], right[:, :, 1])
    real = jnp.einsum("eaij,eajk->eaik", lre, rre, precision=highest) - jnp.einsum(
        "eaij,eajk->eaik", lim, rim, precision=highest
    )
    imag = jnp.einsum("eaij,eajk->eaik", lre, rim, precision=highest) + jnp.einsum(
        "eaij,eajk->eaik", lim, rre, precision=highest
    )
    return jnp.stack([real, imag], axis=2)


def sandwich(grad_h, picked):
    highest = lax.Precision.HIGHEST
    left = jnp.einsum("akij,eakcjl->eakcil", grad_h, picked, precision=highest)
    return jnp.einsum("eakcil,akml->eacim", left, grad_h, precision=highest)


def shift_total(extended, shifts, coupling, e_count):
    total = jnp.zeros((e_count,) + extended.shape[1:], jnp.float32)
    for shift_index in range(SHIFTS):
        start = REACH + shifts[shift_index]
        total = total + coupling[shift_index] * lax.dynamic_slice_in_dim(
            extended, start, e_count, 0
        )
    return total


def per_device(green0, grad_h, neighbours, shifts, coupling):
    e_count = green0.shape[0]
    a_count = green0.shape[1]
    first_atom = lax.axis_index("space") * a_count
    local_index = neighbours - first_atom + REACH
    green = green0
    for step in range(ITERS):
        beside = with_halo(green, (("space", 1),), REACH)
        inner = sandwich(grad_h, beside[:, local_index])
        widened = with_halo(inner, (("energy", 0),), REACH)
        sigma = shift_total(widened, shifts, coupling, e_count)
        green = green0 + complex_mul(complex_mul(green0, sigma), green0)
    return green


def solution(mesh):
    return jax.shard_map(
        per_device,
        mesh=mesh,
        in_specs=(
            P("energy", "space", None, None, None),
            P("space", None, None, None),
            P("space", None),
            P(),
            P(),
        ),
        out_specs=P("energy", "space", None, None, None),
        check_vma=False,
    )
```

profile of v0, /device:TPU:12, one launch (start us, length us, event | category | flops | bytes accessed | tf_op | source)
XLA Modules:
  0.0 106.3 jit_solution(6648903398025500262)
XLA Ops:
  0.0 2.5 %collective-permute-start.1 = (f32[2,2,2,128,128]{4,3,2,1,0:T(8,128)}, f32[2,2,2,128,128]{4,3,2,1,0:T(8,128)S(1)}, u32[]{:S(2)}, u32[]{:S(2)}) collective-permute-start(f32[2,2,2,128,128]{4,3,2,1,0:T(8,128)} %param.5), channel_id=1, source_target_pairs={{1,0},{2,1},{3,2},{5,4},{6,5},{7,6},{9,8},{10,9},{11,10},{13,12},{... | collective-permute-start | bytes 1572872 | tf_op jit(solution)/shard_map/ppermute | solution.py:21
  2.5 3.5 %collective-permute-start = (f32[2,2,2,128,128]{4,3,2,1,0:T(8,128)}, f32[2,2,2,128,128]{4,3,2,1,0:T(8,128)}, u32[]{:S(2)}, u32[]{:S(2)}) collective-permute-start(f32[2,2,2,128,128]{4,3,2,1,0:T(8,128)} %param.5), channel_id=1, source_target_pairs={{0,1},{1,2},{2,3},{4,5},{5,6},{6,7},{8,9},{9,10},{10,11},{12,13},{... | collective-permute-start | bytes 1572872 | tf_op jit(solution)/shard_map/ppermute | solution.py:19
  6.0 0.7 compare_select_fusion
  6.8 9.1 %collective-permute-done.1 = f32[2,2,2,128,128]{4,3,2,1,0:T(8,128)S(1)} collective-permute-done((f32[2,2,2,128,128]{4,3,2,1,0:T(8,128)}, f32[2,2,2,128,128]{4,3,2,1,0:T(8,128)S(1)}, u32[]{:S(2)}, u32[]{:S(2)}) %collective-permute-start.1) | collective-permute-done | bytes 524320 | tf_op jit(solution)/shard_map/ppermute | solution.py:21
  15.9 2.2 %collective-permute-done = f32[2,2,2,128,128]{4,3,2,1,0:T(8,128)} collective-permute-done((f32[2,2,2,128,128]{4,3,2,1,0:T(8,128)}, f32[2,2,2,128,128]{4,3,2,1,0:T(8,128)}, u32[]{:S(2)}, u32[]{:S(2)}) %collective-permute-start) | collective-permute-done | bytes 524320 | tf_op jit(solution)/shard_map/ppermute | solution.py:19
  18.1 1.3 %pad_maximum_fusion = f32[2,6,2,128,128]{4,3,2,1,0:T(8,128)S(1)} fusion(f32[2,2,2,128,128]{4,3,2,1,0:T(8,128)S(1)} %collective-permute-done.1, f32[2,2,2,128,128]{4,3,2,1,0:T(8,128)} %param.5, f32[2,2,2,128,128]{4,3,2,1,0:T(8,128)} %collective-permute-done), kind=kLoop, calls=%fused_computation.10 | loop fusion | flops 786432 | bytes 3145728 | tf_op jit(solution)/shard_map/concatenate | solution.py:17
  19.4 2.8 %gather_fusion = f32[16,2,2,128,128]{4,3,2,1,0:T(8,128)} fusion(f32[2,6,2,128,128]{4,3,2,1,0:T(8,128)S(1)} %pad_maximum_fusion, s32[1024]{0:T(1024)S(1)} %pad_clamp_fusion), kind=kCustom, calls=%fused_computation | custom fusion | bytes 8388672 | tf_op jit(solution)/shard_map/gather | solution.py:65
  22.2 5.5 %fusion.6 = f32[2,8,2,2,128,128]{4,5,1,3,2,0:T(8,128)S(1)} fusion(f32[2,2,8,2,128,128]{5,4,3,0,2,1:T(8,128)} %bitcast.94, f32[2,8,128,128]{3,2,1,0:T(8,128)S(1)} %copy-done), kind=kOutput, calls=%fused_computation.8 | convolution fusion | flops 1610612736 | bytes 9437184 | tf_op jit(solution)/shard_map/akij,eakcjl->eakcil/dot_general | solution.py:43
  27.7 3.6 %fusion.8 = f32[2,2,2,128,128]{4,3,2,0,1:T(8,128)S(1)} fusion(f32[2,8,2,2,128,128]{4,5,1,3,2,0:T(8,128)S(1)} %fusion.6, f32[2,8,128,128]{3,2,1,0:T(8,128)S(1)} %copy-done), kind=kOutput, calls=%fused_computation.14 | convolution fusion | flops 1610612736 | bytes 5767168 | tf_op jit(solution)/shard_map/eakcil,akml->eacim/dot_general | solution.py:44
  31.4 1.9 %collective-permute-start.3 = (f32[2,2,2,128,128]{4,3,2,0,1:T(8,128)S(1)}, f32[2,2,2,128,128]{4,3,2,0,1:T(8,128)S(1)}, u32[]{:S(2)}, u32[]{:S(2)}) collective-permute-start(f32[2,2,2,128,128]{4,3,2,0,1:T(8,128)S(1)} %fusion.8), channel_id=1, source_target_pairs={{4,0},{8,4},{12,8},{16,12},{20,16},{24,20},{28,24},{5,1},{9,5},{13... | collective-permute-start | bytes 1572872 | tf_op jit(solution)/shard_map/ppermute | solution.py:21
  33.3 2.4 %collective-permute-start.2 = (f32[2,2,2,128,128]{4,3,2,0,1:T(8,128)S(1)}, f32[2,2,2,128,128]{4,3,2,0,1:T(8,128)S(1)}, u32[]{:S(2)}, u32[]{:S(2)}) collective-permute-start(f32[2,2,2,128,128]{4,3,2,0,1:T(8,128)S(1)} %fusion.8), channel_id=1, source_target_pairs={{0,4},{4,8},{8,12},{12,16},{16,20},{20,24},{24,28},{1,5},{5,9},{9,... | collective-permute-start | bytes 1572872 | tf_op jit(solution)/shard_map/ppermute | solution.py:19
  35.7 0.7 fusion.39
  41.3 0.7 fusion.38
  42.0 0.8 collective-permute-done.3
  42.8 4.7 %collective-permute-done.2 = f32[2,2,2,128,128]{4,3,2,0,1:T(8,128)S(1)} collective-permute-done((f32[2,2,2,128,128]{4,3,2,0,1:T(8,128)S(1)}, f32[2,2,2,128,128]{4,3,2,0,1:T(8,128)S(1)}, u32[]{:S(2)}, u32[]{:S(2)}) %collective-permute-start.2) | collective-permute-done | bytes 524320 | tf_op jit(solution)/shard_map/ppermute | solution.py:19
  47.7 2.7 %multiply_add_fusion.1 = f32[2,2,2,128,128]{4,3,2,0,1:T(8,128)S(1)} fusion(f32[6,2,2,128,128]{4,3,2,0,1:T(8,128)S(1)} %pad_maximum_fusion.1, s32[]{:T(128)S(6)} %select_n.24, s32[]{:T(128)S(6)} %select_n.23, s32[]{:T(128)S(6)} %select_n.22, s32[]{:T(128)S(6)} %select_n.21, f32[]{:T(128)} %bitcast.18, f32[]{:T(128)} %bitcast.15, f32[]{:T(128)} %bitcast.12, ...), kind=kLoop, calls=%fused_computation.35 | loop fusion | flops 917504 | bytes 2621472 | tf_op jit(solution)/shard_map/add | solution.py:51
  51.7 0.6 convolution_subtract_fusion.3
  55.4 1.9 %collective-permute-start.5 = (f32[2,2,2,128,128]{4,3,1,0,2:T(8,128)S(1)}, f32[2,2,2,128,128]{4,3,1,0,2:T(8,128)S(1)}, u32[]{:S(2)}, u32[]{:S(2)}) collective-permute-start(f32[2,2,2,128,128]{4,3,1,0,2:T(8,128)S(1)} %maximum_add_fusion), channel_id=1, source_target_pairs={{1,0},{2,1},{3,2},{5,4},{6,5},{7,6},{9,8},{10,9},{11,10},{13,12},{... | collective-permute-start | bytes 1572872 | tf_op jit(solution)/shard_map/ppermute | solution.py:21
  57.4 4.1 %collective-permute-start.4 = (f32[2,2,2,128,128]{4,3,1,0,2:T(8,128)S(1)}, f32[2,2,2,128,128]{4,3,1,0,2:T(8,128)S(1)}, u32[]{:S(2)}, u32[]{:S(2)}) collective-permute-start(f32[2,2,2,128,128]{4,3,1,0,2:T(8,128)S(1)} %maximum_add_fusion), channel_id=1, source_target_pairs={{0,1},{1,2},{2,3},{4,5},{5,6},{6,7},{8,9},{9,10},{10,11},{12,13},{... | collective-permute-start | bytes 1572872 | tf_op jit(solution)/shard_map/ppermute | solution.py:19
  61.5 7.9 %collective-permute-done.5 = f32[2,2,2,128,128]{4,3,1,0,2:T(8,128)S(1)} collective-permute-done((f32[2,2,2,128,128]{4,3,1,0,2:T(8,128)S(1)}, f32[2,2,2,128,128]{4,3,1,0,2:T(8,128)S(1)}, u32[]{:S(2)}, u32[]{:S(2)}) %collective-permute-start.5) | collective-permute-done | bytes 524320 | tf_op jit(solution)/shard_map/ppermute | solution.py:21
  69.4 1.9 %collective-permute-done.4 = f32[2,2,2,128,128]{4,3,1,0,2:T(8,128)S(1)} collective-permute-done((f32[2,2,2,128,128]{4,3,1,0,2:T(8,128)S(1)}, f32[2,2,2,128,128]{4,3,1,0,2:T(8,128)S(1)}, u32[]{:S(2)}, u32[]{:S(2)}) %collective-permute-start.4) | collective-permute-done | bytes 524320 | tf_op jit(solution)/shard_map/ppermute | solution.py:19
  71.5 2.8 %gather_fusion.1 = f32[16,2,2,128,128]{4,3,1,2,0:T(8,128)} fusion(f32[2,6,2,128,128]{4,3,1,0,2:T(8,128)S(1)} %pad_maximum_fusion.2, s32[1024]{0:T(1024)S(1)} %pad_clamp_fusion), kind=kCustom, calls=%fused_computation.1 | custom fusion | bytes 8388672 | tf_op jit(solution)/shard_map/gather | solution.py:65
  74.2 5.5 %fusion.4 = f32[2,8,2,2,128,128]{4,5,1,3,2,0:T(8,128)S(1)} fusion(f32[2,2,8,2,128,128]{5,4,0,3,2,1:T(8,128)} %bitcast.93, f32[2,8,128,128]{3,2,1,0:T(8,128)S(1)} %copy-done), kind=kOutput, calls=%fused_computation.6 | convolution fusion | flops 1610612736 | bytes 9437184 | tf_op jit(solution)/shard_map/akij,eakcjl->eakcil/dot_general | solution.py:43
  79.7 3.7 %fusion.11 = f32[2,2,2,128,128]{4,3,2,0,1:T(8,128)S(1)} fusion(f32[2,8,2,2,128,128]{4,5,1,3,2,0:T(8,128)S(1)} %fusion.4, f32[2,8,128,128]{3,2,1,0:T(8,128)S(1)} %copy-done), kind=kOutput, calls=%fused_computation.15 | convolution fusion | flops 1610612736 | bytes 5767168 | tf_op jit(solution)/shard_map/eakcil,akml->eacim/dot_general | solution.py:44
  83.4 1.9 %collective-permute-start.7 = (f32[2,2,2,128,128]{4,3,2,0,1:T(8,128)S(1)}, f32[2,2,2,128,128]{4,3,2,0,1:T(8,128)S(1)}, u32[]{:S(2)}, u32[]{:S(2)}) collective-permute-start(f32[2,2,2,128,128]{4,3,2,0,1:T(8,128)S(1)} %fusion.11), channel_id=1, source_target_pairs={{4,0},{8,4},{12,8},{16,12},{20,16},{24,20},{28,24},{5,1},{9,5},{13... | collective-permute-start | bytes 1572872 | tf_op jit(solution)/shard_map/ppermute | solution.py:21
  85.3 2.4 %collective-permute-start.6 = (f32[2,2,2,128,128]{4,3,2,0,1:T(8,128)S(1)}, f32[2,2,2,128,128]{4,3,2,0,1:T(8,128)S(1)}, u32[]{:S(2)}, u32[]{:S(2)}) collective-permute-start(f32[2,2,2,128,128]{4,3,2,0,1:T(8,128)S(1)} %fusion.11), channel_id=1, source_target_pairs={{0,4},{4,8},{8,12},{12,16},{16,20},{20,24},{24,28},{1,5},{5,9},{9,... | collective-permute-start | bytes 1572872 | tf_op jit(solution)/shard_map/ppermute | solution.py:19
  87.7 8.1 %collective-permute-done.7 = f32[2,2,2,128,128]{4,3,2,0,1:T(8,128)S(1)} collective-permute-done((f32[2,2,2,128,128]{4,3,2,0,1:T(8,128)S(1)}, f32[2,2,2,128,128]{4,3,2,0,1:T(8,128)S(1)}, u32[]{:S(2)}, u32[]{:S(2)}) %collective-permute-start.7) | collective-permute-done | bytes 524320 | tf_op jit(solution)/shard_map/ppermute | solution.py:21
  95.9 1.7 %collective-permute-done.6 = f32[2,2,2,128,128]{4,3,2,0,1:T(8,128)S(1)} collective-permute-done((f32[2,2,2,128,128]{4,3,2,0,1:T(8,128)S(1)}, f32[2,2,2,128,128]{4,3,2,0,1:T(8,128)S(1)}, u32[]{:S(2)}, u32[]{:S(2)}) %collective-permute-start.6) | collective-permute-done | bytes 524320 | tf_op jit(solution)/shard_map/ppermute | solution.py:19
  97.8 2.7 %multiply_add_fusion = f32[2,2,2,128,128]{4,3,2,0,1:T(8,128)S(1)} fusion(f32[6,2,2,128,128]{4,3,2,0,1:T(8,128)S(1)} %pad_maximum_fusion.3, s32[]{:T(128)S(6)} %select_n.24, s32[]{:T(128)S(6)} %select_n.23, s32[]{:T(128)S(6)} %select_n.22, s32[]{:T(128)S(6)} %select_n.21, f32[]{:T(128)} %bitcast.18, f32[]{:T(128)} %bitcast.15, f32[]{:T(128)} %bitcast.12, f32[]{:T(128)} %bitcast), kind=kLoop, calls=%fused_computation.34 | loop fusion | flops 917504 | bytes 2621472 | tf_op jit(solution)/shard_map/add | solution.py:51
  101.7 0.6 convolution_subtract_fusion.1
  103.5 0.6 convolution_add_fusion.1
  105.5 0.8 copy.26
  (30 shorter events, 8.6 us)
Async XLA Ops:
  0.0 22.2 %copy-start = (f32[2,8,128,128]{3,2,1,0:T(8,128)S(1)}, f32[2,8,128,128]{3,2,1,0:T(8,128)}, u32[]{:S(2)}) copy-start(f32[2,8,128,128]{3,2,1,0:T(8,128)} %param.6) | copy-start | bytes 3145732
  0.0 15.9 %collective-permute-start.1 = (f32[2,2,2,128,128]{4,3,2,1,0:T(8,128)}, f32[2,2,2,128,128]{4,3,2,1,0:T(8,128)S(1)}, u32[]{:S(2)}, u32[]{:S(2)}) collective-permute-start(f32[2,2,2,128,128]{4,3,2,1,0:T(8,128)} %param.5), channel_id=1, source_target_pairs={{1,0},{2,1},{3,2},{5,4},{6,5},{7,6},{9,8},{10,9},{11,10},{13,12},{... | collective-permute-start | bytes 1572872 | tf_op jit(solution)/shard_map/ppermute | solution.py:21
  2.5 15.6 %collective-permute-start = (f32[2,2,2,128,128]{4,3,2,1,0:T(8,128)}, f32[2,2,2,128,128]{4,3,2,1,0:T(8,128)}, u32[]{:S(2)}, u32[]{:S(2)}) collective-permute-start(f32[2,2,2,128,128]{4,3,2,1,0:T(8,128)} %param.5), channel_id=1, source_target_pairs={{0,1},{1,2},{2,3},{4,5},{5,6},{6,7},{8,9},{9,10},{10,11},{12,13},{... | collective-permute-start | bytes 1572872 | tf_op jit(solution)/shard_map/ppermute | solution.py:19
  27.7 8.0 %copy-start.2 = (s32[4]{0:T(128)S(1)}, s32[4]{0:T(128)}, u32[]{:S(2)}) copy-start(s32[4]{0:T(128)} %param.8) | copy-start | bytes 52
  27.7 13.6 %copy-start.3 = (f32[4]{0:T(128)S(1)}, f32[4]{0:T(128)}, u32[]{:S(2)}) copy-start(f32[4]{0:T(128)} %param.9) | copy-start | bytes 52
  31.4 11.4 %collective-permute-start.3 = (f32[2,2,2,128,128]{4,3,2,0,1:T(8,128)S(1)}, f32[2,2,2,128,128]{4,3,2,0,1:T(8,128)S(1)}, u32[]{:S(2)}, u32[]{:S(2)}) collective-permute-start(f32[2,2,2,128,128]{4,3,2,0,1:T(8,128)S(1)} %fusion.8), channel_id=1, source_target_pairs={{4,0},{8,4},{12,8},{16,12},{20,16},{24,20},{28,24},{5,1},{9,5},{13... | collective-permute-start | bytes 1572872 | tf_op jit(solution)/shard_map/ppermute | solution.py:21
  33.3 14.2 %collective-permute-start.2 = (f32[2,2,2,128,128]{4,3,2,0,1:T(8,128)S(1)}, f32[2,2,2,128,128]{4,3,2,0,1:T(8,128)S(1)}, u32[]{:S(2)}, u32[]{:S(2)}) collective-permute-start(f32[2,2,2,128,128]{4,3,2,0,1:T(8,128)S(1)} %fusion.8), channel_id=1, source_target_pairs={{0,4},{4,8},{8,12},{12,16},{16,20},{20,24},{24,28},{1,5},{5,9},{9,... | collective-permute-start | bytes 1572872 | tf_op jit(solution)/shard_map/ppermute | solution.py:19
  47.6 2.8 %copy-start.1 = (f32[2,2,2,128,128]{4,3,2,1,0:T(8,128)S(1)}, f32[2,2,2,128,128]{4,3,2,1,0:T(8,128)}, u32[]{:S(2)}) copy-start(f32[2,2,2,128,128]{4,3,2,1,0:T(8,128)} %param.5) | copy-start | bytes 1572868
  55.4 13.9 %collective-permute-start.5 = (f32[2,2,2,128,128]{4,3,1,0,2:T(8,128)S(1)}, f32[2,2,2,128,128]{4,3,1,0,2:T(8,128)S(1)}, u32[]{:S(2)}, u32[]{:S(2)}) collective-permute-start(f32[2,2,2,128,128]{4,3,1,0,2:T(8,128)S(1)} %maximum_add_fusion), channel_id=1, source_target_pairs={{1,0},{2,1},{3,2},{5,4},{6,5},{7,6},{9,8},{10,9},{11,10},{13,12},{... | collective-permute-start | bytes 1572872 | tf_op jit(solution)/shard_map/ppermute | solution.py:21
  57.4 13.9 %collective-permute-start.4 = (f32[2,2,2,128,128]{4,3,1,0,2:T(8,128)S(1)}, f32[2,2,2,128,128]{4,3,1,0,2:T(8,128)S(1)}, u32[]{:S(2)}, u32[]{:S(2)}) collective-permute-start(f32[2,2,2,128,128]{4,3,1,0,2:T(8,128)S(1)} %maximum_add_fusion), channel_id=1, source_target_pairs={{0,1},{1,2},{2,3},{4,5},{5,6},{6,7},{8,9},{9,10},{10,11},{12,13},{... | collective-permute-start | bytes 1572872 | tf_op jit(solution)/shard_map/ppermute | solution.py:19
  83.4 12.5 %collective-permute-start.7 = (f32[2,2,2,128,128]{4,3,2,0,1:T(8,128)S(1)}, f32[2,2,2,128,128]{4,3,2,0,1:T(8,128)S(1)}, u32[]{:S(2)}, u32[]{:S(2)}) collective-permute-start(f32[2,2,2,128,128]{4,3,2,0,1:T(8,128)S(1)} %fusion.11), channel_id=1, source_target_pairs={{4,0},{8,4},{12,8},{16,12},{20,16},{24,20},{28,24},{5,1},{9,5},{13... | collective-permute-start | bytes 1572872 | tf_op jit(solution)/shard_map/ppermute | solution.py:21
  85.3 12.3 %collective-permute-start.6 = (f32[2,2,2,128,128]{4,3,2,0,1:T(8,128)S(1)}, f32[2,2,2,128,128]{4,3,2,0,1:T(8,128)S(1)}, u32[]{:S(2)}, u32[]{:S(2)}) collective-permute-start(f32[2,2,2,128,128]{4,3,2,0,1:T(8,128)S(1)} %fusion.11), channel_id=1, source_target_pairs={{0,4},{4,8},{8,12},{12,16},{16,20},{20,24},{24,28},{1,5},{5,9},{9,... | collective-permute-start | bytes 1572872 | tf_op jit(solution)/shard_map/ppermute | solution.py:19
where the time goes:
time: 108 us; the launch traced here: 106 us
  waiting for transfers between devices  36.6 us (34%)
  matrix products  28 us (26%)
  starting transfers between devices  20.6 us (19%)
  other arithmetic  8 us (7%)
  local copies, waits for them, and re-layouts  7.9 us (7%)
  between operations  5.22 us (5%)
    ppermute x4, waiting for transfers between devices, with_halo(): lax.ppermute(head, axis, [((i + 1) % count, i) for i in range(ends)])  26 us
    ppermute x4, starting transfers between devices, with_halo(): lax.ppermute(tail, axis, [(i, (i + 1) % count) for i in range(ends)])  12.4 us
    dot_general x2, matrix products, sandwich(): left = jnp.einsum('akij,eakcjl->eakcil', grad_h, picked, precision=highest)  11 us
    ppermute x4, waiting for transfers between devices, with_halo(): lax.ppermute(tail, axis, [(i, (i + 1) % count) for i in range(ends)])  10.6 us
    ppermute x4, starting transfers between devices, with_halo(): lax.ppermute(head, axis, [((i + 1) % count, i) for i in range(ends)])  8.24 us
    dot_general x2, matrix products, sandwich(): return jnp.einsum('eakcil,akml->eacim', left, grad_h, precision=highest)  7.3 us
    gather x2, local copies, waits for them, and re-layouts, per_device(): inner = sandwich(grad_h, beside[:, local_index])  5.54 us
    add x2, other arithmetic, shift_total(): total + coupling[shift_index] * lax.dynamic_slice_in_dim(extended, start,...  5.41 us
  transfers between devices with their start and end apart: 8, of which 8 were waited for; matrix products, arithmetic and copies ran while one was open for 2% of the time, Pallas kernels for 0%

commit v1 on v0

v1 whole, which is shorter than its diff:
```python
import functools

import jax
import jax.numpy as jnp
from jax import lax
from jax.experimental import pallas as pl
from jax.experimental.pallas import tpu as pltpu
from jax.sharding import PartitionSpec as P

REACH = 2
ITERS = 2
VMEM = pl.BlockSpec(memory_space=pltpu.VMEM)
SMEM = pl.BlockSpec(memory_space=pltpu.SMEM)


def swaps(count, parity):
    pairs, i = [(j, j) for j in range(parity)], parity
    while i + 1 < count:
        pairs += [(i, i + 1), (i + 1, i)]
        i += 2
    if i < count:
        pairs.append((i, i))
    return pairs


def partners(axis):
    even = lax.axis_index(axis) % 2 == 0
    first = jnp.where(even, 1, -1)
    return first, -first


def trade(cells, axis, dim):
    count, own = lax.axis_size(axis), cells.shape[dim]
    got = []
    for parity, side in enumerate(partners(axis)):
        edge = cells
        if own != REACH:
            edge = lax.dynamic_slice_in_dim(cells, jnp.where(side > 0, own - REACH, 0), REACH, dim)
        got.append(lax.ppermute(edge, axis, swaps(count, parity)))
    return got


def split(value):
    high = value.astype(jnp.bfloat16)
    return high, (value - high.astype(jnp.float32)).astype(jnp.bfloat16)


def dot(left, right):
    return lax.dot_general(left, right, (((1,), (0,)), ((), ())), preferred_element_type=jnp.float32)


def prepare_kernel(grad_ref, right_ref, left_ref):
    atoms, entries, orb, _ = grad_ref.shape
    for a in range(atoms):
        for k in range(entries):
            high, low = split(grad_ref[a, k])
            left_ref[a, :orb, k * orb : (k + 1) * orb] = high
            left_ref[a, orb:, k * orb : (k + 1) * orb] = low
            high, low = split(grad_ref[a, k].T)
            right_ref[a, k, :, :orb] = high
            right_ref[a, k, :, orb:] = low


def prepare(grad_h):
    atoms, entries, orb, _ = grad_h.shape
    return pl.pallas_call(
        prepare_kernel,
        out_shape=(
            jax.ShapeDtypeStruct((atoms, entries, orb, 2 * orb), jnp.bfloat16),
            jax.ShapeDtypeStruct((atoms, 2 * orb, entries * orb), jnp.bfloat16),
        ),
        in_specs=[VMEM],
        out_specs=(VMEM, VMEM),
        name="prepare",
    )(grad_h)


def sandwich_kernel(index_ref, right_ref, left_ref, own_ref, one_ref, two_ref, out_ref, green_ref, high_ref, low_ref):
    energies, atoms, parts, orb, _ = out_ref.shape
    entries = right_ref.shape[1]
    at = 0
    for ref in (own_ref, one_ref, two_ref):
        for a in range(ref.shape[1]):
            for e in range(energies):
                for c in range(parts):
                    row = (e * parts + c) * orb
                    high, low = split(ref[e, a, c])
                    green_ref[at, row : row + orb, :orb] = high
                    green_ref[at, row : row + orb, orb:] = low
            at += 1
    for a in range(atoms):
        for k in range(entries):
            weight = right_ref[a, k]
            both = dot(green_ref[index_ref[a, k]], jnp.concatenate([weight, weight], axis=0))
            high, low = split(both[:, :orb] + both[:, orb:])
            for b in range(energies * parts):
                here = (slice(k * orb, (k + 1) * orb), slice(b * orb, (b + 1) * orb))
                high_ref[here] = high[b * orb : (b + 1) * orb]
                low_ref[here] = low[b * orb : (b + 1) * orb]
        main = dot(left_ref[a], high_ref[...])
        total = main[:orb] + (main[orb:] + dot(left_ref[a, :orb], low_ref[...]))
        for e in range(energies):
            for c in range(parts):
                col = (e * parts + c) * orb
                out_ref[e, a, c] = total[:, col : col + orb]


def sandwich(index, right, left, own, one, two):
    energies, atoms, parts, orb, _ = own.shape
    entries = right.shape[1]
    sources = atoms + one.shape[1] + two.shape[1]
    wide = energies * parts * orb
    return pl.pallas_call(
        sandwich_kernel,
        out_shape=jax.ShapeDtypeStruct(own.shape, jnp.float32),
        in_specs=[SMEM] + [VMEM] * 5,
        out_specs=VMEM,
        scratch_shapes=[
            pltpu.VMEM((sources, wide, 2 * orb), jnp.bfloat16),
            pltpu.VMEM((entries * orb, wide), jnp.bfloat16),
            pltpu.VMEM((entries * orb, wide), jnp.bfloat16),
        ],
        name="sandwich",
    )(index, right, left, own, one, two)


def complex_product(left, right):
    high, low = split(jnp.concatenate(left, axis=1))
    block = jnp.concatenate([jnp.concatenate(right, axis=1), jnp.concatenate([-right[1], right[0]], axis=1)], axis=0)
    block_high, block_low = split(block)
    orb = left[0].shape[0]
    main = dot(jnp.concatenate([high, low], axis=0), block_high)
    total = main[:orb] + (main[orb:] + dot(high, block_low))
    return total[:, :orb], total[:, orb:]


def dyson_kernel(weight_ref, own_ref, one_ref, two_ref, base_ref, out_ref):
    energies, atoms, parts, orb, _ = out_ref.shape
    sources = [(ref, s) for ref in (own_ref, one_ref, two_ref) for s in range(ref.shape[0])]
    for e in range(energies):
        for a in range(atoms):
            sigma = []
            for c in range(parts):
                total = jnp.zeros((orb, orb), jnp.float32)
                for at, (ref, s) in enumerate(sources):
                    total = total + weight_ref[e, at] * ref[s, a, c]
                sigma.append(total)
            base = (base_ref[e, a, 0], base_ref[e, a, 1])
            real, imag = complex_product(complex_product(base, sigma), base)
            out_ref[e, a, 0] = base[0] + real
            out_ref[e, a, 1] = base[1] + imag


def dyson(weights, own, one, two, base):
    return pl.pallas_call(
        dyson_kernel,
        out_shape=jax.ShapeDtypeStruct(base.shape, jnp.float32),
        in_specs=[SMEM] + [VMEM] * 4,
        out_specs=VMEM,
        name="dyson",
    )(weights, own, one, two, base)


def source_index(neighbours, atoms):
    away = neighbours - lax.axis_index("space") * atoms
    first, _ = partners("space")
    below = jnp.where(first < 0, atoms, atoms + REACH) + away + REACH
    above = jnp.where(first > 0, atoms, atoms + REACH) + away - atoms
    return jnp.where(away < 0, below, jnp.where(away < atoms, away, above)).astype(jnp.int32)


def shift_weights(shifts, coupling, energies):
    here, last = lax.axis_index("energy"), lax.axis_size("energy") - 1
    columns = [(jnp.arange(energies), True)]
    for side in partners("energy"):
        start = jnp.where(side > 0, energies, -REACH)
        there = here + side
        columns.append((start + jnp.arange(REACH), (there >= 0) & (there <= last)))
    source = jnp.concatenate([c for c, _ in columns])
    valid = jnp.concatenate([jnp.broadcast_to(jnp.asarray(v), c.shape) for c, v in columns])
    distance = source[None, :] - jnp.arange(energies)[:, None]
    hit = (distance[:, :, None] == shifts) & valid[None, :, None]
    return jnp.sum(jnp.where(hit, coupling, 0.0), axis=-1)


def per_device(green0, grad_h, neighbours, shifts, coupling):
    energies, atoms = green0.shape[:2]
    right, left = prepare(grad_h)
    index = source_index(neighbours, atoms)
    weights = shift_weights(shifts, coupling, energies)
    green = green0
    for step in range(ITERS):
        inner = sandwich(index, right, left, green, *trade(green, "space", 1))
        green = dyson(weights, inner, *trade(inner, "energy", 0), green0)
    return green


def solution(mesh):
    return jax.shard_map(
        per_device,
        mesh=mesh,
        in_specs=(
            P("energy", "space", None, None, None),
            P("space", None, None, None),
            P("space", None),
            P(),
            P(),
        ),
        out_specs=P("energy", "space", None, None, None),
        check_vma=False,
    )
```

time: 108 us -> 85.8 us (0.79); the launches traced: 106 us -> 85.3 us
  matrix products: 28 us -> 0 us
  Pallas kernels: 0 us -> 19.4 us
  waiting for transfers between devices: 36.6 us -> 45.2 us
  starting transfers between devices: 20.6 us -> 12.6 us
  other arithmetic: 8 us -> 1.34 us
  between operations: 5.22 us -> 0.14 us
  local copies, waits for them, and re-layouts: 7.9 us -> 6.67 us
    dot_general x20 -> x0, matrix products: 28 us -> none  [the longest x2 11 us: sandwich(): left = jnp.einsum('akij,eakcjl->eakcil', grad_h, picked, precision=highest)]
    pallas_call x0 -> x5, Pallas kernels: none -> 19.4 us  [the longest x2 10.2 us: sandwich(): pl.pallas_call(sandwich_kernel, out_shape=jax.ShapeDtypeStruct(own.shape,...]
    ppermute x8, waiting for transfers between devices: 36.6 us -> 45.2 us  [trade(): got.append(lax.ppermute(edge, axis, swaps(count, parity)))]
    ppermute x8, starting transfers between devices: 20.6 us -> 12.6 us  [trade(): got.append(lax.ppermute(edge, axis, swaps(count, parity)))]
    unnamed x8 -> x22, local copies, waits for them, and re-layouts: 0.02 us -> 6.65 us
    add x4 -> x1, other arithmetic: 5.57 us -> 0.01 us  [shift_weights(): columns.append((start + jnp.arange(REACH), (there >= 0) & (there <= last)))]
    gather x2 -> x0, local copies, waits for them, and re-layouts: 5.54 us -> none  [per_device(): inner = sandwich(grad_h, beside[:, local_index])]
    concatenate x4 -> x2, other arithmetic: 1.74 us -> 0.16 us  [the longest x1 0.08 us: shift_weights(): jnp.concatenate([jnp.broadcast_to(jnp.asarray(v), c.shape) for c, v in co...]
  transfers between devices with their start and end apart: 8 -> 8, of which waited for: 8 -> 6; matrix products, arithmetic and copies ran while one was open for 2% -> 2% of each run, Pallas kernels for 0% -> 3%
where the time goes in v1:
time: 85.8 us; the launch traced here: 85.3 us
  waiting for transfers between devices  45.2 us (53%)
  Pallas kernels  19.4 us (23%)
  starting transfers between devices  12.6 us (15%)
  local copies, waits for them, and re-layouts  6.67 us (8%)
  other arithmetic  1.34 us (2%)
    ppermute x8, waiting for transfers between devices, trade(): got.append(lax.ppermute(edge, axis, swaps(count, parity)))  45.2 us
    ppermute x8, starting transfers between devices, trade(): got.append(lax.ppermute(edge, axis, swaps(count, parity)))  12.6 us
    pallas_call x2, Pallas kernels, sandwich(): pl.pallas_call(sandwich_kernel, out_shape=jax.ShapeDtypeStruct(own.shape,...  10.2 us
    unnamed x22, local copies, waits for them, and re-layouts  6.65 us
    pallas_call x2, Pallas kernels, dyson(): pl.pallas_call(dyson_kernel, out_shape=jax.ShapeDtypeStruct(base.shape, j...  6.24 us
    pallas_call x1, Pallas kernels, prepare(): pl.pallas_call(prepare_kernel, out_shape=(jax.ShapeDtypeStruct((atoms, en...  2.93 us
  transfers between devices with their start and end apart: 8, of which 6 were waited for; matrix products, arithmetic and copies ran while one was open for 2% of the time, Pallas kernels for 3%

profile of v1, /device:TPU:12, one launch (start us, length us, event | category | flops | bytes accessed | tf_op | source)
XLA Modules:
  0.0 85.3 jit_solution(16109424620487394789)
XLA Ops:
  0.0 3.5 %collective-permute-start.1 = (f32[2,2,2,128,128]{4,3,2,1,0:T(8,128)}, f32[2,2,2,128,128]{4,3,2,1,0:T(8,128)S(1)}, u32[]{:S(2)}, u32[]{:S(2)}) collective-permute-start(f32[2,2,2,128,128]{4,3,2,1,0:T(8,128)} %base_ref.3), channel_id=1, source_target_pairs={{0,0},{1,2},{2,1},{3,3},{4,4},{5,6},{6,5},{7,7},{8,8},{9,10},{10,9... | collective-permute-start | bytes 1572872 | tf_op jit(solution)/shard_map/ppermute | solution.py:39
  3.5 0.1 collective-permute-start
  3.6 2.9 %prepare.1 = (bf16[2,8,128,256]{3,2,1,0:T(8,128)(2,1)}, bf16[2,256,1024]{2,1,0:T(8,128)(2,1)}) custom-call(f32[2,8,128,128]{3,2,1,0:T(8,128)} %grad_ref.1), custom_call_target="tpu_custom_call" | custom-call | tf_op jit(solution)/shard_map/prepare/pallas_call | solution.py:66
  6.5 0.7 copy-done.8
  7.2 0.5 compare_select_fusion.1.index_ref
  7.8 8.0 %collective-permute-done.1.two_ref = f32[2,2,2,128,128]{4,3,2,1,0:T(8,128)S(1)} collective-permute-done((f32[2,2,2,128,128]{4,3,2,1,0:T(8,128)}, f32[2,2,2,128,128]{4,3,2,1,0:T(8,128)S(1)}, u32[]{:S(2)}, u32[]{:S(2)}) %collective-permute-start.1) | collective-permute-done | bytes 524320 | tf_op jit(solution)/shard_map/ppermute | solution.py:39
  15.8 1.4 %collective-permute-done.one_ref = f32[2,2,2,128,128]{4,3,2,1,0:T(8,128)S(1)} collective-permute-done((f32[2,2,2,128,128]{4,3,2,1,0:T(8,128)}, f32[2,2,2,128,128]{4,3,2,1,0:T(8,128)S(1)}, u32[]{:S(2)}, u32[]{:S(2)}) %collective-permute-start) | collective-permute-done | bytes 524320 | tf_op jit(solution)/shard_map/ppermute | solution.py:39
  17.1 0.8 copy-done.1
  17.9 5.1 %sandwich.2.own_ref = f32[2,2,2,128,128]{4,3,2,1,0:T(8,128)} custom-call(s32[2,8]{1,0:T(2,128)} %compare_select_fusion.1.index_ref, bf16[2,8,128,256]{3,2,1,0:T(8,128)(2,1)} %get-tuple-element.7.right_ref, bf16[2,256,1024]{2,1,0:T(8,128)(2,1)} %get-tuple-element.8.left_ref, f32[2,2,2,128,128]{4,3,2,1,0:T(8,128)} %base_ref.3, ...), custom_call_target="tpu_custom_call" | custom-call | tf_op jit(solution)/shard_map/sandwich/pallas_call | solution.py:113
  23.1 1.9 %collective-permute-start.3 = (f32[2,2,2,128,128]{4,3,2,1,0:T(8,128)}, f32[2,2,2,128,128]{4,3,2,1,0:T(8,128)S(1)}, u32[]{:S(2)}, u32[]{:S(2)}) collective-permute-start(f32[2,2,2,128,128]{4,3,2,1,0:T(8,128)} %sandwich.2.own_ref), channel_id=1, source_target_pairs={{0,0},{4,8},{8,4},{12,16},{16,12},{20,24},{24,20},{28,28},{1,1},{5... | collective-permute-start | bytes 1572872 | tf_op jit(solution)/shard_map/ppermute | solution.py:39
  25.0 1.7 %collective-permute-start.2 = (f32[2,2,2,128,128]{4,3,2,1,0:T(8,128)}, f32[2,2,2,128,128]{4,3,2,1,0:T(8,128)S(1)}, u32[]{:S(2)}, u32[]{:S(2)}) collective-permute-start(f32[2,2,2,128,128]{4,3,2,1,0:T(8,128)} %sandwich.2.own_ref), channel_id=1, source_target_pairs={{0,4},{4,0},{8,12},{12,8},{16,20},{20,16},{24,28},{28,24},{1,5},{5... | collective-permute-start | bytes 1572872 | tf_op jit(solution)/shard_map/ppermute | solution.py:39
  26.7 0.1 pad_add_fusion
  26.7 0.1 pad_add_fusion.1
  26.8 0.6 copy-done.9
  27.5 0.6 select_reduce_fusion.weight_ref
  28.1 11.2 %collective-permute-done.3.two_ref = f32[2,2,2,128,128]{4,3,2,1,0:T(8,128)S(1)} collective-permute-done((f32[2,2,2,128,128]{4,3,2,1,0:T(8,128)}, f32[2,2,2,128,128]{4,3,2,1,0:T(8,128)S(1)}, u32[]{:S(2)}, u32[]{:S(2)}) %collective-permute-start.3) | collective-permute-done | bytes 524320 | tf_op jit(solution)/shard_map/ppermute | solution.py:39
  39.4 0.8 copy-done.2
  40.2 0.8 copy-done.3
  41.0 3.1 %dyson.2.own_ref = f32[2,2,2,128,128]{4,3,2,1,0:T(8,128)} custom-call(f32[2,6]{1,0:T(2,128)} %select_reduce_fusion.weight_ref, f32[2,2,2,128,128]{4,3,2,1,0:T(8,128)} %sandwich.2.own_ref, f32[2,2,2,128,128]{4,3,2,1,0:T(8,128)} %copy-done.3, f32[2,2,2,128,128]{4,3,2,1,0:T(8,128)} %copy-done.2, f32[2,2,2,128,128]{4,3,2,1,0:T(8,128)} %base_ref.3), custom_call_target="tpu_custom_call" | custom-call | tf_op jit(solution)/shard_map/dyson/pallas_call | solution.py:155
  44.1 2.3 %collective-permute-start.5 = (f32[2,2,2,128,128]{4,3,2,1,0:T(8,128)}, f32[2,2,2,128,128]{4,3,2,1,0:T(8,128)S(1)}, u32[]{:S(2)}, u32[]{:S(2)}) collective-permute-start(f32[2,2,2,128,128]{4,3,2,1,0:T(8,128)} %dyson.2.own_ref), channel_id=1, source_target_pairs={{0,0},{1,2},{2,1},{3,3},{4,4},{5,6},{6,5},{7,7},{8,8},{9,10},{10,9... | collective-permute-start | bytes 1572872 | tf_op jit(solution)/shard_map/ppermute | solution.py:39
  46.4 0.1 collective-permute-start.4
  46.5 11.8 %collective-permute-done.5.two_ref = f32[2,2,2,128,128]{4,3,2,1,0:T(8,128)S(1)} collective-permute-done((f32[2,2,2,128,128]{4,3,2,1,0:T(8,128)}, f32[2,2,2,128,128]{4,3,2,1,0:T(8,128)S(1)}, u32[]{:S(2)}, u32[]{:S(2)}) %collective-permute-start.5) | collective-permute-done | bytes 524320 | tf_op jit(solution)/shard_map/ppermute | solution.py:39
  58.3 0.3 collective-permute-done.4.one_ref
  58.6 0.5 copy-done.4
  59.1 0.8 copy-done.6
  59.9 5.1 %sandwich.3.own_ref = f32[2,2,2,128,128]{4,3,2,1,0:T(8,128)} custom-call(s32[2,8]{1,0:T(2,128)} %compare_select_fusion.1.index_ref, bf16[2,8,128,256]{3,2,1,0:T(8,128)(2,1)} %get-tuple-element.7.right_ref, bf16[2,256,1024]{2,1,0:T(8,128)(2,1)} %get-tuple-element.8.left_ref, f32[2,2,2,128,128]{4,3,2,1,0:T(8,128)} %dyson.2.own_ref, ...), custom_call_target="tpu_custom_call" | custom-call | tf_op jit(solution)/shard_map/sandwich/pallas_call | solution.py:113
  65.0 3.0 %collective-permute-start.7 = (f32[2,2,2,128,128]{4,3,2,1,0:T(8,128)}, f32[2,2,2,128,128]{4,3,2,1,0:T(8,128)S(1)}, u32[]{:S(2)}, u32[]{:S(2)}) collective-permute-start(f32[2,2,2,128,128]{4,3,2,1,0:T(8,128)} %sandwich.3.own_ref), channel_id=1, source_target_pairs={{0,0},{4,8},{8,4},{12,16},{16,12},{20,24},{24,20},{28,28},{1,1},{5... | collective-permute-start | bytes 1572872 | tf_op jit(solution)/shard_map/ppermute | solution.py:39
  68.0 0.1 collective-permute-start.6
  68.1 12.5 %collective-permute-done.7.two_ref = f32[2,2,2,128,128]{4,3,2,1,0:T(8,128)S(1)} collective-permute-done((f32[2,2,2,128,128]{4,3,2,1,0:T(8,128)}, f32[2,2,2,128,128]{4,3,2,1,0:T(8,128)S(1)}, u32[]{:S(2)}, u32[]{:S(2)}) %collective-permute-start.7) | collective-permute-done | bytes 524320 | tf_op jit(solution)/shard_map/ppermute | solution.py:39
  80.6 0.8 copy-done.5
  81.4 0.8 copy-done.7
  82.2 3.1 %dyson.3 = f32[2,2,2,128,128]{4,3,2,1,0:T(8,128)} custom-call(f32[2,6]{1,0:T(2,128)} %select_reduce_fusion.weight_ref, f32[2,2,2,128,128]{4,3,2,1,0:T(8,128)} %sandwich.3.own_ref, f32[2,2,2,128,128]{4,3,2,1,0:T(8,128)} %copy-done.7, f32[2,2,2,128,128]{4,3,2,1,0:T(8,128)} %copy-done.5, f32[2,2,2,128,128]{4,3,2,1,0:T(8,128)} %base_ref.3), custom_call_target="tpu_custom_call" | custom-call | tf_op jit(solution)/shard_map/dyson/pallas_call | solution.py:155
  (21 shorter events, 0.1 us)
Async XLA Ops:
  0.0 15.8 %collective-permute-start.1 = (f32[2,2,2,128,128]{4,3,2,1,0:T(8,128)}, f32[2,2,2,128,128]{4,3,2,1,0:T(8,128)S(1)}, u32[]{:S(2)}, u32[]{:S(2)}) collective-permute-start(f32[2,2,2,128,128]{4,3,2,1,0:T(8,128)} %base_ref.3), channel_id=1, source_target_pairs={{0,0},{1,2},{2,1},{3,3},{4,4},{5,6},{6,5},{7,7},{8,8},{9,10},{10,9... | collective-permute-start | bytes 1572872 | tf_op jit(solution)/shard_map/ppermute | solution.py:39
  3.5 13.7 %collective-permute-start = (f32[2,2,2,128,128]{4,3,2,1,0:T(8,128)}, f32[2,2,2,128,128]{4,3,2,1,0:T(8,128)S(1)}, u32[]{:S(2)}, u32[]{:S(2)}) collective-permute-start(f32[2,2,2,128,128]{4,3,2,1,0:T(8,128)} %base_ref.3), channel_id=1, source_target_pairs={{0,1},{1,0},{2,3},{3,2},{4,5},{5,4},{6,7},{7,6},{8,9},{9,8},{10,11... | collective-permute-start | bytes 1572872 | tf_op jit(solution)/shard_map/ppermute | solution.py:39
  6.5 0.7 copy-start.8
  15.8 1.4 %copy-start = (f32[2,2,2,128,128]{4,3,2,1,0:T(8,128)}, f32[2,2,2,128,128]{4,3,2,1,0:T(8,128)S(1)}, u32[]{:S(2)}) copy-start(f32[2,2,2,128,128]{4,3,2,1,0:T(8,128)S(1)} %collective-permute-done.1.two_ref) | copy-start | bytes 1572868
  17.1 0.8 copy-start.1
  23.1 16.3 %collective-permute-start.3 = (f32[2,2,2,128,128]{4,3,2,1,0:T(8,128)}, f32[2,2,2,128,128]{4,3,2,1,0:T(8,128)S(1)}, u32[]{:S(2)}, u32[]{:S(2)}) collective-permute-start(f32[2,2,2,128,128]{4,3,2,1,0:T(8,128)} %sandwich.2.own_ref), channel_id=1, source_target_pairs={{0,0},{4,8},{8,4},{12,16},{16,12},{20,24},{24,20},{28,28},{1,1},{5... | collective-permute-start | bytes 1572872 | tf_op jit(solution)/shard_map/ppermute | solution.py:39
  25.0 14.4 %collective-permute-start.2 = (f32[2,2,2,128,128]{4,3,2,1,0:T(8,128)}, f32[2,2,2,128,128]{4,3,2,1,0:T(8,128)S(1)}, u32[]{:S(2)}, u32[]{:S(2)}) collective-permute-start(f32[2,2,2,128,128]{4,3,2,1,0:T(8,128)} %sandwich.2.own_ref), channel_id=1, source_target_pairs={{0,4},{4,0},{8,12},{12,8},{16,20},{20,16},{24,28},{28,24},{1,5},{5... | collective-permute-start | bytes 1572872 | tf_op jit(solution)/shard_map/ppermute | solution.py:39
  26.8 0.7 copy-start.9
  26.8 0.7 copy-start.10
  39.4 0.8 copy-start.2
  40.2 0.8 copy-start.3
  44.1 14.3 %collective-permute-start.5 = (f32[2,2,2,128,128]{4,3,2,1,0:T(8,128)}, f32[2,2,2,128,128]{4,3,2,1,0:T(8,128)S(1)}, u32[]{:S(2)}, u32[]{:S(2)}) collective-permute-start(f32[2,2,2,128,128]{4,3,2,1,0:T(8,128)} %dyson.2.own_ref), channel_id=1, source_target_pairs={{0,0},{1,2},{2,1},{3,3},{4,4},{5,6},{6,5},{7,7},{8,8},{9,10},{10,9... | collective-permute-start | bytes 1572872 | tf_op jit(solution)/shard_map/ppermute | solution.py:39
  46.4 12.2 %collective-permute-start.4 = (f32[2,2,2,128,128]{4,3,2,1,0:T(8,128)}, f32[2,2,2,128,128]{4,3,2,1,0:T(8,128)S(1)}, u32[]{:S(2)}, u32[]{:S(2)}) collective-permute-start(f32[2,2,2,128,128]{4,3,2,1,0:T(8,128)} %dyson.2.own_ref), channel_id=1, source_target_pairs={{0,1},{1,0},{2,3},{3,2},{4,5},{5,4},{6,7},{7,6},{8,9},{9,8},{10,11... | collective-permute-start | bytes 1572872 | tf_op jit(solution)/shard_map/ppermute | solution.py:39
  58.3 0.8 copy-start.4
  59.1 0.8 copy-start.6
  65.0 15.6 %collective-permute-start.7 = (f32[2,2,2,128,128]{4,3,2,1,0:T(8,128)}, f32[2,2,2,128,128]{4,3,2,1,0:T(8,128)S(1)}, u32[]{:S(2)}, u32[]{:S(2)}) collective-permute-start(f32[2,2,2,128,128]{4,3,2,1,0:T(8,128)} %sandwich.3.own_ref), channel_id=1, source_target_pairs={{0,0},{4,8},{8,4},{12,16},{16,12},{20,24},{24,20},{28,28},{1,1},{5... | collective-permute-start | bytes 1572872 | tf_op jit(solution)/shard_map/ppermute | solution.py:39
  68.0 12.6 %collective-permute-start.6 = (f32[2,2,2,128,128]{4,3,2,1,0:T(8,128)}, f32[2,2,2,128,128]{4,3,2,1,0:T(8,128)S(1)}, u32[]{:S(2)}, u32[]{:S(2)}) collective-permute-start(f32[2,2,2,128,128]{4,3,2,1,0:T(8,128)} %sandwich.3.own_ref), channel_id=1, source_target_pairs={{0,4},{4,0},{8,12},{12,8},{16,20},{20,16},{24,28},{28,24},{1,5},{5... | collective-permute-start | bytes 1572872 | tf_op jit(solution)/shard_map/ppermute | solution.py:39
  80.6 0.8 copy-start.5
  81.4 0.8 copy-start.7

commit v2 on v1

--- a/solution.py
+++ b/solution.py
@@ -7,19 +7,35 @@
 from jax.experimental.pallas import tpu as pltpu
 from jax.sharding import PartitionSpec as P
 
+AXES = ("energy", "space")
 REACH = 2
 ITERS = 2
 VMEM = pl.BlockSpec(memory_space=pltpu.VMEM)
 SMEM = pl.BlockSpec(memory_space=pltpu.SMEM)
 
 
-def swaps(count, parity):
-    pairs, i = [(j, j) for j in range(parity)], parity
-    while i + 1 < count:
-        pairs += [(i, i + 1), (i + 1, i)]
-        i += 2
-    if i < count:
-        pairs.append((i, i))
+def near(*arrays):
+    return [pltpu.with_memory_space_constraint(a, pltpu.VMEM) for a in arrays]
+
+
+def at_hand(shape, dtype=jnp.float32):
+    return pltpu.VMEM(shape, dtype)
+
+
+def swaps(axis, parity):
+    sizes = {name: lax.axis_size(name) for name in AXES}
+    count, pairs = sizes[axis], []
+    for energy in range(sizes["energy"]):
+        for space in range(sizes["space"]):
+            to = {"energy": energy, "space": space}
+            there = to[axis] + (1 if to[axis] % 2 == parity else -1)
+            if 0 <= there < count:
+                to[axis] = there
+            elif axis == "space" and sizes["energy"] % 2 == 0:
+                to["energy"] = energy ^ 1
+            elif axis == "energy" and count % 2 == 0:
+                to["energy"] = there % count
+            pairs.append((energy * sizes["space"] + space, to["energy"] * sizes["space"] + to["space"]))
     return pairs
 
 
@@ -30,13 +46,13 @@
 
 
 def trade(cells, axis, dim):
-    count, own = lax.axis_size(axis), cells.shape[dim]
+    own = cells.shape[dim]
     got = []
     for parity, side in enumerate(partners(axis)):
         edge = cells
         if own != REACH:
             edge = lax.dynamic_slice_in_dim(cells, jnp.where(side > 0, own - REACH, 0), REACH, dim)
-        got.append(lax.ppermute(edge, axis, swaps(count, parity)))
+        got.append(lax.ppermute(edge, AXES, swaps(axis, parity)))
     return got
 
 
@@ -66,11 +82,12 @@
     return pl.pallas_call(
         prepare_kernel,
         out_shape=(
-            jax.ShapeDtypeStruct((atoms, entries, orb, 2 * orb), jnp.bfloat16),
-            jax.ShapeDtypeStruct((atoms, 2 * orb, entries * orb), jnp.bfloat16),
+            at_hand((atoms, entries, orb, 2 * orb), jnp.bfloat16),
+            at_hand((atoms, 2 * orb, entries * orb), jnp.bfloat16),
         ),
         in_specs=[VMEM],
         out_specs=(VMEM, VMEM),
+        compiler_params=pltpu.CompilerParams(vmem_limit_bytes=24 << 20),
         name="prepare",
     )(grad_h)
 
@@ -112,7 +129,7 @@
     wide = energies * parts * orb
     return pl.pallas_call(
         sandwich_kernel,
-        out_shape=jax.ShapeDtypeStruct(own.shape, jnp.float32),
+        out_shape=at_hand(own.shape),
         in_specs=[SMEM] + [VMEM] * 5,
         out_specs=VMEM,
         scratch_shapes=[
@@ -120,8 +137,9 @@
             pltpu.VMEM((entries * orb, wide), jnp.bfloat16),
             pltpu.VMEM((entries * orb, wide), jnp.bfloat16),
         ],
+        compiler_params=pltpu.CompilerParams(vmem_limit_bytes=24 << 20),
         name="sandwich",
-    )(index, right, left, own, one, two)
+    )(index, *near(right, left, own, one, two))
 
 
 def complex_product(left, right):
@@ -157,8 +175,9 @@
         out_shape=jax.ShapeDtypeStruct(base.shape, jnp.float32),
         in_specs=[SMEM] + [VMEM] * 4,
         out_specs=VMEM,
+        compiler_params=pltpu.CompilerParams(vmem_limit_bytes=24 << 20),
         name="dyson",
-    )(weights, own, one, two, base)
+    )(weights, *near(own, one, two, base))
 
 
 def source_index(neighbours, atoms):

time: 85.8 us -> 70.4 us (0.82)
  the two profiles are of different devices: /device:TPU:12 before, /device:TPU:0 now
where the time goes in v2:
time: 70.4 us; the launch traced here: 70.2 us
  waiting for transfers between devices  47.3 us (67%)
  Pallas kernels  10.4 us (15%)
  starting transfers between devices  9.61 us (14%)
  local copies, waits for them, and re-layouts  2.57 us (4%)
    ppermute x8, waiting for transfers between devices, trade(): got.append(lax.ppermute(edge, AXES, swaps(axis, parity)))  47.3 us
    ppermute x8, starting transfers between devices, trade(): got.append(lax.ppermute(edge, AXES, swaps(axis, parity)))  9.61 us
    pallas_call x2, Pallas kernels, sandwich(): pl.pallas_call(sandwich_kernel, out_shape=at_hand(own.shape), in_specs=[S...  6.22 us
    pallas_call x2, Pallas kernels, dyson(): pl.pallas_call(dyson_kernel, out_shape=jax.ShapeDtypeStruct(base.shape, j...  3.59 us
    unnamed x10, local copies, waits for them, and re-layouts  2.56 us
  transfers between devices with their start and end apart: 8, of which 4 were waited for; matrix products, arithmetic and copies ran while one was open for 0% of the time, Pallas kernels for 1%

profile of v2, /device:TPU:0, one launch (start us, length us, event | category | flops | bytes accessed | tf_op | source)
XLA Modules:
  0.0 70.2 jit_solution(4478678417977033092)
XLA Ops:
  0.0 0.5 collective-permute-start.1
  0.5 4.1 %collective-permute-start = (f32[2,2,2,128,128]{4,3,2,1,0:T(8,128)}, f32[2,2,2,128,128]{4,3,2,1,0:T(8,128)}, u32[]{:S(2)}, u32[]{:S(2)}) collective-permute-start(f32[2,2,2,128,128]{4,3,2,1,0:T(8,128)} %base_ref.3), channel_id=1, source_target_pairs={{0,1},{1,0},{2,3},{3,2},{4,5},{5,4},{6,7},{7,6},{8,9},{9,8},{10,11... | collective-permute-start | bytes 1572872 | tf_op jit(solution)/shard_map/ppermute | solution.py:55
  4.6 0.0 copy-start.1
  4.6 1.2 %copy-done.1 = f32[2,8,128,128]{3,2,1,0:T(8,128)S(1)} copy-done((f32[2,8,128,128]{3,2,1,0:T(8,128)S(1)}, f32[2,8,128,128]{3,2,1,0:T(8,128)}, u32[]{:S(2)}) %copy-start.1) | copy-done | bytes 1048600
  5.9 0.0 copy-start
  5.9 0.6 prepare.1
  6.5 0.0 copy-start.2
  6.5 0.7 copy-done.2
  7.1 0.0 collective-permute-done.1.two_ref
  7.1 9.5 %collective-permute-done.one_ref = f32[2,2,2,128,128]{4,3,2,1,0:T(8,128)} collective-permute-done((f32[2,2,2,128,128]{4,3,2,1,0:T(8,128)}, f32[2,2,2,128,128]{4,3,2,1,0:T(8,128)}, u32[]{:S(2)}, u32[]{:S(2)}) %collective-permute-start) | collective-permute-done | bytes 524320 | tf_op jit(solution)/shard_map/ppermute | solution.py:55
  16.6 0.0 copy-done
  16.6 3.4 %sandwich.2.own_ref = f32[2,2,2,128,128]{4,3,2,1,0:T(8,128)S(1)} custom-call(s32[2,8]{1,0:T(2,128)S(1)} %compare_select_fusion.1.index_ref, bf16[2,8,128,256]{3,2,1,0:T(8,128)(2,1)S(1)} %get-tuple-element.7.right_ref, bf16[2,256,1024]{2,1,0:T(8,128)(2,1)S(1)} %get-tuple-element.8.left_ref, f32[2,2,2,128,128]{4,3,2,1,0:T(8,128)S(1)} %copy-done, ...), custom_call_target="tpu_custom_call" | custom-call | tf_op jit(solution)/shard_map/sandwich/pallas_call | solution.py:130
  20.0 1.1 %collective-permute-start.3 = (f32[2,2,2,128,128]{4,3,2,1,0:T(8,128)S(1)}, f32[2,2,2,128,128]{4,3,2,1,0:T(8,128)S(1)}, u32[]{:S(2)}, u32[]{:S(2)}) collective-permute-start(f32[2,2,2,128,128]{4,3,2,1,0:T(8,128)S(1)} %sandwich.2.own_ref), channel_id=1, source_target_pairs={{0,28},{1,29},{2,30},{3,31},{4,8},{5,9},{6,10},{7,11},{8,4},{9,5},... | collective-permute-start | bytes 1572872 | tf_op jit(solution)/shard_map/ppermute | solution.py:55
  21.1 0.6 collective-permute-start.2
  21.7 0.1 pad_add_fusion
  21.8 0.1 pad_add_fusion.1
  21.9 0.6 copy-done.3
  22.5 0.0 copy-done.4
  22.5 0.1 select_reduce_fusion.weight_ref
  22.6 12.5 %collective-permute-done.3.two_ref = f32[2,2,2,128,128]{4,3,2,1,0:T(8,128)S(1)} collective-permute-done((f32[2,2,2,128,128]{4,3,2,1,0:T(8,128)S(1)}, f32[2,2,2,128,128]{4,3,2,1,0:T(8,128)S(1)}, u32[]{:S(2)}, u32[]{:S(2)}) %collective-permute-start.3) | collective-permute-done | bytes 524320 | tf_op jit(solution)/shard_map/ppermute | solution.py:55
  35.1 0.0 collective-permute-done.2.one_ref
  35.1 1.4 %dyson.2.own_ref = f32[2,2,2,128,128]{4,3,2,1,0:T(8,128)S(1)} custom-call(f32[2,6]{1,0:T(2,128)S(1)} %select_reduce_fusion.weight_ref, f32[2,2,2,128,128]{4,3,2,1,0:T(8,128)S(1)} %sandwich.2.own_ref, f32[2,2,2,128,128]{4,3,2,1,0:T(8,128)S(1)} %collective-permute-done.2.one_ref, f32[2,2,2,128,128]{4,3,2,1,0:T(8,128)S(1)} %collective-permute-done.3.two_ref, ...), custom_call_target="tpu_custom_call" | custom-call | tf_op jit(solution)/shard_map/dyson/pallas_call | solution.py:173
  36.5 0.1 collective-permute-start.5
  36.6 2.5 %collective-permute-start.4 = (f32[2,2,2,128,128]{4,3,2,1,0:T(8,128)S(1)}, f32[2,2,2,128,128]{4,3,2,1,0:T(8,128)S(1)}, u32[]{:S(2)}, u32[]{:S(2)}) collective-permute-start(f32[2,2,2,128,128]{4,3,2,1,0:T(8,128)S(1)} %dyson.2.own_ref), channel_id=1, source_target_pairs={{0,1},{1,0},{2,3},{3,2},{4,5},{5,4},{6,7},{7,6},{8,9},{9,8},{10,11... | collective-permute-start | bytes 1572872 | tf_op jit(solution)/shard_map/ppermute | solution.py:55
  39.0 0.0 collective-permute-done.5.two_ref
  39.0 11.8 %collective-permute-done.4.one_ref = f32[2,2,2,128,128]{4,3,2,1,0:T(8,128)S(1)} collective-permute-done((f32[2,2,2,128,128]{4,3,2,1,0:T(8,128)S(1)}, f32[2,2,2,128,128]{4,3,2,1,0:T(8,128)S(1)}, u32[]{:S(2)}, u32[]{:S(2)}) %collective-permute-start.4) | collective-permute-done | bytes 524320 | tf_op jit(solution)/shard_map/ppermute | solution.py:55
  50.9 2.9 %sandwich.3.own_ref = f32[2,2,2,128,128]{4,3,2,1,0:T(8,128)S(1)} custom-call(s32[2,8]{1,0:T(2,128)S(1)} %compare_select_fusion.1.index_ref, bf16[2,8,128,256]{3,2,1,0:T(8,128)(2,1)S(1)} %get-tuple-element.7.right_ref, bf16[2,256,1024]{2,1,0:T(8,128)(2,1)S(1)} %get-tuple-element.8.left_ref, f32[2,2,2,128,128]{4,3,2,1,0:T(8,128)S(1)} %dyson.2.own_ref, ...), custom_call_target="tpu_custom_call" | custom-call | tf_op jit(solution)/shard_map/sandwich/pallas_call | solution.py:130
  53.8 0.7 collective-permute-start.7
  54.4 0.1 collective-permute-start.6
  54.5 13.5 %collective-permute-done.7.two_ref = f32[2,2,2,128,128]{4,3,2,1,0:T(8,128)S(1)} collective-permute-done((f32[2,2,2,128,128]{4,3,2,1,0:T(8,128)S(1)}, f32[2,2,2,128,128]{4,3,2,1,0:T(8,128)S(1)}, u32[]{:S(2)}, u32[]{:S(2)}) %collective-permute-start.7) | collective-permute-done | bytes 524320 | tf_op jit(solution)/shard_map/ppermute | solution.py:55
  68.0 0.0 collective-permute-done.6.one_ref
  68.0 2.2 %dyson.3 = f32[2,2,2,128,128]{4,3,2,1,0:T(8,128)} custom-call(f32[2,6]{1,0:T(2,128)S(1)} %select_reduce_fusion.weight_ref, f32[2,2,2,128,128]{4,3,2,1,0:T(8,128)S(1)} %sandwich.3.own_ref, f32[2,2,2,128,128]{4,3,2,1,0:T(8,128)S(1)} %collective-permute-done.6.one_ref, f32[2,2,2,128,128]{4,3,2,1,0:T(8,128)S(1)} %collective-permute-done.7.two_ref, ...), custom_call_target="tpu_custom_call" | custom-call | tf_op jit(solution)/shard_map/dyson/pallas_call | solution.py:173
  (9 shorter events, 0.0 us)
Async XLA Ops:
  0.0 7.1 %collective-permute-start.1 = (f32[2,2,2,128,128]{4,3,2,1,0:T(8,128)}, f32[2,2,2,128,128]{4,3,2,1,0:T(8,128)S(1)}, u32[]{:S(2)}, u32[]{:S(2)}) collective-permute-start(f32[2,2,2,128,128]{4,3,2,1,0:T(8,128)} %base_ref.3), channel_id=1, source_target_pairs={{0,4},{1,2},{2,1},{3,7},{4,0},{5,6},{6,5},{7,3},{8,12},{9,10},{10,... | collective-permute-start | bytes 1572872 | tf_op jit(solution)/shard_map/ppermute | solution.py:55
  0.5 16.1 %collective-permute-start = (f32[2,2,2,128,128]{4,3,2,1,0:T(8,128)}, f32[2,2,2,128,128]{4,3,2,1,0:T(8,128)}, u32[]{:S(2)}, u32[]{:S(2)}) collective-permute-start(f32[2,2,2,128,128]{4,3,2,1,0:T(8,128)} %base_ref.3), channel_id=1, source_target_pairs={{0,1},{1,0},{2,3},{3,2},{4,5},{5,4},{6,7},{7,6},{8,9},{9,8},{10,11... | collective-permute-start | bytes 1572872 | tf_op jit(solution)/shard_map/ppermute | solution.py:55
  4.6 1.2 %copy-start.1 = (f32[2,8,128,128]{3,2,1,0:T(8,128)S(1)}, f32[2,8,128,128]{3,2,1,0:T(8,128)}, u32[]{:S(2)}) copy-start(f32[2,8,128,128]{3,2,1,0:T(8,128)} %grad_ref.1) | copy-start | bytes 3145732
  5.9 10.8 %copy-start = (f32[2,2,2,128,128]{4,3,2,1,0:T(8,128)S(1)}, f32[2,2,2,128,128]{4,3,2,1,0:T(8,128)}, u32[]{:S(2)}) copy-start(f32[2,2,2,128,128]{4,3,2,1,0:T(8,128)} %base_ref.3) | copy-start | bytes 1572868
  6.5 0.7 copy-start.2
  20.0 15.1 %collective-permute-start.3 = (f32[2,2,2,128,128]{4,3,2,1,0:T(8,128)S(1)}, f32[2,2,2,128,128]{4,3,2,1,0:T(8,128)S(1)}, u32[]{:S(2)}, u32[]{:S(2)}) collective-permute-start(f32[2,2,2,128,128]{4,3,2,1,0:T(8,128)S(1)} %sandwich.2.own_ref), channel_id=1, source_target_pairs={{0,28},{1,29},{2,30},{3,31},{4,8},{5,9},{6,10},{7,11},{8,4},{9,5},... | collective-permute-start | bytes 1572872 | tf_op jit(solution)/shard_map/ppermute | solution.py:55
  21.1 14.0 %collective-permute-start.2 = (f32[2,2,2,128,128]{4,3,2,1,0:T(8,128)S(1)}, f32[2,2,2,128,128]{4,3,2,1,0:T(8,128)S(1)}, u32[]{:S(2)}, u32[]{:S(2)}) collective-permute-start(f32[2,2,2,128,128]{4,3,2,1,0:T(8,128)S(1)} %sandwich.2.own_ref), channel_id=1, source_target_pairs={{0,4},{1,5},{2,6},{3,7},{4,0},{5,1},{6,2},{7,3},{8,12},{9,13},{10,... | collective-permute-start | bytes 1572872 | tf_op jit(solution)/shard_map/ppermute | solution.py:55
  21.8 0.7 copy-start.3
  21.8 0.7 copy-start.4
  36.5 2.6 %collective-permute-start.5 = (f32[2,2,2,128,128]{4,3,2,1,0:T(8,128)S(1)}, f32[2,2,2,128,128]{4,3,2,1,0:T(8,128)S(1)}, u32[]{:S(2)}, u32[]{:S(2)}) collective-permute-start(f32[2,2,2,128,128]{4,3,2,1,0:T(8,128)S(1)} %dyson.2.own_ref), channel_id=1, source_target_pairs={{0,4},{1,2},{2,1},{3,7},{4,0},{5,6},{6,5},{7,3},{8,12},{9,10},{10,... | collective-permute-start | bytes 1572872 | tf_op jit(solution)/shard_map/ppermute | solution.py:55
  36.6 14.3 %collective-permute-start.4 = (f32[2,2,2,128,128]{4,3,2,1,0:T(8,128)S(1)}, f32[2,2,2,128,128]{4,3,2,1,0:T(8,128)S(1)}, u32[]{:S(2)}, u32[]{:S(2)}) collective-permute-start(f32[2,2,2,128,128]{4,3,2,1,0:T(8,128)S(1)} %dyson.2.own_ref), channel_id=1, source_target_pairs={{0,1},{1,0},{2,3},{3,2},{4,5},{5,4},{6,7},{7,6},{8,9},{9,8},{10,11... | collective-permute-start | bytes 1572872 | tf_op jit(solution)/shard_map/ppermute | solution.py:55
  53.8 14.2 %collective-permute-start.7 = (f32[2,2,2,128,128]{4,3,2,1,0:T(8,128)S(1)}, f32[2,2,2,128,128]{4,3,2,1,0:T(8,128)S(1)}, u32[]{:S(2)}, u32[]{:S(2)}) collective-permute-start(f32[2,2,2,128,128]{4,3,2,1,0:T(8,128)S(1)} %sandwich.3.own_ref), channel_id=1, source_target_pairs={{0,28},{1,29},{2,30},{3,31},{4,8},{5,9},{6,10},{7,11},{8,4},{9,5},... | collective-permute-start | bytes 1572872 | tf_op jit(solution)/shard_map/ppermute | solution.py:55
  54.4 13.6 %collective-permute-start.6 = (f32[2,2,2,128,128]{4,3,2,1,0:T(8,128)S(1)}, f32[2,2,2,128,128]{4,3,2,1,0:T(8,128)S(1)}, u32[]{:S(2)}, u32[]{:S(2)}) collective-permute-start(f32[2,2,2,128,128]{4,3,2,1,0:T(8,128)S(1)} %sandwich.3.own_ref), channel_id=1, source_target_pairs={{0,4},{1,5},{2,6},{3,7},{4,0},{5,1},{6,2},{7,3},{8,12},{9,13},{10,... | collective-permute-start | bytes 1572872 | tf_op jit(solution)/shard_map/ppermute | solution.py:55

commit v3 on v2

--- a/solution.py
+++ b/solution.py
@@ -1,5 +1,3 @@
-import functools
-
 import jax
 import jax.numpy as jnp
 from jax import lax
@@ -12,6 +10,7 @@
 ITERS = 2
 VMEM = pl.BlockSpec(memory_space=pltpu.VMEM)
 SMEM = pl.BlockSpec(memory_space=pltpu.SMEM)
+PARAMS = pltpu.CompilerParams(vmem_limit_bytes=24 << 20)
 
 
 def near(*arrays):
@@ -87,59 +86,100 @@
         ),
         in_specs=[VMEM],
         out_specs=(VMEM, VMEM),
-        compiler_params=pltpu.CompilerParams(vmem_limit_bytes=24 << 20),
+        compiler_params=PARAMS,
         name="prepare",
     )(grad_h)
 
 
 def sandwich_kernel(index_ref, right_ref, left_ref, own_ref, one_ref, two_ref, out_ref, green_ref, high_ref, low_ref):
-    energies, atoms, parts, orb, _ = out_ref.shape
+    energies, atoms, orb, _ = out_ref.shape
     entries = right_ref.shape[1]
     at = 0
     for ref in (own_ref, one_ref, two_ref):
         for a in range(ref.shape[1]):
             for e in range(energies):
-                for c in range(parts):
-                    row = (e * parts + c) * orb
-                    high, low = split(ref[e, a, c])
-                    green_ref[at, row : row + orb, :orb] = high
-                    green_ref[at, row : row + orb, orb:] = low
+                high, low = split(ref[e, a])
+                green_ref[at, e * orb : (e + 1) * orb, :orb] = high
+                green_ref[at, e * orb : (e + 1) * orb, orb:] = low
             at += 1
     for a in range(atoms):
         for k in range(entries):
             weight = right_ref[a, k]
             both = dot(green_ref[index_ref[a, k]], jnp.concatenate([weight, weight], axis=0))
             high, low = split(both[:, :orb] + both[:, orb:])
-            for b in range(energies * parts):
-                here = (slice(k * orb, (k + 1) * orb), slice(b * orb, (b + 1) * orb))
-                high_ref[here] = high[b * orb : (b + 1) * orb]
-                low_ref[here] = low[b * orb : (b + 1) * orb]
+            for e in range(energies):
+                here = (slice(k * orb, (k + 1) * orb), slice(e * orb, (e + 1) * orb))
+                high_ref[here] = high[e * orb : (e + 1) * orb]
+                low_ref[here] = low[e * orb : (e + 1) * orb]
         main = dot(left_ref[a], high_ref[...])
         total = main[:orb] + (main[orb:] + dot(left_ref[a, :orb], low_ref[...]))
         for e in range(energies):
-            for c in range(parts):
-                col = (e * parts + c) * orb
-                out_ref[e, a, c] = total[:, col : col + orb]
+            out_ref[e, a] = total[:, e * orb : (e + 1) * orb]
 
 
 def sandwich(index, right, left, own, one, two):
-    energies, atoms, parts, orb, _ = own.shape
+    energies, atoms, orb, _ = own.shape
     entries = right.shape[1]
     sources = atoms + one.shape[1] + two.shape[1]
-    wide = energies * parts * orb
     return pl.pallas_call(
         sandwich_kernel,
         out_shape=at_hand(own.shape),
         in_specs=[SMEM] + [VMEM] * 5,
         out_specs=VMEM,
         scratch_shapes=[
-            pltpu.VMEM((sources, wide, 2 * orb), jnp.bfloat16),
-            pltpu.VMEM((entries * orb, wide), jnp.bfloat16),
-            pltpu.VMEM((entries * orb, wide), jnp.bfloat16),
+            pltpu.VMEM((sources, energies * orb, 2 * orb), jnp.bfloat16),
+            pltpu.VMEM((entries * orb, energies * orb), jnp.bfloat16),
+            pltpu.VMEM((entries * orb, energies * orb), jnp.bfloat16),
         ],
-        compiler_params=pltpu.CompilerParams(vmem_limit_bytes=24 << 20),
+        compiler_params=PARAMS,
         name="sandwich",
     )(index, *near(right, left, own, one, two))
+
+
+def parts_kernel(green_ref, real_ref, imag_ref, sems):
+    copies = [pltpu.make_async_copy(green_ref.at[:, :, c], ref, sems.at[c]) for c, ref in enumerate((real_ref, imag_ref))]
+    for copy in copies:
+        copy.start()
+    for copy in copies:
+        copy.wait()
+
+
+def parts(green):
+    shape = green.shape[:2] + green.shape[3:]
+    return pl.pallas_call(
+        parts_kernel,
+        out_shape=(at_hand(shape), at_hand(shape)),
+        in_specs=[pl.BlockSpec(memory_space=pltpu.HBM)],
+        out_specs=(VMEM, VMEM),
+        scratch_shapes=[pltpu.SemaphoreType.DMA((2,))],
+        compiler_params=PARAMS,
+        name="parts",
+    )(green)
+
+
+def shifted(weight_ref, refs, e, a):
+    sources = [(ref, s) for ref in refs for s in range(ref.shape[0])]
+    total = weight_ref[e, 0] * sources[0][0][sources[0][1], a]
+    for at, (ref, s) in enumerate(sources[1:]):
+        total = total + weight_ref[e, at + 1] * ref[s, a]
+    return total
+
+
+def shift_sum_kernel(weight_ref, own_ref, one_ref, two_ref, out_ref):
+    for e in range(out_ref.shape[0]):
+        for a in range(out_ref.shape[1]):
+            out_ref[e, a] = shifted(weight_ref, (own_ref, one_ref, two_ref), e, a)
+
+
+def shift_sum(weights, own, one, two):
+    return pl.pallas_call(
+        shift_sum_kernel,
+        out_shape=at_hand(own.shape),
+        in_specs=[SMEM] + [VMEM] * 3,
+        out_specs=VMEM,
+        compiler_params=PARAMS,
+        name="shift_sum",
+    )(weights, *near(own, one, two))
 
 
 def complex_product(left, right):
@@ -152,32 +192,33 @@
     return total[:, :orb], total[:, orb:]
 
 
-def dyson_kernel(weight_ref, own_ref, one_ref, two_ref, base_ref, out_ref):
-    energies, atoms, parts, orb, _ = out_ref.shape
-    sources = [(ref, s) for ref in (own_ref, one_ref, two_ref) for s in range(ref.shape[0])]
-    for e in range(energies):
-        for a in range(atoms):
-            sigma = []
-            for c in range(parts):
-                total = jnp.zeros((orb, orb), jnp.float32)
-                for at, (ref, s) in enumerate(sources):
-                    total = total + weight_ref[e, at] * ref[s, a, c]
-                sigma.append(total)
-            base = (base_ref[e, a, 0], base_ref[e, a, 1])
-            real, imag = complex_product(complex_product(base, sigma), base)
-            out_ref[e, a, 0] = base[0] + real
-            out_ref[e, a, 1] = base[1] + imag
-
-
-def dyson(weights, own, one, two, base):
+def dyson_kernel(weight_ref, sigma_ref, own_ref, one_ref, two_ref, real_ref, imag_ref, *out_refs):
+    for e in range(real_ref.shape[0]):
+        for a in range(real_ref.shape[1]):
+            sigma = (sigma_ref[e, a], shifted(weight_ref, (own_ref, one_ref, two_ref), e, a))
+            base = (real_ref[e, a], imag_ref[e, a])
+            moved = complex_product(complex_product(base, sigma), base)
+            for c in range(2):
+                if len(out_refs) == 2:
+                    out_refs[c][e, a] = base[c] + moved[c]
+                else:
+                    out_refs[0][e, a, c] = base[c] + moved[c]
+
+
+def dyson(weights, sigma, own, one, two, base, whole):
+    shape = base[0].shape
+    if whole:
+        out_shape = jax.ShapeDtypeStruct(shape[:2] + (2,) + shape[2:], jnp.float32)
+    else:
+        out_shape = (at_hand(shape), at_hand(shape))
     return pl.pallas_call(
         dyson_kernel,
-        out_shape=jax.ShapeDtypeStruct(base.shape, jnp.float32),
-        in_specs=[SMEM] + [VMEM] * 4,
-        out_specs=VMEM,
-        compiler_params=pltpu.CompilerParams(vmem_limit_bytes=24 << 20),
+        out_shape=out_shape,
+        in_specs=[SMEM] + [VMEM] * 6,
+        out_specs=VMEM if whole else (VMEM, VMEM),
+        compiler_params=PARAMS,
         name="dyson",
-    )(weights, *near(own, one, two, base))
+    )(weights, *near(sigma, own, one, two, *base))
 
 
 def source_index(neighbours, atoms):
@@ -204,13 +245,21 @@
 
 def per_device(green0, grad_h, neighbours, shifts, coupling):
     energies, atoms = green0.shape[:2]
+    base = real, imag = parts(green0)
     right, left = prepare(grad_h)
     index = source_index(neighbours, atoms)
     weights = shift_weights(shifts, coupling, energies)
-    green = green0
     for step in range(ITERS):
-        inner = sandwich(index, right, left, green, *trade(green, "space", 1))
-        green = dyson(weights, inner, *trade(inner, "energy", 0), green0)
+        real_beside = trade(real, "energy", 0)
+        imag_beside = trade(imag, "space", 1)
+        summed = shift_sum(weights, real, *real_beside)
+        summed_beside = trade(summed, "space", 1)
+        inner = sandwich(index, right, left, imag, *imag_beside)
+        inner_beside = trade(inner, "energy", 0)
+        sigma = sandwich(index, right, left, summed, *summed_beside)
+        green = dyson(weights, sigma, inner, *inner_beside, base, step == ITERS - 1)
+        if step < ITERS - 1:
+            real, imag = green
     return green
 
 

time: 70.4 us -> 52 us (0.74)
  waiting for transfers between devices: 47.3 us -> 16.7 us
  starting transfers between devices: 9.61 us -> 17.3 us
  Pallas kernels: 10.4 us -> 14.3 us
    ppermute x8 -> x16, waiting for transfers between devices: 47.3 us -> 16.7 us  [trade(): got.append(lax.ppermute(edge, AXES, swaps(axis, parity)))]
    ppermute x8 -> x16, starting transfers between devices: 9.61 us -> 17.3 us  [trade(): got.append(lax.ppermute(edge, AXES, swaps(axis, parity)))]
    pallas_call x2 -> x4, Pallas kernels: 6.22 us -> 8.86 us  [sandwich(): pl.pallas_call(sandwich_kernel, out_shape=at_hand(own.shape), in_specs=[S...]
    pallas_call x2 -> x5, Pallas kernels: 3.59 us -> 4.84 us  [the longest x2 3.48 us: dyson(): pl.pallas_call(dyson_kernel, out_shape=out_shape, in_specs=[SMEM] + [VMEM...]
  transfers between devices with their start and end apart: 8 -> 16, of which waited for: 4 -> 5; matrix products, arithmetic and copies ran while one was open for 0% -> 1% of each run, Pallas kernels for 1% -> 21%
where the time goes in v3:
time: 52 us; the launch traced here: 51.8 us
  starting transfers between devices  17.3 us (33%)
  waiting for transfers between devices  16.7 us (32%)
  Pallas kernels  14.3 us (28%)
  local copies, waits for them, and re-layouts  2.95 us (6%)
    ppermute x16, starting transfers between devices, trade(): got.append(lax.ppermute(edge, AXES, swaps(axis, parity)))  17.3 us
    ppermute x16, waiting for transfers between devices, trade(): got.append(lax.ppermute(edge, AXES, swaps(axis, parity)))  16.7 us
    pallas_call x4, Pallas kernels, sandwich(): pl.pallas_call(sandwich_kernel, out_shape=at_hand(own.shape), in_specs=[S...  8.86 us
    pallas_call x2, Pallas kernels, dyson(): pl.pallas_call(dyson_kernel, out_shape=out_shape, in_specs=[SMEM] + [VMEM...  3.48 us
    unnamed x10, local copies, waits for them, and re-layouts  2.93 us
    pallas_call x2, Pallas kernels, shift_sum(): pl.pallas_call(shift_sum_kernel, out_shape=at_hand(own.shape), in_specs=[...  1.3 us
  transfers between devices with their start and end apart: 16, of which 5 were waited for; matrix products, arithmetic and copies ran while one was open for 1% of the time, Pallas kernels for 21%

profile of v3, /device:TPU:0, one launch (start us, length us, event | category | flops | bytes accessed | tf_op | source)
XLA Modules:
  0.0 51.8 jit_solution(17057652028587330597)
XLA Ops:
  0.0 1.0 %copy-done.1 = f32[2,2,2,128,128]{4,3,2,1,0:T(8,128)S(1)} copy-done((f32[2,2,2,128,128]{4,3,2,1,0:T(8,128)S(1)}, f32[2,2,2,128,128]{4,3,2,1,0:T(8,128)}, u32[]{:S(2)}) %copy-start.1) | copy-done | bytes 524312
  1.1 3.4 %collective-permute-start.1 = (f32[2,2,128,128]{3,2,1,0:T(8,128)S(1)}, f32[2,2,128,128]{3,2,1,0:T(8,128)S(1)}, u32[]{:S(2)}, u32[]{:S(2)}) collective-permute-start(f32[2,2,128,128]{3,2,1,0:T(8,128)S(1)} %get-tuple-element.13.own_ref.real_ref), channel_id=1, source_target_pairs={{0,28},{1,29},{2,30},{3,31},{4,8},{5,9},{6,10},{7,11},{8,4},{9,5},... | collective-permute-start | bytes 786440 | tf_op jit(solution)/shard_map/ppermute | solution.py:54
  4.5 0.5 collective-permute-start.5
  5.0 2.6 %collective-permute-start.4 = (f32[2,2,128,128]{3,2,1,0:T(8,128)S(1)}, f32[2,2,128,128]{3,2,1,0:T(8,128)S(1)}, u32[]{:S(2)}, u32[]{:S(2)}) collective-permute-start(f32[2,2,128,128]{3,2,1,0:T(8,128)S(1)} %get-tuple-element.14.own_ref.imag_ref), channel_id=1, source_target_pairs={{0,1},{1,0},{2,3},{3,2},{4,5},{5,4},{6,7},{7,6},{8,9},{9,8},{10,11... | collective-permute-start | bytes 786440 | tf_op jit(solution)/shard_map/ppermute | solution.py:54
  7.7 0.1 pad_add_fusion.1
  7.8 0.1 pad_add_fusion
  7.9 0.6 %copy-done.3 = f32[4]{0:T(128)S(1)} copy-done((f32[4]{0:T(128)S(1)}, f32[4]{0:T(128)}, u32[]{:S(2)}) %copy-start.3) | copy-done | bytes 40
  8.5 0.1 select_reduce_fusion.weight_ref
  8.6 1.2 %copy-done = f32[2,8,128,128]{3,2,1,0:T(8,128)S(1)} copy-done((f32[2,8,128,128]{3,2,1,0:T(8,128)S(1)}, f32[2,8,128,128]{3,2,1,0:T(8,128)}, u32[]{:S(2)}) %copy-start) | copy-done | bytes 1048600
  9.8 0.6 %prepare.1 = (bf16[2,8,128,256]{3,2,1,0:T(8,128)(2,1)S(1)}, bf16[2,256,1024]{2,1,0:T(8,128)(2,1)S(1)}) custom-call(f32[2,8,128,128]{3,2,1,0:T(8,128)S(1)} %copy-done), custom_call_target="tpu_custom_call" | custom-call | tf_op jit(solution)/shard_map/prepare/pallas_call | solution.py:81
  10.4 0.1 copy-done.2
  10.5 0.7 %shift_sum.2.own_ref = f32[2,2,128,128]{3,2,1,0:T(8,128)S(1)} custom-call(f32[2,6]{1,0:T(2,128)S(1)} %select_reduce_fusion.weight_ref, f32[2,2,128,128]{3,2,1,0:T(8,128)S(1)} %get-tuple-element.13.own_ref.real_ref, f32[2,2,128,128]{3,2,1,0:T(8,128)S(1)} %collective-permute-done.one_ref, f32[2,2,128,128]{3,2,1,0:T(8,128)S(1)} %collective-permute-done.1.two_ref), custom_call_target="tpu_custom_call" | custom-call | tf_op jit(solution)/shard_map/shift_sum/pallas_call | solution.py:175
  11.2 0.1 collective-permute-start.3
  11.3 4.6 %collective-permute-start.2 = (f32[2,2,128,128]{3,2,1,0:T(8,128)S(1)}, f32[2,2,128,128]{3,2,1,0:T(8,128)S(1)}, u32[]{:S(2)}, u32[]{:S(2)}) collective-permute-start(f32[2,2,128,128]{3,2,1,0:T(8,128)S(1)} %shift_sum.2.own_ref), channel_id=1, source_target_pairs={{0,1},{1,0},{2,3},{3,2},{4,5},{5,4},{6,7},{7,6},{8,9},{9,8},{10,11... | collective-permute-start | bytes 786440 | tf_op jit(solution)/shard_map/ppermute | solution.py:54
  15.9 2.2 %sandwich.5.own_ref = f32[2,2,128,128]{3,2,1,0:T(8,128)S(1)} custom-call(s32[2,8]{1,0:T(2,128)S(1)} %compare_select_fusion.1.index_ref, bf16[2,8,128,256]{3,2,1,0:T(8,128)(2,1)S(1)} %get-tuple-element.11.right_ref, bf16[2,256,1024]{2,1,0:T(8,128)(2,1)S(1)} %get-tuple-element.12.left_ref, f32[2,2,128,128]{3,2,1,0:T(8,128)S(1)} %get-tuple-element.14.own_ref.imag_ref, ...), custom_call_target="tpu_custom_call" | custom-call | tf_op jit(solution)/shard_map/sandwich/pallas_call | solution.py:124
  18.2 0.5 %collective-permute-start.7 = (f32[2,2,128,128]{3,2,1,0:T(8,128)S(1)}, f32[2,2,128,128]{3,2,1,0:T(8,128)S(1)}, u32[]{:S(2)}, u32[]{:S(2)}) collective-permute-start(f32[2,2,128,128]{3,2,1,0:T(8,128)S(1)} %sandwich.5.own_ref), channel_id=1, source_target_pairs={{0,28},{1,29},{2,30},{3,31},{4,8},{5,9},{6,10},{7,11},{8,4},{9,5},... | collective-permute-start | bytes 786440 | tf_op jit(solution)/shard_map/ppermute | solution.py:54
  18.7 1.9 %collective-permute-done.2.one_ref = f32[2,2,128,128]{3,2,1,0:T(8,128)S(1)} collective-permute-done((f32[2,2,128,128]{3,2,1,0:T(8,128)S(1)}, f32[2,2,128,128]{3,2,1,0:T(8,128)S(1)}, u32[]{:S(2)}, u32[]{:S(2)}) %collective-permute-start.2) | collective-permute-done | bytes 262176 | tf_op jit(solution)/shard_map/ppermute | solution.py:54
  20.6 2.2 %sandwich.4.sigma_ref = f32[2,2,128,128]{3,2,1,0:T(8,128)S(1)} custom-call(s32[2,8]{1,0:T(2,128)S(1)} %compare_select_fusion.1.index_ref, bf16[2,8,128,256]{3,2,1,0:T(8,128)(2,1)S(1)} %get-tuple-element.11.right_ref, bf16[2,256,1024]{2,1,0:T(8,128)(2,1)S(1)} %get-tuple-element.12.left_ref, f32[2,2,128,128]{3,2,1,0:T(8,128)S(1)} %shift_sum.2.own_ref, ...), custom_call_target="tpu_custom_call" | custom-call | tf_op jit(solution)/shard_map/sandwich/pallas_call | solution.py:124
  22.8 4.2 %collective-permute-done.7.two_ref = f32[2,2,128,128]{3,2,1,0:T(8,128)S(1)} collective-permute-done((f32[2,2,128,128]{3,2,1,0:T(8,128)S(1)}, f32[2,2,128,128]{3,2,1,0:T(8,128)S(1)}, u32[]{:S(2)}, u32[]{:S(2)}) %collective-permute-start.7) | collective-permute-done | bytes 262176 | tf_op jit(solution)/shard_map/ppermute | solution.py:54
  27.0 1.3 %dyson.2 = (f32[2,2,128,128]{3,2,1,0:T(8,128)S(1)}, f32[2,2,128,128]{3,2,1,0:T(8,128)S(1)}) custom-call(f32[2,6]{1,0:T(2,128)S(1)} %select_reduce_fusion.weight_ref, f32[2,2,128,128]{3,2,1,0:T(8,128)S(1)} %sandwich.4.sigma_ref, f32[2,2,128,128]{3,2,1,0:T(8,128)S(1)} %sandwich.5.own_ref, f32[2,2,128,128]{3,2,1,0:T(8,128)S(1)} %collective-permute-done.6.one_ref, ...), custom_call_target="tpu_custom_call" | custom-call | tf_op jit(solution)/shard_map/dyson/pallas_call | solution.py:214
  28.4 0.1 collective-permute-start.9
  28.5 0.5 collective-permute-start.13
  29.0 2.5 %collective-permute-start.12 = (f32[2,2,128,128]{3,2,1,0:T(8,128)S(1)}, f32[2,2,128,128]{3,2,1,0:T(8,128)S(1)}, u32[]{:S(2)}, u32[]{:S(2)}) collective-permute-start(f32[2,2,128,128]{3,2,1,0:T(8,128)S(1)} %get-tuple-element.16.own_ref), channel_id=1, source_target_pairs={{0,1},{1,0},{2,3},{3,2},{4,5},{5,4},{6,7},{7,6},{8,9},{9,8},{10,11... | collective-permute-start | bytes 786440 | tf_op jit(solution)/shard_map/ppermute | solution.py:54
  31.5 5.2 %collective-permute-done.9.two_ref = f32[2,2,128,128]{3,2,1,0:T(8,128)S(1)} collective-permute-done((f32[2,2,128,128]{3,2,1,0:T(8,128)S(1)}, f32[2,2,128,128]{3,2,1,0:T(8,128)S(1)}, u32[]{:S(2)}, u32[]{:S(2)}) %collective-permute-start.9) | collective-permute-done | bytes 262176 | tf_op jit(solution)/shard_map/ppermute | solution.py:54
  36.7 0.7 %shift_sum.3.own_ref = f32[2,2,128,128]{3,2,1,0:T(8,128)S(1)} custom-call(f32[2,6]{1,0:T(2,128)S(1)} %select_reduce_fusion.weight_ref, f32[2,2,128,128]{3,2,1,0:T(8,128)S(1)} %get-tuple-element.15.own_ref, f32[2,2,128,128]{3,2,1,0:T(8,128)S(1)} %collective-permute-done.8.one_ref, f32[2,2,128,128]{3,2,1,0:T(8,128)S(1)} %collective-permute-done.9.two_ref), custom_call_target="tpu_custom_call" | custom-call | tf_op jit(solution)/shard_map/shift_sum/pallas_call | solution.py:175
  37.5 2.1 %collective-permute-start.10 = (f32[2,2,128,128]{3,2,1,0:T(8,128)S(1)}, f32[2,2,128,128]{3,2,1,0:T(8,128)S(1)}, u32[]{:S(2)}, u32[]{:S(2)}) collective-permute-start(f32[2,2,128,128]{3,2,1,0:T(8,128)S(1)} %shift_sum.3.own_ref), channel_id=1, source_target_pairs={{0,1},{1,0},{2,3},{3,2},{4,5},{5,4},{6,7},{7,6},{8,9},{9,8},{10,11... | collective-permute-start | bytes 786440 | tf_op jit(solution)/shard_map/ppermute | solution.py:54
  39.6 2.2 %sandwich.7.own_ref = f32[2,2,128,128]{3,2,1,0:T(8,128)S(1)} custom-call(s32[2,8]{1,0:T(2,128)S(1)} %compare_select_fusion.1.index_ref, bf16[2,8,128,256]{3,2,1,0:T(8,128)(2,1)S(1)} %get-tuple-element.11.right_ref, bf16[2,256,1024]{2,1,0:T(8,128)(2,1)S(1)} %get-tuple-element.12.left_ref, f32[2,2,128,128]{3,2,1,0:T(8,128)S(1)} %get-tuple-element.16.own_ref, ...), custom_call_target="tpu_custom_call" | custom-call | tf_op jit(solution)/shard_map/sandwich/pallas_call | solution.py:124
  41.8 0.1 collective-permute-start.15
  42.0 4.2 %collective-permute-done.10.one_ref = f32[2,2,128,128]{3,2,1,0:T(8,128)S(1)} collective-permute-done((f32[2,2,128,128]{3,2,1,0:T(8,128)S(1)}, f32[2,2,128,128]{3,2,1,0:T(8,128)S(1)}, u32[]{:S(2)}, u32[]{:S(2)}) %collective-permute-start.10) | collective-permute-done | bytes 262176 | tf_op jit(solution)/shard_map/ppermute | solution.py:54
  46.2 2.2 %sandwich.6.sigma_ref = f32[2,2,128,128]{3,2,1,0:T(8,128)S(1)} custom-call(s32[2,8]{1,0:T(2,128)S(1)} %compare_select_fusion.1.index_ref, bf16[2,8,128,256]{3,2,1,0:T(8,128)(2,1)S(1)} %get-tuple-element.11.right_ref, bf16[2,256,1024]{2,1,0:T(8,128)(2,1)S(1)} %get-tuple-element.12.left_ref, f32[2,2,128,128]{3,2,1,0:T(8,128)S(1)} %shift_sum.3.own_ref, ...), custom_call_target="tpu_custom_call" | custom-call | tf_op jit(solution)/shard_map/sandwich/pallas_call | solution.py:124
  48.4 1.2 %collective-permute-done.15.two_ref = f32[2,2,128,128]{3,2,1,0:T(8,128)S(1)} collective-permute-done((f32[2,2,128,128]{3,2,1,0:T(8,128)S(1)}, f32[2,2,128,128]{3,2,1,0:T(8,128)S(1)}, u32[]{:S(2)}, u32[]{:S(2)}) %collective-permute-start.15) | collective-permute-done | bytes 262176 | tf_op jit(solution)/shard_map/ppermute | solution.py:54
  49.6 2.1 %dyson.3 = f32[2,2,2,128,128]{4,3,2,1,0:T(8,128)} custom-call(f32[2,6]{1,0:T(2,128)S(1)} %select_reduce_fusion.weight_ref, f32[2,2,128,128]{3,2,1,0:T(8,128)S(1)} %sandwich.6.sigma_ref, f32[2,2,128,128]{3,2,1,0:T(8,128)S(1)} %sandwich.7.own_ref, f32[2,2,128,128]{3,2,1,0:T(8,128)S(1)} %collective-permute-done.14.one_ref, ...), custom_call_target="tpu_custom_call" | custom-call | tf_op jit(solution)/shard_map/dyson/pallas_call | solution.py:214
  (30 shorter events, 0.3 us)
Async XLA Ops:
  0.0 1.0 %copy-start.1 = (f32[2,2,2,128,128]{4,3,2,1,0:T(8,128)S(1)}, f32[2,2,2,128,128]{4,3,2,1,0:T(8,128)}, u32[]{:S(2)}) copy-start(f32[2,2,2,128,128]{4,3,2,1,0:T(8,128)} %green_ref.1) | copy-start | bytes 1572868
  1.1 9.4 %collective-permute-start.1 = (f32[2,2,128,128]{3,2,1,0:T(8,128)S(1)}, f32[2,2,128,128]{3,2,1,0:T(8,128)S(1)}, u32[]{:S(2)}, u32[]{:S(2)}) collective-permute-start(f32[2,2,128,128]{3,2,1,0:T(8,128)S(1)} %get-tuple-element.13.own_ref.real_ref), channel_id=1, source_target_pairs={{0,28},{1,29},{2,30},{3,31},{4,8},{5,9},{6,10},{7,11},{8,4},{9,5},... | collective-permute-start | bytes 786440 | tf_op jit(solution)/shard_map/ppermute | solution.py:54
  4.5 6.0 %collective-permute-start = (f32[2,2,128,128]{3,2,1,0:T(8,128)S(1)}, f32[2,2,128,128]{3,2,1,0:T(8,128)S(1)}, u32[]{:S(2)}, u32[]{:S(2)}) collective-permute-start(f32[2,2,128,128]{3,2,1,0:T(8,128)S(1)} %get-tuple-element.13.own_ref.real_ref), channel_id=1, source_target_pairs={{0,4},{1,5},{2,6},{3,7},{4,0},{5,1},{6,2},{7,3},{8,12},{9,13},{10,... | collective-permute-start | bytes 786440 | tf_op jit(solution)/shard_map/ppermute | solution.py:54
  4.5 11.4 %collective-permute-start.5 = (f32[2,2,128,128]{3,2,1,0:T(8,128)S(1)}, f32[2,2,128,128]{3,2,1,0:T(8,128)S(1)}, u32[]{:S(2)}, u32[]{:S(2)}) collective-permute-start(f32[2,2,128,128]{3,2,1,0:T(8,128)S(1)} %get-tuple-element.14.own_ref.imag_ref), channel_id=1, source_target_pairs={{0,4},{1,2},{2,1},{3,7},{4,0},{5,6},{6,5},{7,3},{8,12},{9,10},{10,... | collective-permute-start | bytes 786440 | tf_op jit(solution)/shard_map/ppermute | solution.py:54
  5.0 10.9 %collective-permute-start.4 = (f32[2,2,128,128]{3,2,1,0:T(8,128)S(1)}, f32[2,2,128,128]{3,2,1,0:T(8,128)S(1)}, u32[]{:S(2)}, u32[]{:S(2)}) collective-permute-start(f32[2,2,128,128]{3,2,1,0:T(8,128)S(1)} %get-tuple-element.14.own_ref.imag_ref), channel_id=1, source_target_pairs={{0,1},{1,0},{2,3},{3,2},{4,5},{5,4},{6,7},{7,6},{8,9},{9,8},{10,11... | collective-permute-start | bytes 786440 | tf_op jit(solution)/shard_map/ppermute | solution.py:54
  7.8 0.7 %copy-start.3 = (f32[4]{0:T(128)S(1)}, f32[4]{0:T(128)}, u32[]{:S(2)}) copy-start(f32[4]{0:T(128)} %param.9) | copy-start | bytes 52
  7.8 0.7 %copy-start.4 = (s32[4]{0:T(128)S(1)}, s32[4]{0:T(128)}, u32[]{:S(2)}) copy-start(s32[4]{0:T(128)} %param.8) | copy-start | bytes 52
  8.6 1.2 %copy-start = (f32[2,8,128,128]{3,2,1,0:T(8,128)S(1)}, f32[2,8,128,128]{3,2,1,0:T(8,128)}, u32[]{:S(2)}) copy-start(f32[2,8,128,128]{3,2,1,0:T(8,128)} %grad_ref.1) | copy-start | bytes 3145732
  9.8 0.7 %copy-start.2 = (s32[2,8]{1,0:T(2,128)S(1)}, s32[2,8]{1,0:T(2,128)}, u32[]{:S(2)}) copy-start(s32[2,8]{1,0:T(2,128)} %param.7) | copy-start | bytes 196
  11.2 7.5 %collective-permute-start.3 = (f32[2,2,128,128]{3,2,1,0:T(8,128)S(1)}, f32[2,2,128,128]{3,2,1,0:T(8,128)S(1)}, u32[]{:S(2)}, u32[]{:S(2)}) collective-permute-start(f32[2,2,128,128]{3,2,1,0:T(8,128)S(1)} %shift_sum.2.own_ref), channel_id=1, source_target_pairs={{0,4},{1,2},{2,1},{3,7},{4,0},{5,6},{6,5},{7,3},{8,12},{9,10},{10,... | collective-permute-start | bytes 786440 | tf_op jit(solution)/shard_map/ppermute | solution.py:54
  11.3 9.3 %collective-permute-start.2 = (f32[2,2,128,128]{3,2,1,0:T(8,128)S(1)}, f32[2,2,128,128]{3,2,1,0:T(8,128)S(1)}, u32[]{:S(2)}, u32[]{:S(2)}) collective-permute-start(f32[2,2,128,128]{3,2,1,0:T(8,128)S(1)} %shift_sum.2.own_ref), channel_id=1, source_target_pairs={{0,1},{1,0},{2,3},{3,2},{4,5},{5,4},{6,7},{7,6},{8,9},{9,8},{10,11... | collective-permute-start | bytes 786440 | tf_op jit(solution)/shard_map/ppermute | solution.py:54
  18.2 8.8 %collective-permute-start.7 = (f32[2,2,128,128]{3,2,1,0:T(8,128)S(1)}, f32[2,2,128,128]{3,2,1,0:T(8,128)S(1)}, u32[]{:S(2)}, u32[]{:S(2)}) collective-permute-start(f32[2,2,128,128]{3,2,1,0:T(8,128)S(1)} %sandwich.5.own_ref), channel_id=1, source_target_pairs={{0,28},{1,29},{2,30},{3,31},{4,8},{5,9},{6,10},{7,11},{8,4},{9,5},... | collective-permute-start | bytes 786440 | tf_op jit(solution)/shard_map/ppermute | solution.py:54
  18.7 8.3 %collective-permute-start.6 = (f32[2,2,128,128]{3,2,1,0:T(8,128)S(1)}, f32[2,2,128,128]{3,2,1,0:T(8,128)S(1)}, u32[]{:S(2)}, u32[]{:S(2)}) collective-permute-start(f32[2,2,128,128]{3,2,1,0:T(8,128)S(1)} %sandwich.5.own_ref), channel_id=1, source_target_pairs={{0,4},{1,5},{2,6},{3,7},{4,0},{5,1},{6,2},{7,3},{8,12},{9,13},{10,... | collective-permute-start | bytes 786440 | tf_op jit(solution)/shard_map/ppermute | solution.py:54
  28.4 8.4 %collective-permute-start.9 = (f32[2,2,128,128]{3,2,1,0:T(8,128)S(1)}, f32[2,2,128,128]{3,2,1,0:T(8,128)S(1)}, u32[]{:S(2)}, u32[]{:S(2)}) collective-permute-start(f32[2,2,128,128]{3,2,1,0:T(8,128)S(1)} %get-tuple-element.15.own_ref), channel_id=1, source_target_pairs={{0,28},{1,29},{2,30},{3,31},{4,8},{5,9},{6,10},{7,11},{8,4},{9,5},... | collective-permute-start | bytes 786440 | tf_op jit(solution)/shard_map/ppermute | solution.py:54
  28.4 8.3 %collective-permute-start.8 = (f32[2,2,128,128]{3,2,1,0:T(8,128)S(1)}, f32[2,2,128,128]{3,2,1,0:T(8,128)S(1)}, u32[]{:S(2)}, u32[]{:S(2)}) collective-permute-start(f32[2,2,128,128]{3,2,1,0:T(8,128)S(1)} %get-tuple-element.15.own_ref), channel_id=1, source_target_pairs={{0,4},{1,5},{2,6},{3,7},{4,0},{5,1},{6,2},{7,3},{8,12},{9,13},{10,... | collective-permute-start | bytes 786440 | tf_op jit(solution)/shard_map/ppermute | solution.py:54
  28.5 11.1 %collective-permute-start.13 = (f32[2,2,128,128]{3,2,1,0:T(8,128)S(1)}, f32[2,2,128,128]{3,2,1,0:T(8,128)S(1)}, u32[]{:S(2)}, u32[]{:S(2)}) collective-permute-start(f32[2,2,128,128]{3,2,1,0:T(8,128)S(1)} %get-tuple-element.16.own_ref), channel_id=1, source_target_pairs={{0,4},{1,2},{2,1},{3,7},{4,0},{5,6},{6,5},{7,3},{8,12},{9,10},{10,... | collective-permute-start | bytes 786440 | tf_op jit(solution)/shard_map/ppermute | solution.py:54
  29.0 10.6 %collective-permute-start.12 = (f32[2,2,128,128]{3,2,1,0:T(8,128)S(1)}, f32[2,2,128,128]{3,2,1,0:T(8,128)S(1)}, u32[]{:S(2)}, u32[]{:S(2)}) collective-permute-start(f32[2,2,128,128]{3,2,1,0:T(8,128)S(1)} %get-tuple-element.16.own_ref), channel_id=1, source_target_pairs={{0,1},{1,0},{2,3},{3,2},{4,5},{5,4},{6,7},{7,6},{8,9},{9,8},{10,11... | collective-permute-start | bytes 786440 | tf_op jit(solution)/shard_map/ppermute | solution.py:54
  37.4 4.6 %collective-permute-start.11 = (f32[2,2,128,128]{3,2,1,0:T(8,128)S(1)}, f32[2,2,128,128]{3,2,1,0:T(8,128)S(1)}, u32[]{:S(2)}, u32[]{:S(2)}) collective-permute-start(f32[2,2,128,128]{3,2,1,0:T(8,128)S(1)} %shift_sum.3.own_ref), channel_id=1, source_target_pairs={{0,4},{1,2},{2,1},{3,7},{4,0},{5,6},{6,5},{7,3},{8,12},{9,10},{10,... | collective-permute-start | bytes 786440 | tf_op jit(solution)/shard_map/ppermute | solution.py:54
  37.5 8.7 %collective-permute-start.10 = (f32[2,2,128,128]{3,2,1,0:T(8,128)S(1)}, f32[2,2,128,128]{3,2,1,0:T(8,128)S(1)}, u32[]{:S(2)}, u32[]{:S(2)}) collective-permute-start(f32[2,2,128,128]{3,2,1,0:T(8,128)S(1)} %shift_sum.3.own_ref), channel_id=1, source_target_pairs={{0,1},{1,0},{2,3},{3,2},{4,5},{5,4},{6,7},{7,6},{8,9},{9,8},{10,11... | collective-permute-start | bytes 786440 | tf_op jit(solution)/shard_map/ppermute | solution.py:54
  41.8 7.8 %collective-permute-start.15 = (f32[2,2,128,128]{3,2,1,0:T(8,128)S(1)}, f32[2,2,128,128]{3,2,1,0:T(8,128)S(1)}, u32[]{:S(2)}, u32[]{:S(2)}) collective-permute-start(f32[2,2,128,128]{3,2,1,0:T(8,128)S(1)} %sandwich.7.own_ref), channel_id=1, source_target_pairs={{0,28},{1,29},{2,30},{3,31},{4,8},{5,9},{6,10},{7,11},{8,4},{9,5},... | collective-permute-start | bytes 786440 | tf_op jit(solution)/shard_map/ppermute | solution.py:54
  42.0 7.7 %collective-permute-start.14 = (f32[2,2,128,128]{3,2,1,0:T(8,128)S(1)}, f32[2,2,128,128]{3,2,1,0:T(8,128)S(1)}, u32[]{:S(2)}, u32[]{:S(2)}) collective-permute-start(f32[2,2,128,128]{3,2,1,0:T(8,128)S(1)} %sandwich.7.own_ref), channel_id=1, source_target_pairs={{0,4},{1,5},{2,6},{3,7},{4,0},{5,1},{6,2},{7,3},{8,12},{9,13},{10,... | collective-permute-start | bytes 786440 | tf_op jit(solution)/shard_map/ppermute | solution.py:54

commit v4 on v3

--- a/solution.py
+++ b/solution.py
@@ -33,7 +33,7 @@
             elif axis == "space" and sizes["energy"] % 2 == 0:
                 to["energy"] = energy ^ 1
             elif axis == "energy" and count % 2 == 0:
-                to["energy"] = there % count
+                to["space"] = space ^ 1
             pairs.append((energy * sizes["space"] + space, to["energy"] * sizes["space"] + to["space"]))
     return pairs
 
@@ -154,7 +154,7 @@
         scratch_shapes=[pltpu.SemaphoreType.DMA((2,))],
         compiler_params=PARAMS,
         name="parts",
-    )(green)
+    )(pltpu.with_memory_space_constraint(green, pltpu.HBM))
 
 
 def shifted(weight_ref, refs, e, a):

time: 52 us -> 49.4 us (0.950)
  the two profiles are of different devices: /device:TPU:0 before, /device:TPU:12 now
where the time goes in v4:
time: 49.4 us; the launch traced here: 49.2 us
  waiting for transfers between devices  20.1 us (41%)
  Pallas kernels  15.3 us (31%)
  starting transfers between devices  11.4 us (23%)
  local copies, waits for them, and re-layouts  1.91 us (4%)
    ppermute x16, waiting for transfers between devices, trade(): got.append(lax.ppermute(edge, AXES, swaps(axis, parity)))  20.1 us
    ppermute x16, starting transfers between devices, trade(): got.append(lax.ppermute(edge, AXES, swaps(axis, parity)))  11.4 us
    pallas_call x4, Pallas kernels, sandwich(): pl.pallas_call(sandwich_kernel, out_shape=at_hand(own.shape), in_specs=[S...  8.85 us
    pallas_call x2, Pallas kernels, dyson(): pl.pallas_call(dyson_kernel, out_shape=out_shape, in_specs=[SMEM] + [VMEM...  3.48 us
    unnamed x8, local copies, waits for them, and re-layouts  1.89 us
    pallas_call x2, Pallas kernels, shift_sum(): pl.pallas_call(shift_sum_kernel, out_shape=at_hand(own.shape), in_specs=[...  1.3 us
    pallas_call x1, Pallas kernels, parts(): pl.pallas_call(parts_kernel, out_shape=(at_hand(shape), at_hand(shape)),...  1.04 us
  transfers between devices with their start and end apart: 16, of which 10 were waited for; matrix products, arithmetic and copies ran while one was open for 1% of the time, Pallas kernels for 22%

profile of v4, /device:TPU:12, one launch (start us, length us, event | category | flops | bytes accessed | tf_op | source)
XLA Modules:
  0.0 49.2 jit_solution(15950613197217485685)
XLA Ops:
  0.0 1.0 %parts.1 = (f32[2,2,128,128]{3,2,1,0:T(8,128)S(1)}, f32[2,2,128,128]{3,2,1,0:T(8,128)S(1)}) custom-call(f32[2,2,2,128,128]{4,3,2,1,0:T(8,128)} %green_ref.1), custom_call_target="tpu_custom_call" | custom-call | tf_op jit(solution)/shard_map/parts/pallas_call | solution.py:149
  1.1 0.9 %collective-permute-start.1 = (f32[2,2,128,128]{3,2,1,0:T(8,128)S(1)}, f32[2,2,128,128]{3,2,1,0:T(8,128)S(1)}, u32[]{:S(2)}, u32[]{:S(2)}) collective-permute-start(f32[2,2,128,128]{3,2,1,0:T(8,128)S(1)} %get-tuple-element.13.own_ref.real_ref), channel_id=1, source_target_pairs={{0,1},{1,0},{2,3},{3,2},{4,8},{5,9},{6,10},{7,11},{8,4},{9,5},{10,... | collective-permute-start | bytes 786440 | tf_op jit(solution)/shard_map/ppermute | solution.py:54
  2.0 0.7 %collective-permute-start = (f32[2,2,128,128]{3,2,1,0:T(8,128)S(1)}, f32[2,2,128,128]{3,2,1,0:T(8,128)S(1)}, u32[]{:S(2)}, u32[]{:S(2)}) collective-permute-start(f32[2,2,128,128]{3,2,1,0:T(8,128)S(1)} %get-tuple-element.13.own_ref.real_ref), channel_id=1, source_target_pairs={{0,4},{1,5},{2,6},{3,7},{4,0},{5,1},{6,2},{7,3},{8,12},{9,13},{10,... | collective-permute-start | bytes 786440 | tf_op jit(solution)/shard_map/ppermute | solution.py:54
  2.7 1.6 %collective-permute-start.5 = (f32[2,2,128,128]{3,2,1,0:T(8,128)S(1)}, f32[2,2,128,128]{3,2,1,0:T(8,128)S(1)}, u32[]{:S(2)}, u32[]{:S(2)}) collective-permute-start(f32[2,2,128,128]{3,2,1,0:T(8,128)S(1)} %get-tuple-element.14.own_ref.imag_ref), channel_id=1, source_target_pairs={{0,4},{1,2},{2,1},{3,7},{4,0},{5,6},{6,5},{7,3},{8,12},{9,10},{10,... | collective-permute-start | bytes 786440 | tf_op jit(solution)/shard_map/ppermute | solution.py:54
  4.5 0.6 %copy-done.2 = f32[4]{0:T(128)S(1)} copy-done((f32[4]{0:T(128)S(1)}, f32[4]{0:T(128)}, u32[]{:S(2)}) %copy-start.2) | copy-done | bytes 40
  5.2 1.2 %copy-done = f32[2,8,128,128]{3,2,1,0:T(8,128)S(1)} copy-done((f32[2,8,128,128]{3,2,1,0:T(8,128)S(1)}, f32[2,8,128,128]{3,2,1,0:T(8,128)}, u32[]{:S(2)}) %copy-start) | copy-done | bytes 1048600
  6.4 0.6 %prepare.1 = (bf16[2,8,128,256]{3,2,1,0:T(8,128)(2,1)S(1)}, bf16[2,256,1024]{2,1,0:T(8,128)(2,1)S(1)}) custom-call(f32[2,8,128,128]{3,2,1,0:T(8,128)S(1)} %copy-done), custom_call_target="tpu_custom_call" | custom-call | tf_op jit(solution)/shard_map/prepare/pallas_call | solution.py:81
  7.1 2.6 %collective-permute-done.1.two_ref = f32[2,2,128,128]{3,2,1,0:T(8,128)S(1)} collective-permute-done((f32[2,2,128,128]{3,2,1,0:T(8,128)S(1)}, f32[2,2,128,128]{3,2,1,0:T(8,128)S(1)}, u32[]{:S(2)}, u32[]{:S(2)}) %collective-permute-start.1) | collective-permute-done | bytes 262176 | tf_op jit(solution)/shard_map/ppermute | solution.py:54
  9.7 0.7 %shift_sum.2.own_ref = f32[2,2,128,128]{3,2,1,0:T(8,128)S(1)} custom-call(f32[2,6]{1,0:T(2,128)S(1)} %select_reduce_fusion.weight_ref, f32[2,2,128,128]{3,2,1,0:T(8,128)S(1)} %get-tuple-element.13.own_ref.real_ref, f32[2,2,128,128]{3,2,1,0:T(8,128)S(1)} %collective-permute-done.one_ref, f32[2,2,128,128]{3,2,1,0:T(8,128)S(1)} %collective-permute-done.1.two_ref), custom_call_target="tpu_custom_call" | custom-call | tf_op jit(solution)/shard_map/shift_sum/pallas_call | solution.py:175
  10.4 1.6 %collective-permute-start.3 = (f32[2,2,128,128]{3,2,1,0:T(8,128)S(1)}, f32[2,2,128,128]{3,2,1,0:T(8,128)S(1)}, u32[]{:S(2)}, u32[]{:S(2)}) collective-permute-start(f32[2,2,128,128]{3,2,1,0:T(8,128)S(1)} %shift_sum.2.own_ref), channel_id=1, source_target_pairs={{0,4},{1,2},{2,1},{3,7},{4,0},{5,6},{6,5},{7,3},{8,12},{9,10},{10,... | collective-permute-start | bytes 786440 | tf_op jit(solution)/shard_map/ppermute | solution.py:54
  12.0 0.2 collective-permute-done.4.one_ref
  12.2 2.2 %sandwich.5.own_ref = f32[2,2,128,128]{3,2,1,0:T(8,128)S(1)} custom-call(s32[2,8]{1,0:T(2,128)S(1)} %compare_select_fusion.1.index_ref, bf16[2,8,128,256]{3,2,1,0:T(8,128)(2,1)S(1)} %get-tuple-element.11.right_ref, bf16[2,256,1024]{2,1,0:T(8,128)(2,1)S(1)} %get-tuple-element.12.left_ref, f32[2,2,128,128]{3,2,1,0:T(8,128)S(1)} %get-tuple-element.14.own_ref.imag_ref, ...), custom_call_target="tpu_custom_call" | custom-call | tf_op jit(solution)/shard_map/sandwich/pallas_call | solution.py:124
  14.5 1.3 %collective-permute-start.7 = (f32[2,2,128,128]{3,2,1,0:T(8,128)S(1)}, f32[2,2,128,128]{3,2,1,0:T(8,128)S(1)}, u32[]{:S(2)}, u32[]{:S(2)}) collective-permute-start(f32[2,2,128,128]{3,2,1,0:T(8,128)S(1)} %sandwich.5.own_ref), channel_id=1, source_target_pairs={{0,1},{1,0},{2,3},{3,2},{4,8},{5,9},{6,10},{7,11},{8,4},{9,5},{10,... | collective-permute-start | bytes 786440 | tf_op jit(solution)/shard_map/ppermute | solution.py:54
  15.9 1.9 %collective-permute-done.3.two_ref = f32[2,2,128,128]{3,2,1,0:T(8,128)S(1)} collective-permute-done((f32[2,2,128,128]{3,2,1,0:T(8,128)S(1)}, f32[2,2,128,128]{3,2,1,0:T(8,128)S(1)}, u32[]{:S(2)}, u32[]{:S(2)}) %collective-permute-start.3) | collective-permute-done | bytes 262176 | tf_op jit(solution)/shard_map/ppermute | solution.py:54
  17.8 1.3 %collective-permute-done.2.one_ref = f32[2,2,128,128]{3,2,1,0:T(8,128)S(1)} collective-permute-done((f32[2,2,128,128]{3,2,1,0:T(8,128)S(1)}, f32[2,2,128,128]{3,2,1,0:T(8,128)S(1)}, u32[]{:S(2)}, u32[]{:S(2)}) %collective-permute-start.2) | collective-permute-done | bytes 262176 | tf_op jit(solution)/shard_map/ppermute | solution.py:54
  19.1 2.2 %sandwich.4.sigma_ref = f32[2,2,128,128]{3,2,1,0:T(8,128)S(1)} custom-call(s32[2,8]{1,0:T(2,128)S(1)} %compare_select_fusion.1.index_ref, bf16[2,8,128,256]{3,2,1,0:T(8,128)(2,1)S(1)} %get-tuple-element.11.right_ref, bf16[2,256,1024]{2,1,0:T(8,128)(2,1)S(1)} %get-tuple-element.12.left_ref, f32[2,2,128,128]{3,2,1,0:T(8,128)S(1)} %shift_sum.2.own_ref, ...), custom_call_target="tpu_custom_call" | custom-call | tf_op jit(solution)/shard_map/sandwich/pallas_call | solution.py:124
  21.3 2.5 %collective-permute-done.7.two_ref = f32[2,2,128,128]{3,2,1,0:T(8,128)S(1)} collective-permute-done((f32[2,2,128,128]{3,2,1,0:T(8,128)S(1)}, f32[2,2,128,128]{3,2,1,0:T(8,128)S(1)}, u32[]{:S(2)}, u32[]{:S(2)}) %collective-permute-start.7) | collective-permute-done | bytes 262176 | tf_op jit(solution)/shard_map/ppermute | solution.py:54
  23.8 1.3 %dyson.2 = (f32[2,2,128,128]{3,2,1,0:T(8,128)S(1)}, f32[2,2,128,128]{3,2,1,0:T(8,128)S(1)}) custom-call(f32[2,6]{1,0:T(2,128)S(1)} %select_reduce_fusion.weight_ref, f32[2,2,128,128]{3,2,1,0:T(8,128)S(1)} %sandwich.4.sigma_ref, f32[2,2,128,128]{3,2,1,0:T(8,128)S(1)} %sandwich.5.own_ref, f32[2,2,128,128]{3,2,1,0:T(8,128)S(1)} %collective-permute-done.6.one_ref, ...), custom_call_target="tpu_custom_call" | custom-call | tf_op jit(solution)/shard_map/dyson/pallas_call | solution.py:214
  25.2 0.9 %collective-permute-start.9 = (f32[2,2,128,128]{3,2,1,0:T(8,128)S(1)}, f32[2,2,128,128]{3,2,1,0:T(8,128)S(1)}, u32[]{:S(2)}, u32[]{:S(2)}) collective-permute-start(f32[2,2,128,128]{3,2,1,0:T(8,128)S(1)} %get-tuple-element.15.own_ref), channel_id=1, source_target_pairs={{0,1},{1,0},{2,3},{3,2},{4,8},{5,9},{6,10},{7,11},{8,4},{9,5},{10,... | collective-permute-start | bytes 786440 | tf_op jit(solution)/shard_map/ppermute | solution.py:54
  26.1 1.6 %collective-permute-start.13 = (f32[2,2,128,128]{3,2,1,0:T(8,128)S(1)}, f32[2,2,128,128]{3,2,1,0:T(8,128)S(1)}, u32[]{:S(2)}, u32[]{:S(2)}) collective-permute-start(f32[2,2,128,128]{3,2,1,0:T(8,128)S(1)} %get-tuple-element.16.own_ref), channel_id=1, source_target_pairs={{0,4},{1,2},{2,1},{3,7},{4,0},{5,6},{6,5},{7,3},{8,12},{9,10},{10,... | collective-permute-start | bytes 786440 | tf_op jit(solution)/shard_map/ppermute | solution.py:54
  27.8 0.9 %collective-permute-start.12 = (f32[2,2,128,128]{3,2,1,0:T(8,128)S(1)}, f32[2,2,128,128]{3,2,1,0:T(8,128)S(1)}, u32[]{:S(2)}, u32[]{:S(2)}) collective-permute-start(f32[2,2,128,128]{3,2,1,0:T(8,128)S(1)} %get-tuple-element.16.own_ref), channel_id=1, source_target_pairs={{0,1},{1,0},{2,3},{3,2},{4,5},{5,4},{6,7},{7,6},{8,9},{9,8},{10,11... | collective-permute-start | bytes 786440 | tf_op jit(solution)/shard_map/ppermute | solution.py:54
  28.7 5.0 %collective-permute-done.9.two_ref = f32[2,2,128,128]{3,2,1,0:T(8,128)S(1)} collective-permute-done((f32[2,2,128,128]{3,2,1,0:T(8,128)S(1)}, f32[2,2,128,128]{3,2,1,0:T(8,128)S(1)}, u32[]{:S(2)}, u32[]{:S(2)}) %collective-permute-start.9) | collective-permute-done | bytes 262176 | tf_op jit(solution)/shard_map/ppermute | solution.py:54
  33.7 0.7 %shift_sum.3.own_ref = f32[2,2,128,128]{3,2,1,0:T(8,128)S(1)} custom-call(f32[2,6]{1,0:T(2,128)S(1)} %select_reduce_fusion.weight_ref, f32[2,2,128,128]{3,2,1,0:T(8,128)S(1)} %get-tuple-element.15.own_ref, f32[2,2,128,128]{3,2,1,0:T(8,128)S(1)} %collective-permute-done.8.one_ref, f32[2,2,128,128]{3,2,1,0:T(8,128)S(1)} %collective-permute-done.9.two_ref), custom_call_target="tpu_custom_call" | custom-call | tf_op jit(solution)/shard_map/shift_sum/pallas_call | solution.py:175
  34.3 1.3 %collective-permute-start.11 = (f32[2,2,128,128]{3,2,1,0:T(8,128)S(1)}, f32[2,2,128,128]{3,2,1,0:T(8,128)S(1)}, u32[]{:S(2)}, u32[]{:S(2)}) collective-permute-start(f32[2,2,128,128]{3,2,1,0:T(8,128)S(1)} %shift_sum.3.own_ref), channel_id=1, source_target_pairs={{0,4},{1,2},{2,1},{3,7},{4,0},{5,6},{6,5},{7,3},{8,12},{9,10},{10,... | collective-permute-start | bytes 786440 | tf_op jit(solution)/shard_map/ppermute | solution.py:54
  35.7 1.0 %collective-permute-done.12.one_ref = f32[2,2,128,128]{3,2,1,0:T(8,128)S(1)} collective-permute-done((f32[2,2,128,128]{3,2,1,0:T(8,128)S(1)}, f32[2,2,128,128]{3,2,1,0:T(8,128)S(1)}, u32[]{:S(2)}, u32[]{:S(2)}) %collective-permute-start.12) | collective-permute-done | bytes 262176 | tf_op jit(solution)/shard_map/ppermute | solution.py:54
  36.7 2.2 %sandwich.7.own_ref = f32[2,2,128,128]{3,2,1,0:T(8,128)S(1)} custom-call(s32[2,8]{1,0:T(2,128)S(1)} %compare_select_fusion.1.index_ref, bf16[2,8,128,256]{3,2,1,0:T(8,128)(2,1)S(1)} %get-tuple-element.11.right_ref, bf16[2,256,1024]{2,1,0:T(8,128)(2,1)S(1)} %get-tuple-element.12.left_ref, f32[2,2,128,128]{3,2,1,0:T(8,128)S(1)} %get-tuple-element.16.own_ref, ...), custom_call_target="tpu_custom_call" | custom-call | tf_op jit(solution)/shard_map/sandwich/pallas_call | solution.py:124
  38.9 0.4 collective-permute-start.15
  39.3 1.5 %collective-permute-done.11.two_ref = f32[2,2,128,128]{3,2,1,0:T(8,128)S(1)} collective-permute-done((f32[2,2,128,128]{3,2,1,0:T(8,128)S(1)}, f32[2,2,128,128]{3,2,1,0:T(8,128)S(1)}, u32[]{:S(2)}, u32[]{:S(2)}) %collective-permute-start.11) | collective-permute-done | bytes 262176 | tf_op jit(solution)/shard_map/ppermute | solution.py:54
  40.8 1.2 %collective-permute-done.10.one_ref = f32[2,2,128,128]{3,2,1,0:T(8,128)S(1)} collective-permute-done((f32[2,2,128,128]{3,2,1,0:T(8,128)S(1)}, f32[2,2,128,128]{3,2,1,0:T(8,128)S(1)}, u32[]{:S(2)}, u32[]{:S(2)}) %collective-permute-start.10) | collective-permute-done | bytes 262176 | tf_op jit(solution)/shard_map/ppermute | solution.py:54
  42.0 2.2 %sandwich.6.sigma_ref = f32[2,2,128,128]{3,2,1,0:T(8,128)S(1)} custom-call(s32[2,8]{1,0:T(2,128)S(1)} %compare_select_fusion.1.index_ref, bf16[2,8,128,256]{3,2,1,0:T(8,128)(2,1)S(1)} %get-tuple-element.11.right_ref, bf16[2,256,1024]{2,1,0:T(8,128)(2,1)S(1)} %get-tuple-element.12.left_ref, f32[2,2,128,128]{3,2,1,0:T(8,128)S(1)} %shift_sum.3.own_ref, ...), custom_call_target="tpu_custom_call" | custom-call | tf_op jit(solution)/shard_map/sandwich/pallas_call | solution.py:124
  44.2 2.8 %collective-permute-done.15.two_ref = f32[2,2,128,128]{3,2,1,0:T(8,128)S(1)} collective-permute-done((f32[2,2,128,128]{3,2,1,0:T(8,128)S(1)}, f32[2,2,128,128]{3,2,1,0:T(8,128)S(1)}, u32[]{:S(2)}, u32[]{:S(2)}) %collective-permute-start.15) | collective-permute-done | bytes 262176 | tf_op jit(solution)/shard_map/ppermute | solution.py:54
  47.0 2.1 %dyson.3 = f32[2,2,2,128,128]{4,3,2,1,0:T(8,128)} custom-call(f32[2,6]{1,0:T(2,128)S(1)} %select_reduce_fusion.weight_ref, f32[2,2,128,128]{3,2,1,0:T(8,128)S(1)} %sandwich.6.sigma_ref, f32[2,2,128,128]{3,2,1,0:T(8,128)S(1)} %sandwich.7.own_ref, f32[2,2,128,128]{3,2,1,0:T(8,128)S(1)} %collective-permute-done.14.one_ref, ...), custom_call_target="tpu_custom_call" | custom-call | tf_op jit(solution)/shard_map/dyson/pallas_call | solution.py:214
  (28 shorter events, 0.5 us)
Async XLA Ops:
  1.1 8.7 %collective-permute-start.1 = (f32[2,2,128,128]{3,2,1,0:T(8,128)S(1)}, f32[2,2,128,128]{3,2,1,0:T(8,128)S(1)}, u32[]{:S(2)}, u32[]{:S(2)}) collective-permute-start(f32[2,2,128,128]{3,2,1,0:T(8,128)S(1)} %get-tuple-element.13.own_ref.real_ref), channel_id=1, source_target_pairs={{0,1},{1,0},{2,3},{3,2},{4,8},{5,9},{6,10},{7,11},{8,4},{9,5},{10,... | collective-permute-start | bytes 786440 | tf_op jit(solution)/shard_map/ppermute | solution.py:54
  2.0 7.7 %collective-permute-start = (f32[2,2,128,128]{3,2,1,0:T(8,128)S(1)}, f32[2,2,128,128]{3,2,1,0:T(8,128)S(1)}, u32[]{:S(2)}, u32[]{:S(2)}) collective-permute-start(f32[2,2,128,128]{3,2,1,0:T(8,128)S(1)} %get-tuple-element.13.own_ref.real_ref), channel_id=1, source_target_pairs={{0,4},{1,5},{2,6},{3,7},{4,0},{5,1},{6,2},{7,3},{8,12},{9,13},{10,... | collective-permute-start | bytes 786440 | tf_op jit(solution)/shard_map/ppermute | solution.py:54
  2.7 9.3 %collective-permute-start.5 = (f32[2,2,128,128]{3,2,1,0:T(8,128)S(1)}, f32[2,2,128,128]{3,2,1,0:T(8,128)S(1)}, u32[]{:S(2)}, u32[]{:S(2)}) collective-permute-start(f32[2,2,128,128]{3,2,1,0:T(8,128)S(1)} %get-tuple-element.14.own_ref.imag_ref), channel_id=1, source_target_pairs={{0,4},{1,2},{2,1},{3,7},{4,0},{5,6},{6,5},{7,3},{8,12},{9,10},{10,... | collective-permute-start | bytes 786440 | tf_op jit(solution)/shard_map/ppermute | solution.py:54
  4.3 7.9 %collective-permute-start.4 = (f32[2,2,128,128]{3,2,1,0:T(8,128)S(1)}, f32[2,2,128,128]{3,2,1,0:T(8,128)S(1)}, u32[]{:S(2)}, u32[]{:S(2)}) collective-permute-start(f32[2,2,128,128]{3,2,1,0:T(8,128)S(1)} %get-tuple-element.14.own_ref.imag_ref), channel_id=1, source_target_pairs={{0,1},{1,0},{2,3},{3,2},{4,5},{5,4},{6,7},{7,6},{8,9},{9,8},{10,11... | collective-permute-start | bytes 786440 | tf_op jit(solution)/shard_map/ppermute | solution.py:54
  4.4 0.7 %copy-start.2 = (f32[4]{0:T(128)S(1)}, f32[4]{0:T(128)}, u32[]{:S(2)}) copy-start(f32[4]{0:T(128)} %param.9) | copy-start | bytes 52
  4.4 0.7 %copy-start.3 = (s32[4]{0:T(128)S(1)}, s32[4]{0:T(128)}, u32[]{:S(2)}) copy-start(s32[4]{0:T(128)} %param.8) | copy-start | bytes 52
  5.2 1.2 %copy-start = (f32[2,8,128,128]{3,2,1,0:T(8,128)S(1)}, f32[2,8,128,128]{3,2,1,0:T(8,128)}, u32[]{:S(2)}) copy-start(f32[2,8,128,128]{3,2,1,0:T(8,128)} %grad_ref.1) | copy-start | bytes 3145732
  6.4 0.7 %copy-start.1 = (s32[2,8]{1,0:T(2,128)S(1)}, s32[2,8]{1,0:T(2,128)}, u32[]{:S(2)}) copy-start(s32[2,8]{1,0:T(2,128)} %param.7) | copy-start | bytes 196
  10.4 7.4 %collective-permute-start.3 = (f32[2,2,128,128]{3,2,1,0:T(8,128)S(1)}, f32[2,2,128,128]{3,2,1,0:T(8,128)S(1)}, u32[]{:S(2)}, u32[]{:S(2)}) collective-permute-start(f32[2,2,128,128]{3,2,1,0:T(8,128)S(1)} %shift_sum.2.own_ref), channel_id=1, source_target_pairs={{0,4},{1,2},{2,1},{3,7},{4,0},{5,6},{6,5},{7,3},{8,12},{9,10},{10,... | collective-permute-start | bytes 786440 | tf_op jit(solution)/shard_map/ppermute | solution.py:54
  12.0 7.1 %collective-permute-start.2 = (f32[2,2,128,128]{3,2,1,0:T(8,128)S(1)}, f32[2,2,128,128]{3,2,1,0:T(8,128)S(1)}, u32[]{:S(2)}, u32[]{:S(2)}) collective-permute-start(f32[2,2,128,128]{3,2,1,0:T(8,128)S(1)} %shift_sum.2.own_ref), channel_id=1, source_target_pairs={{0,1},{1,0},{2,3},{3,2},{4,5},{5,4},{6,7},{7,6},{8,9},{9,8},{10,11... | collective-permute-start | bytes 786440 | tf_op jit(solution)/shard_map/ppermute | solution.py:54
  14.5 9.4 %collective-permute-start.7 = (f32[2,2,128,128]{3,2,1,0:T(8,128)S(1)}, f32[2,2,128,128]{3,2,1,0:T(8,128)S(1)}, u32[]{:S(2)}, u32[]{:S(2)}) collective-permute-start(f32[2,2,128,128]{3,2,1,0:T(8,128)S(1)} %sandwich.5.own_ref), channel_id=1, source_target_pairs={{0,1},{1,0},{2,3},{3,2},{4,8},{5,9},{6,10},{7,11},{8,4},{9,5},{10,... | collective-permute-start | bytes 786440 | tf_op jit(solution)/shard_map/ppermute | solution.py:54
  15.8 8.1 %collective-permute-start.6 = (f32[2,2,128,128]{3,2,1,0:T(8,128)S(1)}, f32[2,2,128,128]{3,2,1,0:T(8,128)S(1)}, u32[]{:S(2)}, u32[]{:S(2)}) collective-permute-start(f32[2,2,128,128]{3,2,1,0:T(8,128)S(1)} %sandwich.5.own_ref), channel_id=1, source_target_pairs={{0,4},{1,5},{2,6},{3,7},{4,0},{5,1},{6,2},{7,3},{8,12},{9,13},{10,... | collective-permute-start | bytes 786440 | tf_op jit(solution)/shard_map/ppermute | solution.py:54
  25.2 8.5 %collective-permute-start.9 = (f32[2,2,128,128]{3,2,1,0:T(8,128)S(1)}, f32[2,2,128,128]{3,2,1,0:T(8,128)S(1)}, u32[]{:S(2)}, u32[]{:S(2)}) collective-permute-start(f32[2,2,128,128]{3,2,1,0:T(8,128)S(1)} %get-tuple-element.15.own_ref), channel_id=1, source_target_pairs={{0,1},{1,0},{2,3},{3,2},{4,8},{5,9},{6,10},{7,11},{8,4},{9,5},{10,... | collective-permute-start | bytes 786440 | tf_op jit(solution)/shard_map/ppermute | solution.py:54
  26.1 7.6 %collective-permute-start.8 = (f32[2,2,128,128]{3,2,1,0:T(8,128)S(1)}, f32[2,2,128,128]{3,2,1,0:T(8,128)S(1)}, u32[]{:S(2)}, u32[]{:S(2)}) collective-permute-start(f32[2,2,128,128]{3,2,1,0:T(8,128)S(1)} %get-tuple-element.15.own_ref), channel_id=1, source_target_pairs={{0,4},{1,5},{2,6},{3,7},{4,0},{5,1},{6,2},{7,3},{8,12},{9,13},{10,... | collective-permute-start | bytes 786440 | tf_op jit(solution)/shard_map/ppermute | solution.py:54
  26.1 9.5 %collective-permute-start.13 = (f32[2,2,128,128]{3,2,1,0:T(8,128)S(1)}, f32[2,2,128,128]{3,2,1,0:T(8,128)S(1)}, u32[]{:S(2)}, u32[]{:S(2)}) collective-permute-start(f32[2,2,128,128]{3,2,1,0:T(8,128)S(1)} %get-tuple-element.16.own_ref), channel_id=1, source_target_pairs={{0,4},{1,2},{2,1},{3,7},{4,0},{5,6},{6,5},{7,3},{8,12},{9,10},{10,... | collective-permute-start | bytes 786440 | tf_op jit(solution)/shard_map/ppermute | solution.py:54
  27.8 8.9 %collective-permute-start.12 = (f32[2,2,128,128]{3,2,1,0:T(8,128)S(1)}, f32[2,2,128,128]{3,2,1,0:T(8,128)S(1)}, u32[]{:S(2)}, u32[]{:S(2)}) collective-permute-start(f32[2,2,128,128]{3,2,1,0:T(8,128)S(1)} %get-tuple-element.16.own_ref), channel_id=1, source_target_pairs={{0,1},{1,0},{2,3},{3,2},{4,5},{5,4},{6,7},{7,6},{8,9},{9,8},{10,11... | collective-permute-start | bytes 786440 | tf_op jit(solution)/shard_map/ppermute | solution.py:54
  34.3 6.4 %collective-permute-start.11 = (f32[2,2,128,128]{3,2,1,0:T(8,128)S(1)}, f32[2,2,128,128]{3,2,1,0:T(8,128)S(1)}, u32[]{:S(2)}, u32[]{:S(2)}) collective-permute-start(f32[2,2,128,128]{3,2,1,0:T(8,128)S(1)} %shift_sum.3.own_ref), channel_id=1, source_target_pairs={{0,4},{1,2},{2,1},{3,7},{4,0},{5,6},{6,5},{7,3},{8,12},{9,10},{10,... | collective-permute-start | bytes 786440 | tf_op jit(solution)/shard_map/ppermute | solution.py:54
  35.6 6.4 %collective-permute-start.10 = (f32[2,2,128,128]{3,2,1,0:T(8,128)S(1)}, f32[2,2,128,128]{3,2,1,0:T(8,128)S(1)}, u32[]{:S(2)}, u32[]{:S(2)}) collective-permute-start(f32[2,2,128,128]{3,2,1,0:T(8,128)S(1)} %shift_sum.3.own_ref), channel_id=1, source_target_pairs={{0,1},{1,0},{2,3},{3,2},{4,5},{5,4},{6,7},{7,6},{8,9},{9,8},{10,11... | collective-permute-start | bytes 786440 | tf_op jit(solution)/shard_map/ppermute | solution.py:54
  38.9 8.1 %collective-permute-start.15 = (f32[2,2,128,128]{3,2,1,0:T(8,128)S(1)}, f32[2,2,128,128]{3,2,1,0:T(8,128)S(1)}, u32[]{:S(2)}, u32[]{:S(2)}) collective-permute-start(f32[2,2,128,128]{3,2,1,0:T(8,128)S(1)} %sandwich.7.own_ref), channel_id=1, source_target_pairs={{0,1},{1,0},{2,3},{3,2},{4,8},{5,9},{6,10},{7,11},{8,4},{9,5},{10,... | collective-permute-start | bytes 786440 | tf_op jit(solution)/shard_map/ppermute | solution.py:54
  39.3 7.8 %collective-permute-start.14 = (f32[2,2,128,128]{3,2,1,0:T(8,128)S(1)}, f32[2,2,128,128]{3,2,1,0:T(8,128)S(1)}, u32[]{:S(2)}, u32[]{:S(2)}) collective-permute-start(f32[2,2,128,128]{3,2,1,0:T(8,128)S(1)} %sandwich.7.own_ref), channel_id=1, source_target_pairs={{0,4},{1,5},{2,6},{3,7},{4,0},{5,1},{6,2},{7,3},{8,12},{9,13},{10,... | collective-permute-start | bytes 786440 | tf_op jit(solution)/shard_map/ppermute | solution.py:54

commit v5 on v4

--- a/solution.py
+++ b/solution.py
@@ -91,28 +91,30 @@
     )(grad_h)
 
 
-def sandwich_kernel(index_ref, right_ref, left_ref, own_ref, one_ref, two_ref, out_ref, green_ref, high_ref, low_ref):
+def sandwich_kernel(index_ref, right_ref, left_ref, own_ref, one_ref, two_ref, out_ref, green_ref, rest_ref, high_ref, low_ref):
     energies, atoms, orb, _ = out_ref.shape
     entries = right_ref.shape[1]
+    places = index_ref[...]
     at = 0
     for ref in (own_ref, one_ref, two_ref):
         for a in range(ref.shape[1]):
             for e in range(energies):
                 high, low = split(ref[e, a])
-                green_ref[at, e * orb : (e + 1) * orb, :orb] = high
-                green_ref[at, e * orb : (e + 1) * orb, orb:] = low
+                green_ref[at, e * orb : (e + 1) * orb] = high
+                rest_ref[at, e * orb : (e + 1) * orb] = low
             at += 1
     for a in range(atoms):
         for k in range(entries):
             weight = right_ref[a, k]
-            both = dot(green_ref[index_ref[a, k]], jnp.concatenate([weight, weight], axis=0))
+            n = places[a, k]
+            both = dot(jnp.concatenate([green_ref[n], rest_ref[n]], axis=1), jnp.concatenate([weight, weight], axis=0))
             high, low = split(both[:, :orb] + both[:, orb:])
             for e in range(energies):
-                here = (slice(k * orb, (k + 1) * orb), slice(e * orb, (e + 1) * orb))
-                high_ref[here] = high[e * orb : (e + 1) * orb]
-                low_ref[here] = low[e * orb : (e + 1) * orb]
-        main = dot(left_ref[a], high_ref[...])
-        total = main[:orb] + (main[orb:] + dot(left_ref[a, :orb], low_ref[...]))
+                high_ref[a, e, k * orb : (k + 1) * orb] = high[e * orb : (e + 1) * orb]
+                low_ref[a, e, k * orb : (k + 1) * orb] = low[e * orb : (e + 1) * orb]
+    for a in range(atoms):
+        main = dot(left_ref[a], jnp.concatenate([high_ref[a, e] for e in range(energies)], axis=1))
+        total = main[:orb] + (main[orb:] + dot(left_ref[a, :orb], jnp.concatenate([low_ref[a, e] for e in range(energies)], axis=1)))
         for e in range(energies):
             out_ref[e, a] = total[:, e * orb : (e + 1) * orb]
 
@@ -124,16 +126,17 @@
     return pl.pallas_call(
         sandwich_kernel,
         out_shape=at_hand(own.shape),
-        in_specs=[SMEM] + [VMEM] * 5,
+        in_specs=[VMEM] * 6,
         out_specs=VMEM,
         scratch_shapes=[
-            pltpu.VMEM((sources, energies * orb, 2 * orb), jnp.bfloat16),
-            pltpu.VMEM((entries * orb, energies * orb), jnp.bfloat16),
-            pltpu.VMEM((entries * orb, energies * orb), jnp.bfloat16),
+            pltpu.VMEM((sources, energies * orb, orb), jnp.bfloat16),
+            pltpu.VMEM((sources, energies * orb, orb), jnp.bfloat16),
+            pltpu.VMEM((atoms, energies, entries * orb, orb), jnp.bfloat16),
+            pltpu.VMEM((atoms, energies, entries * orb, orb), jnp.bfloat16),
         ],
         compiler_params=PARAMS,
         name="sandwich",
-    )(index, *near(right, left, own, one, two))
+    )(*near(index, right, left, own, one, two))
 
 
 def parts_kernel(green_ref, real_ref, imag_ref, sems):
@@ -159,9 +162,9 @@
 
 def shifted(weight_ref, refs, e, a):
     sources = [(ref, s) for ref in refs for s in range(ref.shape[0])]
-    total = weight_ref[e, 0] * sources[0][0][sources[0][1], a]
+    total = weight_ref[e : e + 1, :1] * sources[0][0][sources[0][1], a]
     for at, (ref, s) in enumerate(sources[1:]):
-        total = total + weight_ref[e, at + 1] * ref[s, a]
+        total = total + weight_ref[e : e + 1, at + 1 : at + 2] * ref[s, a]
     return total
 
 
@@ -175,11 +178,11 @@
     return pl.pallas_call(
         shift_sum_kernel,
         out_shape=at_hand(own.shape),
-        in_specs=[SMEM] + [VMEM] * 3,
+        in_specs=[VMEM] * 4,
         out_specs=VMEM,
         compiler_params=PARAMS,
         name="shift_sum",
-    )(weights, *near(own, one, two))
+    )(*near(weights, own, one, two))
 
 
 def complex_product(left, right):
@@ -214,11 +217,11 @@
     return pl.pallas_call(
         dyson_kernel,
         out_shape=out_shape,
-        in_specs=[SMEM] + [VMEM] * 6,
+        in_specs=[VMEM] * 7,
         out_specs=VMEM if whole else (VMEM, VMEM),
         compiler_params=PARAMS,
         name="dyson",
-    )(weights, *near(sigma, own, one, two, *base))
+    )(*near(weights, sigma, own, one, two, *base))
 
 
 def source_index(neighbours, atoms):

time: 49.4 us -> 46.4 us (0.939)
  Pallas kernels: 15.3 us -> 9.73 us
  waiting for transfers between devices: 20.1 us -> 23.4 us
  starting transfers between devices: 11.4 us -> 10.5 us
    pallas_call x6, Pallas kernels: 12.3 us -> 7.7 us  [the longest x4 5.09 us: sandwich(): pl.pallas_call(sandwich_kernel, out_shape=at_hand(own.shape), in_specs=[V...]
    ppermute x16, waiting for transfers between devices: 20.1 us -> 23.4 us  [trade(): got.append(lax.ppermute(edge, AXES, swaps(axis, parity)))]
    ppermute x16, starting transfers between devices: 11.4 us -> 10.5 us  [trade(): got.append(lax.ppermute(edge, AXES, swaps(axis, parity)))]
    pallas_call x2, Pallas kernels: 1.3 us -> 0.4 us  [shift_sum(): pl.pallas_call(shift_sum_kernel, out_shape=at_hand(own.shape), in_specs=[...]
  transfers between devices with their start and end apart: 16 -> 16, of which waited for: 10 -> 11; matrix products, arithmetic and copies ran while one was open for 1% -> 1% of each run, Pallas kernels for 22% -> 13%
where the time goes in v5:
time: 46.4 us; the launch traced here: 46 us
  waiting for transfers between devices  23.4 us (50%)
  starting transfers between devices  10.5 us (23%)
  Pallas kernels  9.73 us (21%)
  local copies, waits for them, and re-layouts  1.91 us (4%)
    ppermute x16, waiting for transfers between devices, trade(): got.append(lax.ppermute(edge, AXES, swaps(axis, parity)))  23.4 us
    ppermute x16, starting transfers between devices, trade(): got.append(lax.ppermute(edge, AXES, swaps(axis, parity)))  10.5 us
    pallas_call x4, Pallas kernels, sandwich(): pl.pallas_call(sandwich_kernel, out_shape=at_hand(own.shape), in_specs=[V...  5.09 us
    pallas_call x2, Pallas kernels, dyson(): pl.pallas_call(dyson_kernel, out_shape=out_shape, in_specs=[VMEM] * 7, ou...  2.61 us
    unnamed x8, local copies, waits for them, and re-layouts  1.89 us
    pallas_call x1, Pallas kernels, parts(): pl.pallas_call(parts_kernel, out_shape=(at_hand(shape), at_hand(shape)),...  1.04 us
  transfers between devices with their start and end apart: 16, of which 11 were waited for; matrix products, arithmetic and copies ran while one was open for 1% of the time, Pallas kernels for 13%

profile of v5, /device:TPU:12, one launch (start us, length us, event | category | flops | bytes accessed | tf_op | source)
XLA Modules:
  0.0 46.0 jit_solution(2228366031161891686)
XLA Ops:
  0.0 1.0 %parts.1 = (f32[2,2,128,128]{3,2,1,0:T(8,128)S(1)}, f32[2,2,128,128]{3,2,1,0:T(8,128)S(1)}) custom-call(f32[2,2,2,128,128]{4,3,2,1,0:T(8,128)} %green_ref.1), custom_call_target="tpu_custom_call" | custom-call | tf_op jit(solution)/shard_map/parts/pallas_call | solution.py:152
  1.1 0.9 %collective-permute-start.1 = (f32[2,2,128,128]{3,2,1,0:T(8,128)S(1)}, f32[2,2,128,128]{3,2,1,0:T(8,128)S(1)}, u32[]{:S(2)}, u32[]{:S(2)}) collective-permute-start(f32[2,2,128,128]{3,2,1,0:T(8,128)S(1)} %get-tuple-element.13.own_ref.real_ref), channel_id=1, source_target_pairs={{0,1},{1,0},{2,3},{3,2},{4,8},{5,9},{6,10},{7,11},{8,4},{9,5},{10,... | collective-permute-start | bytes 786440 | tf_op jit(solution)/shard_map/ppermute | solution.py:54
  2.0 0.7 %collective-permute-start = (f32[2,2,128,128]{3,2,1,0:T(8,128)S(1)}, f32[2,2,128,128]{3,2,1,0:T(8,128)S(1)}, u32[]{:S(2)}, u32[]{:S(2)}) collective-permute-start(f32[2,2,128,128]{3,2,1,0:T(8,128)S(1)} %get-tuple-element.13.own_ref.real_ref), channel_id=1, source_target_pairs={{0,4},{1,5},{2,6},{3,7},{4,0},{5,1},{6,2},{7,3},{8,12},{9,13},{10,... | collective-permute-start | bytes 786440 | tf_op jit(solution)/shard_map/ppermute | solution.py:54
  2.7 1.6 %collective-permute-start.5 = (f32[2,2,128,128]{3,2,1,0:T(8,128)S(1)}, f32[2,2,128,128]{3,2,1,0:T(8,128)S(1)}, u32[]{:S(2)}, u32[]{:S(2)}) collective-permute-start(f32[2,2,128,128]{3,2,1,0:T(8,128)S(1)} %get-tuple-element.14.own_ref.imag_ref), channel_id=1, source_target_pairs={{0,4},{1,2},{2,1},{3,7},{4,0},{5,6},{6,5},{7,3},{8,12},{9,10},{10,... | collective-permute-start | bytes 786440 | tf_op jit(solution)/shard_map/ppermute | solution.py:54
  4.5 0.6 %copy-done.2 = f32[4]{0:T(128)S(1)} copy-done((f32[4]{0:T(128)S(1)}, f32[4]{0:T(128)}, u32[]{:S(2)}) %copy-start.2) | copy-done | bytes 40
  5.2 1.2 %copy-done = f32[2,8,128,128]{3,2,1,0:T(8,128)S(1)} copy-done((f32[2,8,128,128]{3,2,1,0:T(8,128)S(1)}, f32[2,8,128,128]{3,2,1,0:T(8,128)}, u32[]{:S(2)}) %copy-start) | copy-done | bytes 1048600
  6.4 0.6 %prepare.1 = (bf16[2,8,128,256]{3,2,1,0:T(8,128)(2,1)S(1)}, bf16[2,256,1024]{2,1,0:T(8,128)(2,1)S(1)}) custom-call(f32[2,8,128,128]{3,2,1,0:T(8,128)S(1)} %copy-done), custom_call_target="tpu_custom_call" | custom-call | tf_op jit(solution)/shard_map/prepare/pallas_call | solution.py:81
  7.1 2.6 %collective-permute-done.1.two_ref = f32[2,2,128,128]{3,2,1,0:T(8,128)S(1)} collective-permute-done((f32[2,2,128,128]{3,2,1,0:T(8,128)S(1)}, f32[2,2,128,128]{3,2,1,0:T(8,128)S(1)}, u32[]{:S(2)}, u32[]{:S(2)}) %collective-permute-start.1) | collective-permute-done | bytes 262176 | tf_op jit(solution)/shard_map/ppermute | solution.py:54
  9.7 0.2 shift_sum.2.own_ref
  9.9 1.6 %collective-permute-start.3 = (f32[2,2,128,128]{3,2,1,0:T(8,128)S(1)}, f32[2,2,128,128]{3,2,1,0:T(8,128)S(1)}, u32[]{:S(2)}, u32[]{:S(2)}) collective-permute-start(f32[2,2,128,128]{3,2,1,0:T(8,128)S(1)} %shift_sum.2.own_ref), channel_id=1, source_target_pairs={{0,4},{1,2},{2,1},{3,7},{4,0},{5,6},{6,5},{7,3},{8,12},{9,10},{10,... | collective-permute-start | bytes 786440 | tf_op jit(solution)/shard_map/ppermute | solution.py:54
  11.6 0.7 %collective-permute-done.4.one_ref = f32[2,2,128,128]{3,2,1,0:T(8,128)S(1)} collective-permute-done((f32[2,2,128,128]{3,2,1,0:T(8,128)S(1)}, f32[2,2,128,128]{3,2,1,0:T(8,128)S(1)}, u32[]{:S(2)}, u32[]{:S(2)}) %collective-permute-start.4) | collective-permute-done | bytes 262176 | tf_op jit(solution)/shard_map/ppermute | solution.py:54
  12.2 1.3 %sandwich.5.own_ref = f32[2,2,128,128]{3,2,1,0:T(8,128)S(1)} custom-call(s32[2,8]{1,0:T(2,128)S(1)} %compare_select_fusion.1.index_ref, bf16[2,8,128,256]{3,2,1,0:T(8,128)(2,1)S(1)} %get-tuple-element.11.right_ref, bf16[2,256,1024]{2,1,0:T(8,128)(2,1)S(1)} %get-tuple-element.12.left_ref, f32[2,2,128,128]{3,2,1,0:T(8,128)S(1)} %get-tuple-element.14.own_ref.imag_ref, ...), custom_call_target="tpu_custom_call" | custom-call | tf_op jit(solution)/shard_map/sandwich/pallas_call | solution.py:126
  13.5 0.9 %collective-permute-start.7 = (f32[2,2,128,128]{3,2,1,0:T(8,128)S(1)}, f32[2,2,128,128]{3,2,1,0:T(8,128)S(1)}, u32[]{:S(2)}, u32[]{:S(2)}) collective-permute-start(f32[2,2,128,128]{3,2,1,0:T(8,128)S(1)} %sandwich.5.own_ref), channel_id=1, source_target_pairs={{0,1},{1,0},{2,3},{3,2},{4,8},{5,9},{6,10},{7,11},{8,4},{9,5},{10,... | collective-permute-start | bytes 786440 | tf_op jit(solution)/shard_map/ppermute | solution.py:54
  14.4 0.7 %collective-permute-start.6 = (f32[2,2,128,128]{3,2,1,0:T(8,128)S(1)}, f32[2,2,128,128]{3,2,1,0:T(8,128)S(1)}, u32[]{:S(2)}, u32[]{:S(2)}) collective-permute-start(f32[2,2,128,128]{3,2,1,0:T(8,128)S(1)} %sandwich.5.own_ref), channel_id=1, source_target_pairs={{0,4},{1,5},{2,6},{3,7},{4,0},{5,1},{6,2},{7,3},{8,12},{9,13},{10,... | collective-permute-start | bytes 786440 | tf_op jit(solution)/shard_map/ppermute | solution.py:54
  15.1 2.2 %collective-permute-done.3.two_ref = f32[2,2,128,128]{3,2,1,0:T(8,128)S(1)} collective-permute-done((f32[2,2,128,128]{3,2,1,0:T(8,128)S(1)}, f32[2,2,128,128]{3,2,1,0:T(8,128)S(1)}, u32[]{:S(2)}, u32[]{:S(2)}) %collective-permute-start.3) | collective-permute-done | bytes 262176 | tf_op jit(solution)/shard_map/ppermute | solution.py:54
  17.3 1.3 %collective-permute-done.2.one_ref = f32[2,2,128,128]{3,2,1,0:T(8,128)S(1)} collective-permute-done((f32[2,2,128,128]{3,2,1,0:T(8,128)S(1)}, f32[2,2,128,128]{3,2,1,0:T(8,128)S(1)}, u32[]{:S(2)}, u32[]{:S(2)}) %collective-permute-start.2) | collective-permute-done | bytes 262176 | tf_op jit(solution)/shard_map/ppermute | solution.py:54
  18.6 1.3 %sandwich.4.sigma_ref = f32[2,2,128,128]{3,2,1,0:T(8,128)S(1)} custom-call(s32[2,8]{1,0:T(2,128)S(1)} %compare_select_fusion.1.index_ref, bf16[2,8,128,256]{3,2,1,0:T(8,128)(2,1)S(1)} %get-tuple-element.11.right_ref, bf16[2,256,1024]{2,1,0:T(8,128)(2,1)S(1)} %get-tuple-element.12.left_ref, f32[2,2,128,128]{3,2,1,0:T(8,128)S(1)} %shift_sum.2.own_ref, ...), custom_call_target="tpu_custom_call" | custom-call | tf_op jit(solution)/shard_map/sandwich/pallas_call | solution.py:126
  19.9 3.0 %collective-permute-done.7.two_ref = f32[2,2,128,128]{3,2,1,0:T(8,128)S(1)} collective-permute-done((f32[2,2,128,128]{3,2,1,0:T(8,128)S(1)}, f32[2,2,128,128]{3,2,1,0:T(8,128)S(1)}, u32[]{:S(2)}, u32[]{:S(2)}) %collective-permute-start.7) | collective-permute-done | bytes 262176 | tf_op jit(solution)/shard_map/ppermute | solution.py:54
  22.9 0.9 %dyson.2 = (f32[2,2,128,128]{3,2,1,0:T(8,128)S(1)}, f32[2,2,128,128]{3,2,1,0:T(8,128)S(1)}) custom-call(f32[2,6]{1,0:T(2,128)S(1)} %select_reduce_fusion.weight_ref, f32[2,2,128,128]{3,2,1,0:T(8,128)S(1)} %sandwich.4.sigma_ref, f32[2,2,128,128]{3,2,1,0:T(8,128)S(1)} %sandwich.5.own_ref, f32[2,2,128,128]{3,2,1,0:T(8,128)S(1)} %collective-permute-done.6.one_ref, ...), custom_call_target="tpu_custom_call" | custom-call | tf_op jit(solution)/shard_map/dyson/pallas_call | solution.py:217
  23.8 1.0 %collective-permute-start.9 = (f32[2,2,128,128]{3,2,1,0:T(8,128)S(1)}, f32[2,2,128,128]{3,2,1,0:T(8,128)S(1)}, u32[]{:S(2)}, u32[]{:S(2)}) collective-permute-start(f32[2,2,128,128]{3,2,1,0:T(8,128)S(1)} %get-tuple-element.15.own_ref), channel_id=1, source_target_pairs={{0,1},{1,0},{2,3},{3,2},{4,8},{5,9},{6,10},{7,11},{8,4},{9,5},{10,... | collective-permute-start | bytes 786440 | tf_op jit(solution)/shard_map/ppermute | solution.py:54
  24.8 1.1 %collective-permute-start.13 = (f32[2,2,128,128]{3,2,1,0:T(8,128)S(1)}, f32[2,2,128,128]{3,2,1,0:T(8,128)S(1)}, u32[]{:S(2)}, u32[]{:S(2)}) collective-permute-start(f32[2,2,128,128]{3,2,1,0:T(8,128)S(1)} %get-tuple-element.16.own_ref), channel_id=1, source_target_pairs={{0,4},{1,2},{2,1},{3,7},{4,0},{5,6},{6,5},{7,3},{8,12},{9,10},{10,... | collective-permute-start | bytes 786440 | tf_op jit(solution)/shard_map/ppermute | solution.py:54
  26.0 0.9 %collective-permute-start.12 = (f32[2,2,128,128]{3,2,1,0:T(8,128)S(1)}, f32[2,2,128,128]{3,2,1,0:T(8,128)S(1)}, u32[]{:S(2)}, u32[]{:S(2)}) collective-permute-start(f32[2,2,128,128]{3,2,1,0:T(8,128)S(1)} %get-tuple-element.16.own_ref), channel_id=1, source_target_pairs={{0,1},{1,0},{2,3},{3,2},{4,5},{5,4},{6,7},{7,6},{8,9},{9,8},{10,11... | collective-permute-start | bytes 786440 | tf_op jit(solution)/shard_map/ppermute | solution.py:54
  26.8 5.5 %collective-permute-done.9.two_ref = f32[2,2,128,128]{3,2,1,0:T(8,128)S(1)} collective-permute-done((f32[2,2,128,128]{3,2,1,0:T(8,128)S(1)}, f32[2,2,128,128]{3,2,1,0:T(8,128)S(1)}, u32[]{:S(2)}, u32[]{:S(2)}) %collective-permute-start.9) | collective-permute-done | bytes 262176 | tf_op jit(solution)/shard_map/ppermute | solution.py:54
  32.5 0.9 %collective-permute-start.11 = (f32[2,2,128,128]{3,2,1,0:T(8,128)S(1)}, f32[2,2,128,128]{3,2,1,0:T(8,128)S(1)}, u32[]{:S(2)}, u32[]{:S(2)}) collective-permute-start(f32[2,2,128,128]{3,2,1,0:T(8,128)S(1)} %shift_sum.3.own_ref), channel_id=1, source_target_pairs={{0,4},{1,2},{2,1},{3,7},{4,0},{5,6},{6,5},{7,3},{8,12},{9,10},{10,... | collective-permute-start | bytes 786440 | tf_op jit(solution)/shard_map/ppermute | solution.py:54
  33.4 0.6 %collective-permute-done.13.two_ref = f32[2,2,128,128]{3,2,1,0:T(8,128)S(1)} collective-permute-done((f32[2,2,128,128]{3,2,1,0:T(8,128)S(1)}, f32[2,2,128,128]{3,2,1,0:T(8,128)S(1)}, u32[]{:S(2)}, u32[]{:S(2)}) %collective-permute-start.13) | collective-permute-done | bytes 262176 | tf_op jit(solution)/shard_map/ppermute | solution.py:54
  34.0 1.1 %collective-permute-done.12.one_ref = f32[2,2,128,128]{3,2,1,0:T(8,128)S(1)} collective-permute-done((f32[2,2,128,128]{3,2,1,0:T(8,128)S(1)}, f32[2,2,128,128]{3,2,1,0:T(8,128)S(1)}, u32[]{:S(2)}, u32[]{:S(2)}) %collective-permute-start.12) | collective-permute-done | bytes 262176 | tf_op jit(solution)/shard_map/ppermute | solution.py:54
  35.1 1.3 %sandwich.7.own_ref = f32[2,2,128,128]{3,2,1,0:T(8,128)S(1)} custom-call(s32[2,8]{1,0:T(2,128)S(1)} %compare_select_fusion.1.index_ref, bf16[2,8,128,256]{3,2,1,0:T(8,128)(2,1)S(1)} %get-tuple-element.11.right_ref, bf16[2,256,1024]{2,1,0:T(8,128)(2,1)S(1)} %get-tuple-element.12.left_ref, f32[2,2,128,128]{3,2,1,0:T(8,128)S(1)} %get-tuple-element.16.own_ref, ...), custom_call_target="tpu_custom_call" | custom-call | tf_op jit(solution)/shard_map/sandwich/pallas_call | solution.py:126
  36.6 2.6 %collective-permute-done.11.two_ref = f32[2,2,128,128]{3,2,1,0:T(8,128)S(1)} collective-permute-done((f32[2,2,128,128]{3,2,1,0:T(8,128)S(1)}, f32[2,2,128,128]{3,2,1,0:T(8,128)S(1)}, u32[]{:S(2)}, u32[]{:S(2)}) %collective-permute-start.11) | collective-permute-done | bytes 262176 | tf_op jit(solution)/shard_map/ppermute | solution.py:54
  39.2 0.8 %collective-permute-done.10.one_ref = f32[2,2,128,128]{3,2,1,0:T(8,128)S(1)} collective-permute-done((f32[2,2,128,128]{3,2,1,0:T(8,128)S(1)}, f32[2,2,128,128]{3,2,1,0:T(8,128)S(1)}, u32[]{:S(2)}, u32[]{:S(2)}) %collective-permute-start.10) | collective-permute-done | bytes 262176 | tf_op jit(solution)/shard_map/ppermute | solution.py:54
  40.0 1.3 %sandwich.6.sigma_ref = f32[2,2,128,128]{3,2,1,0:T(8,128)S(1)} custom-call(s32[2,8]{1,0:T(2,128)S(1)} %compare_select_fusion.1.index_ref, bf16[2,8,128,256]{3,2,1,0:T(8,128)(2,1)S(1)} %get-tuple-element.11.right_ref, bf16[2,256,1024]{2,1,0:T(8,128)(2,1)S(1)} %get-tuple-element.12.left_ref, f32[2,2,128,128]{3,2,1,0:T(8,128)S(1)} %shift_sum.3.own_ref, ...), custom_call_target="tpu_custom_call" | custom-call | tf_op jit(solution)/shard_map/sandwich/pallas_call | solution.py:126
  41.3 3.0 %collective-permute-done.15.two_ref = f32[2,2,128,128]{3,2,1,0:T(8,128)S(1)} collective-permute-done((f32[2,2,128,128]{3,2,1,0:T(8,128)S(1)}, f32[2,2,128,128]{3,2,1,0:T(8,128)S(1)}, u32[]{:S(2)}, u32[]{:S(2)}) %collective-permute-start.15) | collective-permute-done | bytes 262176 | tf_op jit(solution)/shard_map/ppermute | solution.py:54
  44.3 1.7 %dyson.3 = f32[2,2,2,128,128]{4,3,2,1,0:T(8,128)} custom-call(f32[2,6]{1,0:T(2,128)S(1)} %select_reduce_fusion.weight_ref, f32[2,2,128,128]{3,2,1,0:T(8,128)S(1)} %sandwich.6.sigma_ref, f32[2,2,128,128]{3,2,1,0:T(8,128)S(1)} %sandwich.7.own_ref, f32[2,2,128,128]{3,2,1,0:T(8,128)S(1)} %collective-permute-done.14.one_ref, ...), custom_call_target="tpu_custom_call" | custom-call | tf_op jit(solution)/shard_map/dyson/pallas_call | solution.py:217
  (28 shorter events, 0.8 us)
Async XLA Ops:
  1.1 8.7 %collective-permute-start.1 = (f32[2,2,128,128]{3,2,1,0:T(8,128)S(1)}, f32[2,2,128,128]{3,2,1,0:T(8,128)S(1)}, u32[]{:S(2)}, u32[]{:S(2)}) collective-permute-start(f32[2,2,128,128]{3,2,1,0:T(8,128)S(1)} %get-tuple-element.13.own_ref.real_ref), channel_id=1, source_target_pairs={{0,1},{1,0},{2,3},{3,2},{4,8},{5,9},{6,10},{7,11},{8,4},{9,5},{10,... | collective-permute-start | bytes 786440 | tf_op jit(solution)/shard_map/ppermute | solution.py:54
  2.0 7.7 %collective-permute-start = (f32[2,2,128,128]{3,2,1,0:T(8,128)S(1)}, f32[2,2,128,128]{3,2,1,0:T(8,128)S(1)}, u32[]{:S(2)}, u32[]{:S(2)}) collective-permute-start(f32[2,2,128,128]{3,2,1,0:T(8,128)S(1)} %get-tuple-element.13.own_ref.real_ref), channel_id=1, source_target_pairs={{0,4},{1,5},{2,6},{3,7},{4,0},{5,1},{6,2},{7,3},{8,12},{9,13},{10,... | collective-permute-start | bytes 786440 | tf_op jit(solution)/shard_map/ppermute | solution.py:54
  2.7 8.8 %collective-permute-start.5 = (f32[2,2,128,128]{3,2,1,0:T(8,128)S(1)}, f32[2,2,128,128]{3,2,1,0:T(8,128)S(1)}, u32[]{:S(2)}, u32[]{:S(2)}) collective-permute-start(f32[2,2,128,128]{3,2,1,0:T(8,128)S(1)} %get-tuple-element.14.own_ref.imag_ref), channel_id=1, source_target_pairs={{0,4},{1,2},{2,1},{3,7},{4,0},{5,6},{6,5},{7,3},{8,12},{9,10},{10,... | collective-permute-start | bytes 786440 | tf_op jit(solution)/shard_map/ppermute | solution.py:54
  4.3 7.9 %collective-permute-start.4 = (f32[2,2,128,128]{3,2,1,0:T(8,128)S(1)}, f32[2,2,128,128]{3,2,1,0:T(8,128)S(1)}, u32[]{:S(2)}, u32[]{:S(2)}) collective-permute-start(f32[2,2,128,128]{3,2,1,0:T(8,128)S(1)} %get-tuple-element.14.own_ref.imag_ref), channel_id=1, source_target_pairs={{0,1},{1,0},{2,3},{3,2},{4,5},{5,4},{6,7},{7,6},{8,9},{9,8},{10,11... | collective-permute-start | bytes 786440 | tf_op jit(solution)/shard_map/ppermute | solution.py:54
  4.4 0.7 %copy-start.2 = (f32[4]{0:T(128)S(1)}, f32[4]{0:T(128)}, u32[]{:S(2)}) copy-start(f32[4]{0:T(128)} %param.9) | copy-start | bytes 52
  4.4 0.7 %copy-start.3 = (s32[4]{0:T(128)S(1)}, s32[4]{0:T(128)}, u32[]{:S(2)}) copy-start(s32[4]{0:T(128)} %param.8) | copy-start | bytes 52
  5.2 1.2 %copy-start = (f32[2,8,128,128]{3,2,1,0:T(8,128)S(1)}, f32[2,8,128,128]{3,2,1,0:T(8,128)}, u32[]{:S(2)}) copy-start(f32[2,8,128,128]{3,2,1,0:T(8,128)} %grad_ref.1) | copy-start | bytes 3145732
  6.4 0.7 %copy-start.1 = (s32[2,8]{1,0:T(2,128)S(1)}, s32[2,8]{1,0:T(2,128)}, u32[]{:S(2)}) copy-start(s32[2,8]{1,0:T(2,128)} %param.7) | copy-start | bytes 196
  9.9 7.4 %collective-permute-start.3 = (f32[2,2,128,128]{3,2,1,0:T(8,128)S(1)}, f32[2,2,128,128]{3,2,1,0:T(8,128)S(1)}, u32[]{:S(2)}, u32[]{:S(2)}) collective-permute-start(f32[2,2,128,128]{3,2,1,0:T(8,128)S(1)} %shift_sum.2.own_ref), channel_id=1, source_target_pairs={{0,4},{1,2},{2,1},{3,7},{4,0},{5,6},{6,5},{7,3},{8,12},{9,10},{10,... | collective-permute-start | bytes 786440 | tf_op jit(solution)/shard_map/ppermute | solution.py:54
  11.6 7.1 %collective-permute-start.2 = (f32[2,2,128,128]{3,2,1,0:T(8,128)S(1)}, f32[2,2,128,128]{3,2,1,0:T(8,128)S(1)}, u32[]{:S(2)}, u32[]{:S(2)}) collective-permute-start(f32[2,2,128,128]{3,2,1,0:T(8,128)S(1)} %shift_sum.2.own_ref), channel_id=1, source_target_pairs={{0,1},{1,0},{2,3},{3,2},{4,5},{5,4},{6,7},{7,6},{8,9},{9,8},{10,11... | collective-permute-start | bytes 786440 | tf_op jit(solution)/shard_map/ppermute | solution.py:54
  13.5 9.4 %collective-permute-start.7 = (f32[2,2,128,128]{3,2,1,0:T(8,128)S(1)}, f32[2,2,128,128]{3,2,1,0:T(8,128)S(1)}, u32[]{:S(2)}, u32[]{:S(2)}) collective-permute-start(f32[2,2,128,128]{3,2,1,0:T(8,128)S(1)} %sandwich.5.own_ref), channel_id=1, source_target_pairs={{0,1},{1,0},{2,3},{3,2},{4,8},{5,9},{6,10},{7,11},{8,4},{9,5},{10,... | collective-permute-start | bytes 786440 | tf_op jit(solution)/shard_map/ppermute | solution.py:54
  14.4 8.5 %collective-permute-start.6 = (f32[2,2,128,128]{3,2,1,0:T(8,128)S(1)}, f32[2,2,128,128]{3,2,1,0:T(8,128)S(1)}, u32[]{:S(2)}, u32[]{:S(2)}) collective-permute-start(f32[2,2,128,128]{3,2,1,0:T(8,128)S(1)} %sandwich.5.own_ref), channel_id=1, source_target_pairs={{0,4},{1,5},{2,6},{3,7},{4,0},{5,1},{6,2},{7,3},{8,12},{9,13},{10,... | collective-permute-start | bytes 786440 | tf_op jit(solution)/shard_map/ppermute | solution.py:54
  23.8 8.5 %collective-permute-start.9 = (f32[2,2,128,128]{3,2,1,0:T(8,128)S(1)}, f32[2,2,128,128]{3,2,1,0:T(8,128)S(1)}, u32[]{:S(2)}, u32[]{:S(2)}) collective-permute-start(f32[2,2,128,128]{3,2,1,0:T(8,128)S(1)} %get-tuple-element.15.own_ref), channel_id=1, source_target_pairs={{0,1},{1,0},{2,3},{3,2},{4,8},{5,9},{6,10},{7,11},{8,4},{9,5},{10,... | collective-permute-start | bytes 786440 | tf_op jit(solution)/shard_map/ppermute | solution.py:54
  24.8 7.5 %collective-permute-start.8 = (f32[2,2,128,128]{3,2,1,0:T(8,128)S(1)}, f32[2,2,128,128]{3,2,1,0:T(8,128)S(1)}, u32[]{:S(2)}, u32[]{:S(2)}) collective-permute-start(f32[2,2,128,128]{3,2,1,0:T(8,128)S(1)} %get-tuple-element.15.own_ref), channel_id=1, source_target_pairs={{0,4},{1,5},{2,6},{3,7},{4,0},{5,1},{6,2},{7,3},{8,12},{9,13},{10,... | collective-permute-start | bytes 786440 | tf_op jit(solution)/shard_map/ppermute | solution.py:54
  24.8 9.2 %collective-permute-start.13 = (f32[2,2,128,128]{3,2,1,0:T(8,128)S(1)}, f32[2,2,128,128]{3,2,1,0:T(8,128)S(1)}, u32[]{:S(2)}, u32[]{:S(2)}) collective-permute-start(f32[2,2,128,128]{3,2,1,0:T(8,128)S(1)} %get-tuple-element.16.own_ref), channel_id=1, source_target_pairs={{0,4},{1,2},{2,1},{3,7},{4,0},{5,6},{6,5},{7,3},{8,12},{9,10},{10,... | collective-permute-start | bytes 786440 | tf_op jit(solution)/shard_map/ppermute | solution.py:54
  26.0 9.2 %collective-permute-start.12 = (f32[2,2,128,128]{3,2,1,0:T(8,128)S(1)}, f32[2,2,128,128]{3,2,1,0:T(8,128)S(1)}, u32[]{:S(2)}, u32[]{:S(2)}) collective-permute-start(f32[2,2,128,128]{3,2,1,0:T(8,128)S(1)} %get-tuple-element.16.own_ref), channel_id=1, source_target_pairs={{0,1},{1,0},{2,3},{3,2},{4,5},{5,4},{6,7},{7,6},{8,9},{9,8},{10,11... | collective-permute-start | bytes 786440 | tf_op jit(solution)/shard_map/ppermute | solution.py:54
  32.5 6.6 %collective-permute-start.11 = (f32[2,2,128,128]{3,2,1,0:T(8,128)S(1)}, f32[2,2,128,128]{3,2,1,0:T(8,128)S(1)}, u32[]{:S(2)}, u32[]{:S(2)}) collective-permute-start(f32[2,2,128,128]{3,2,1,0:T(8,128)S(1)} %shift_sum.3.own_ref), channel_id=1, source_target_pairs={{0,4},{1,2},{2,1},{3,7},{4,0},{5,6},{6,5},{7,3},{8,12},{9,10},{10,... | collective-permute-start | bytes 786440 | tf_op jit(solution)/shard_map/ppermute | solution.py:54
  33.4 6.6 %collective-permute-start.10 = (f32[2,2,128,128]{3,2,1,0:T(8,128)S(1)}, f32[2,2,128,128]{3,2,1,0:T(8,128)S(1)}, u32[]{:S(2)}, u32[]{:S(2)}) collective-permute-start(f32[2,2,128,128]{3,2,1,0:T(8,128)S(1)} %shift_sum.3.own_ref), channel_id=1, source_target_pairs={{0,1},{1,0},{2,3},{3,2},{4,5},{5,4},{6,7},{7,6},{8,9},{9,8},{10,11... | collective-permute-start | bytes 786440 | tf_op jit(solution)/shard_map/ppermute | solution.py:54
  36.4 7.9 %collective-permute-start.15 = (f32[2,2,128,128]{3,2,1,0:T(8,128)S(1)}, f32[2,2,128,128]{3,2,1,0:T(8,128)S(1)}, u32[]{:S(2)}, u32[]{:S(2)}) collective-permute-start(f32[2,2,128,128]{3,2,1,0:T(8,128)S(1)} %sandwich.7.own_ref), channel_id=1, source_target_pairs={{0,1},{1,0},{2,3},{3,2},{4,8},{5,9},{6,10},{7,11},{8,4},{9,5},{10,... | collective-permute-start | bytes 786440 | tf_op jit(solution)/shard_map/ppermute | solution.py:54
  36.5 7.8 %collective-permute-start.14 = (f32[2,2,128,128]{3,2,1,0:T(8,128)S(1)}, f32[2,2,128,128]{3,2,1,0:T(8,128)S(1)}, u32[]{:S(2)}, u32[]{:S(2)}) collective-permute-start(f32[2,2,128,128]{3,2,1,0:T(8,128)S(1)} %sandwich.7.own_ref), channel_id=1, source_target_pairs={{0,4},{1,5},{2,6},{3,7},{4,0},{5,1},{6,2},{7,3},{8,12},{9,13},{10,... | collective-permute-start | bytes 786440 | tf_op jit(solution)/shard_map/ppermute | solution.py:54

commit v6 on v5

--- a/solution.py
+++ b/solution.py
@@ -45,8 +45,7 @@
 
 
 def trade(cells, axis, dim):
-    own = cells.shape[dim]
-    got = []
+    own, got = cells.shape[dim], []
     for parity, side in enumerate(partners(axis)):
         edge = cells
         if own != REACH:
@@ -91,18 +90,17 @@
     )(grad_h)
 
 
-def sandwich_kernel(index_ref, right_ref, left_ref, own_ref, one_ref, two_ref, out_ref, green_ref, rest_ref, high_ref, low_ref):
+def sandwich_kernel(index_ref, right_ref, left_ref, *refs):
+    *in_refs, out_ref, green_ref, rest_ref, high_ref, low_ref = refs
     energies, atoms, orb, _ = out_ref.shape
     entries = right_ref.shape[1]
     places = index_ref[...]
-    at = 0
-    for ref in (own_ref, one_ref, two_ref):
-        for a in range(ref.shape[1]):
-            for e in range(energies):
-                high, low = split(ref[e, a])
-                green_ref[at, e * orb : (e + 1) * orb] = high
-                rest_ref[at, e * orb : (e + 1) * orb] = low
-            at += 1
+    sources = [(ref, i) for ref in in_refs for i in range(ref.shape[1])]
+    for at, (ref, i) in enumerate(sources):
+        for e in range(energies):
+            high, low = split(ref[e, i])
+            green_ref[at, e * orb : (e + 1) * orb] = high
+            rest_ref[at, e * orb : (e + 1) * orb] = low
     for a in range(atoms):
         for k in range(entries):
             weight = right_ref[a, k]
@@ -113,8 +111,9 @@
                 high_ref[a, e, k * orb : (k + 1) * orb] = high[e * orb : (e + 1) * orb]
                 low_ref[a, e, k * orb : (k + 1) * orb] = low[e * orb : (e + 1) * orb]
     for a in range(atoms):
-        main = dot(left_ref[a], jnp.concatenate([high_ref[a, e] for e in range(energies)], axis=1))
-        total = main[:orb] + (main[orb:] + dot(left_ref[a, :orb], jnp.concatenate([low_ref[a, e] for e in range(energies)], axis=1)))
+        highs, lows = (jnp.concatenate([ref[a, e] for e in range(energies)], axis=1) for ref in (high_ref, low_ref))
+        main = dot(left_ref[a], highs)
+        total = main[:orb] + (main[orb:] + dot(left_ref[a, :orb], lows))
         for e in range(energies):
             out_ref[e, a] = total[:, e * orb : (e + 1) * orb]
 
@@ -122,15 +121,15 @@
 def sandwich(index, right, left, own, one, two):
     energies, atoms, orb, _ = own.shape
     entries = right.shape[1]
-    sources = atoms + one.shape[1] + two.shape[1]
+    count = atoms + one.shape[1] + two.shape[1]
     return pl.pallas_call(
         sandwich_kernel,
         out_shape=at_hand(own.shape),
         in_specs=[VMEM] * 6,
         out_specs=VMEM,
         scratch_shapes=[
-            pltpu.VMEM((sources, energies * orb, orb), jnp.bfloat16),
-            pltpu.VMEM((sources, energies * orb, orb), jnp.bfloat16),
+            pltpu.VMEM((count, energies * orb, orb), jnp.bfloat16),
+            pltpu.VMEM((count, energies * orb, orb), jnp.bfloat16),
             pltpu.VMEM((atoms, energies, entries * orb, orb), jnp.bfloat16),
             pltpu.VMEM((atoms, energies, entries * orb, orb), jnp.bfloat16),
         ],
@@ -160,18 +159,21 @@
     )(pltpu.with_memory_space_constraint(green, pltpu.HBM))
 
 
-def shifted(weight_ref, refs, e, a):
-    sources = [(ref, s) for ref in refs for s in range(ref.shape[0])]
-    total = weight_ref[e : e + 1, :1] * sources[0][0][sources[0][1], a]
-    for at, (ref, s) in enumerate(sources[1:]):
-        total = total + weight_ref[e : e + 1, at + 1 : at + 2] * ref[s, a]
+def weighted(weight_ref, e, blocks):
+    total = weight_ref[e : e + 1, :1] * blocks[0]
+    for at, block in enumerate(blocks[1:]):
+        total = total + weight_ref[e : e + 1, at + 1 : at + 2] * block
     return total
+
+
+def sources_of(refs, a):
+    return [ref[s, a] for ref in refs for s in range(ref.shape[0])]
 
 
 def shift_sum_kernel(weight_ref, own_ref, one_ref, two_ref, out_ref):
     for e in range(out_ref.shape[0]):
         for a in range(out_ref.shape[1]):
-            out_ref[e, a] = shifted(weight_ref, (own_ref, one_ref, two_ref), e, a)
+            out_ref[e, a] = weighted(weight_ref, e, sources_of((own_ref, one_ref, two_ref), a))
 
 
 def shift_sum(weights, own, one, two):
@@ -196,29 +198,40 @@
 
 
 def dyson_kernel(weight_ref, sigma_ref, own_ref, one_ref, two_ref, real_ref, imag_ref, *out_refs):
-    for e in range(real_ref.shape[0]):
-        for a in range(real_ref.shape[1]):
-            sigma = (sigma_ref[e, a], shifted(weight_ref, (own_ref, one_ref, two_ref), e, a))
-            base = (real_ref[e, a], imag_ref[e, a])
-            moved = complex_product(complex_product(base, sigma), base)
-            for c in range(2):
-                if len(out_refs) == 2:
-                    out_refs[c][e, a] = base[c] + moved[c]
-                else:
-                    out_refs[0][e, a, c] = base[c] + moved[c]
+    energies, atoms = real_ref.shape[:2]
+    cells = [(e, a) for e in range(energies) for a in range(atoms)]
+    base = {at: (real_ref[at], imag_ref[at]) for at in cells}
+    moved = {}
+    for e, a in cells:
+        sigma = (sigma_ref[e, a], weighted(weight_ref, e, sources_of((own_ref, one_ref, two_ref), a)))
+        moved[e, a] = complex_product(base[e, a], sigma)
+    copies = []
+    for at in cells:
+        real, imag = (old + new for old, new in zip(base[at], complex_product(moved[at], base[at])))
+        if len(out_refs) == 2:
+            out_refs[0][at], out_refs[1][at] = real, imag
+        else:
+            out_ref, stage_ref, sems = out_refs
+            stage_ref[*at, 0], stage_ref[*at, 1] = real, imag
+            copies.append(pltpu.make_async_copy(stage_ref.at[*at], out_ref.at[*at], sems.at[len(copies)]))
+            copies[-1].start()
+    for copy in copies:
+        copy.wait()
 
 
 def dyson(weights, sigma, own, one, two, base, whole):
-    shape = base[0].shape
+    energies, atoms, orb, _ = sigma.shape
+    out_shape, out_specs, scratch = (at_hand(sigma.shape), at_hand(sigma.shape)), (VMEM, VMEM), []
     if whole:
-        out_shape = jax.ShapeDtypeStruct(shape[:2] + (2,) + shape[2:], jnp.float32)
-    else:
-        out_shape = (at_hand(shape), at_hand(shape))
+        out_shape = jax.ShapeDtypeStruct((energies, atoms, 2, orb, orb), jnp.float32)
+        out_specs = pl.BlockSpec(memory_space=pltpu.HBM)
+        scratch = [pltpu.VMEM(out_shape.shape, jnp.float32), pltpu.SemaphoreType.DMA((energies * atoms,))]
     return pl.pallas_call(
         dyson_kernel,
         out_shape=out_shape,
         in_specs=[VMEM] * 7,
-        out_specs=VMEM if whole else (VMEM, VMEM),
+        out_specs=out_specs,
+        scratch_shapes=scratch,
         compiler_params=PARAMS,
         name="dyson",
     )(*near(weights, sigma, own, one, two, *base))

time: 46.4 us -> 46.1 us (level)
  no operation moved by 1% of the time
where the time goes in v6:
time: 46.1 us; the launch traced here: 45.7 us
  waiting for transfers between devices  23.4 us (51%)
  starting transfers between devices  10.5 us (23%)
  Pallas kernels  9.41 us (20%)
  local copies, waits for them, and re-layouts  1.91 us (4%)
    ppermute x16, waiting for transfers between devices, trade(): got.append(lax.ppermute(edge, AXES, swaps(axis, parity)))  23.4 us
    ppermute x16, starting transfers between devices, trade(): got.append(lax.ppermute(edge, AXES, swaps(axis, parity)))  10.5 us
    pallas_call x4, Pallas kernels, sandwich(): pl.pallas_call(sandwich_kernel, out_shape=at_hand(own.shape), in_specs=[V...  5.09 us
    pallas_call x2, Pallas kernels, dyson(): pl.pallas_call(dyson_kernel, out_shape=out_shape, in_specs=[VMEM] * 7, ou...  2.29 us
    unnamed x8, local copies, waits for them, and re-layouts  1.89 us
    pallas_call x1, Pallas kernels, parts(): pl.pallas_call(parts_kernel, out_shape=(at_hand(shape), at_hand(shape)),...  1.04 us
  transfers between devices with their start and end apart: 16, of which 11 were waited for; matrix products, arithmetic and copies ran while one was open for 1% of the time, Pallas kernels for 13%

profile of v6, /device:TPU:12, one launch (start us, length us, event | category | flops | bytes accessed | tf_op | source)
XLA Modules:
  0.0 45.7 jit_solution(3167022450307845926)
XLA Ops:
  0.0 1.0 %parts.1 = (f32[2,2,128,128]{3,2,1,0:T(8,128)S(1)}, f32[2,2,128,128]{3,2,1,0:T(8,128)S(1)}) custom-call(f32[2,2,2,128,128]{4,3,2,1,0:T(8,128)} %green_ref.1), custom_call_target="tpu_custom_call" | custom-call | tf_op jit(solution)/shard_map/parts/pallas_call | solution.py:151
  1.1 0.9 %collective-permute-start.1 = (f32[2,2,128,128]{3,2,1,0:T(8,128)S(1)}, f32[2,2,128,128]{3,2,1,0:T(8,128)S(1)}, u32[]{:S(2)}, u32[]{:S(2)}) collective-permute-start(f32[2,2,128,128]{3,2,1,0:T(8,128)S(1)} %get-tuple-element.13.own_ref.real_ref), channel_id=1, source_target_pairs={{0,1},{1,0},{2,3},{3,2},{4,8},{5,9},{6,10},{7,11},{8,4},{9,5},{10,... | collective-permute-start | bytes 786440 | tf_op jit(solution)/shard_map/ppermute | solution.py:53
  2.0 0.7 %collective-permute-start = (f32[2,2,128,128]{3,2,1,0:T(8,128)S(1)}, f32[2,2,128,128]{3,2,1,0:T(8,128)S(1)}, u32[]{:S(2)}, u32[]{:S(2)}) collective-permute-start(f32[2,2,128,128]{3,2,1,0:T(8,128)S(1)} %get-tuple-element.13.own_ref.real_ref), channel_id=1, source_target_pairs={{0,4},{1,5},{2,6},{3,7},{4,0},{5,1},{6,2},{7,3},{8,12},{9,13},{10,... | collective-permute-start | bytes 786440 | tf_op jit(solution)/shard_map/ppermute | solution.py:53
  2.7 1.6 %collective-permute-start.5 = (f32[2,2,128,128]{3,2,1,0:T(8,128)S(1)}, f32[2,2,128,128]{3,2,1,0:T(8,128)S(1)}, u32[]{:S(2)}, u32[]{:S(2)}) collective-permute-start(f32[2,2,128,128]{3,2,1,0:T(8,128)S(1)} %get-tuple-element.14.refs_0_.imag_ref), channel_id=1, source_target_pairs={{0,4},{1,2},{2,1},{3,7},{4,0},{5,6},{6,5},{7,3},{8,12},{9,10},{10,... | collective-permute-start | bytes 786440 | tf_op jit(solution)/shard_map/ppermute | solution.py:53
  4.5 0.6 %copy-done.2 = f32[4]{0:T(128)S(1)} copy-done((f32[4]{0:T(128)S(1)}, f32[4]{0:T(128)}, u32[]{:S(2)}) %copy-start.2) | copy-done | bytes 40
  5.2 1.2 %copy-done = f32[2,8,128,128]{3,2,1,0:T(8,128)S(1)} copy-done((f32[2,8,128,128]{3,2,1,0:T(8,128)S(1)}, f32[2,8,128,128]{3,2,1,0:T(8,128)}, u32[]{:S(2)}) %copy-start) | copy-done | bytes 1048600
  6.4 0.6 %prepare.1 = (bf16[2,8,128,256]{3,2,1,0:T(8,128)(2,1)S(1)}, bf16[2,256,1024]{2,1,0:T(8,128)(2,1)S(1)}) custom-call(f32[2,8,128,128]{3,2,1,0:T(8,128)S(1)} %copy-done), custom_call_target="tpu_custom_call" | custom-call | tf_op jit(solution)/shard_map/prepare/pallas_call | solution.py:80
  7.1 2.6 %collective-permute-done.1.two_ref = f32[2,2,128,128]{3,2,1,0:T(8,128)S(1)} collective-permute-done((f32[2,2,128,128]{3,2,1,0:T(8,128)S(1)}, f32[2,2,128,128]{3,2,1,0:T(8,128)S(1)}, u32[]{:S(2)}, u32[]{:S(2)}) %collective-permute-start.1) | collective-permute-done | bytes 262176 | tf_op jit(solution)/shard_map/ppermute | solution.py:53
  9.7 0.2 shift_sum.2.refs_0_
  9.9 1.6 %collective-permute-start.3 = (f32[2,2,128,128]{3,2,1,0:T(8,128)S(1)}, f32[2,2,128,128]{3,2,1,0:T(8,128)S(1)}, u32[]{:S(2)}, u32[]{:S(2)}) collective-permute-start(f32[2,2,128,128]{3,2,1,0:T(8,128)S(1)} %shift_sum.2.refs_0_), channel_id=1, source_target_pairs={{0,4},{1,2},{2,1},{3,7},{4,0},{5,6},{6,5},{7,3},{8,12},{9,10},{10,... | collective-permute-start | bytes 786440 | tf_op jit(solution)/shard_map/ppermute | solution.py:53
  11.6 0.7 %collective-permute-done.4.refs_1_ = f32[2,2,128,128]{3,2,1,0:T(8,128)S(1)} collective-permute-done((f32[2,2,128,128]{3,2,1,0:T(8,128)S(1)}, f32[2,2,128,128]{3,2,1,0:T(8,128)S(1)}, u32[]{:S(2)}, u32[]{:S(2)}) %collective-permute-start.4) | collective-permute-done | bytes 262176 | tf_op jit(solution)/shard_map/ppermute | solution.py:53
  12.2 1.3 %sandwich.5.own_ref = f32[2,2,128,128]{3,2,1,0:T(8,128)S(1)} custom-call(s32[2,8]{1,0:T(2,128)S(1)} %compare_select_fusion.1.index_ref, bf16[2,8,128,256]{3,2,1,0:T(8,128)(2,1)S(1)} %get-tuple-element.11.right_ref, bf16[2,256,1024]{2,1,0:T(8,128)(2,1)S(1)} %get-tuple-element.12.left_ref, f32[2,2,128,128]{3,2,1,0:T(8,128)S(1)} %get-tuple-element.14.refs_0_.imag_ref, ...), custom_call_target="tpu_custom_call" | custom-call | tf_op jit(solution)/shard_map/sandwich/pallas_call | solution.py:125
  13.5 0.9 %collective-permute-start.7 = (f32[2,2,128,128]{3,2,1,0:T(8,128)S(1)}, f32[2,2,128,128]{3,2,1,0:T(8,128)S(1)}, u32[]{:S(2)}, u32[]{:S(2)}) collective-permute-start(f32[2,2,128,128]{3,2,1,0:T(8,128)S(1)} %sandwich.5.own_ref), channel_id=1, source_target_pairs={{0,1},{1,0},{2,3},{3,2},{4,8},{5,9},{6,10},{7,11},{8,4},{9,5},{10,... | collective-permute-start | bytes 786440 | tf_op jit(solution)/shard_map/ppermute | solution.py:53
  14.4 0.7 %collective-permute-start.6 = (f32[2,2,128,128]{3,2,1,0:T(8,128)S(1)}, f32[2,2,128,128]{3,2,1,0:T(8,128)S(1)}, u32[]{:S(2)}, u32[]{:S(2)}) collective-permute-start(f32[2,2,128,128]{3,2,1,0:T(8,128)S(1)} %sandwich.5.own_ref), channel_id=1, source_target_pairs={{0,4},{1,5},{2,6},{3,7},{4,0},{5,1},{6,2},{7,3},{8,12},{9,13},{10,... | collective-permute-start | bytes 786440 | tf_op jit(solution)/shard_map/ppermute | solution.py:53
  15.1 2.2 %collective-permute-done.3.refs_2_ = f32[2,2,128,128]{3,2,1,0:T(8,128)S(1)} collective-permute-done((f32[2,2,128,128]{3,2,1,0:T(8,128)S(1)}, f32[2,2,128,128]{3,2,1,0:T(8,128)S(1)}, u32[]{:S(2)}, u32[]{:S(2)}) %collective-permute-start.3) | collective-permute-done | bytes 262176 | tf_op jit(solution)/shard_map/ppermute | solution.py:53
  17.3 1.3 %collective-permute-done.2.refs_1_ = f32[2,2,128,128]{3,2,1,0:T(8,128)S(1)} collective-permute-done((f32[2,2,128,128]{3,2,1,0:T(8,128)S(1)}, f32[2,2,128,128]{3,2,1,0:T(8,128)S(1)}, u32[]{:S(2)}, u32[]{:S(2)}) %collective-permute-start.2) | collective-permute-done | bytes 262176 | tf_op jit(solution)/shard_map/ppermute | solution.py:53
  18.6 1.3 %sandwich.4.sigma_ref = f32[2,2,128,128]{3,2,1,0:T(8,128)S(1)} custom-call(s32[2,8]{1,0:T(2,128)S(1)} %compare_select_fusion.1.index_ref, bf16[2,8,128,256]{3,2,1,0:T(8,128)(2,1)S(1)} %get-tuple-element.11.right_ref, bf16[2,256,1024]{2,1,0:T(8,128)(2,1)S(1)} %get-tuple-element.12.left_ref, f32[2,2,128,128]{3,2,1,0:T(8,128)S(1)} %shift_sum.2.refs_0_, ...), custom_call_target="tpu_custom_call" | custom-call | tf_op jit(solution)/shard_map/sandwich/pallas_call | solution.py:125
  19.9 3.0 %collective-permute-done.7.two_ref = f32[2,2,128,128]{3,2,1,0:T(8,128)S(1)} collective-permute-done((f32[2,2,128,128]{3,2,1,0:T(8,128)S(1)}, f32[2,2,128,128]{3,2,1,0:T(8,128)S(1)}, u32[]{:S(2)}, u32[]{:S(2)}) %collective-permute-start.7) | collective-permute-done | bytes 262176 | tf_op jit(solution)/shard_map/ppermute | solution.py:53
  22.9 0.8 %dyson.2 = (f32[2,2,128,128]{3,2,1,0:T(8,128)S(1)}, f32[2,2,128,128]{3,2,1,0:T(8,128)S(1)}) custom-call(f32[2,6]{1,0:T(2,128)S(1)} %select_reduce_fusion.weight_ref, f32[2,2,128,128]{3,2,1,0:T(8,128)S(1)} %sandwich.4.sigma_ref, f32[2,2,128,128]{3,2,1,0:T(8,128)S(1)} %sandwich.5.own_ref, f32[2,2,128,128]{3,2,1,0:T(8,128)S(1)} %collective-permute-done.6.one_ref, ...), custom_call_target="tpu_custom_call" | custom-call | tf_op jit(solution)/shard_map/dyson/pallas_call | solution.py:229
  23.7 1.0 %collective-permute-start.9 = (f32[2,2,128,128]{3,2,1,0:T(8,128)S(1)}, f32[2,2,128,128]{3,2,1,0:T(8,128)S(1)}, u32[]{:S(2)}, u32[]{:S(2)}) collective-permute-start(f32[2,2,128,128]{3,2,1,0:T(8,128)S(1)} %get-tuple-element.15.own_ref), channel_id=1, source_target_pairs={{0,1},{1,0},{2,3},{3,2},{4,8},{5,9},{6,10},{7,11},{8,4},{9,5},{10,... | collective-permute-start | bytes 786440 | tf_op jit(solution)/shard_map/ppermute | solution.py:53
  24.7 1.1 %collective-permute-start.13 = (f32[2,2,128,128]{3,2,1,0:T(8,128)S(1)}, f32[2,2,128,128]{3,2,1,0:T(8,128)S(1)}, u32[]{:S(2)}, u32[]{:S(2)}) collective-permute-start(f32[2,2,128,128]{3,2,1,0:T(8,128)S(1)} %get-tuple-element.16.refs_0_), channel_id=1, source_target_pairs={{0,4},{1,2},{2,1},{3,7},{4,0},{5,6},{6,5},{7,3},{8,12},{9,10},{10,... | collective-permute-start | bytes 786440 | tf_op jit(solution)/shard_map/ppermute | solution.py:53
  25.8 0.9 %collective-permute-start.12 = (f32[2,2,128,128]{3,2,1,0:T(8,128)S(1)}, f32[2,2,128,128]{3,2,1,0:T(8,128)S(1)}, u32[]{:S(2)}, u32[]{:S(2)}) collective-permute-start(f32[2,2,128,128]{3,2,1,0:T(8,128)S(1)} %get-tuple-element.16.refs_0_), channel_id=1, source_target_pairs={{0,1},{1,0},{2,3},{3,2},{4,5},{5,4},{6,7},{7,6},{8,9},{9,8},{10,11... | collective-permute-start | bytes 786440 | tf_op jit(solution)/shard_map/ppermute | solution.py:53
  26.7 5.5 %collective-permute-done.9.two_ref = f32[2,2,128,128]{3,2,1,0:T(8,128)S(1)} collective-permute-done((f32[2,2,128,128]{3,2,1,0:T(8,128)S(1)}, f32[2,2,128,128]{3,2,1,0:T(8,128)S(1)}, u32[]{:S(2)}, u32[]{:S(2)}) %collective-permute-start.9) | collective-permute-done | bytes 262176 | tf_op jit(solution)/shard_map/ppermute | solution.py:53
  32.4 0.9 %collective-permute-start.11 = (f32[2,2,128,128]{3,2,1,0:T(8,128)S(1)}, f32[2,2,128,128]{3,2,1,0:T(8,128)S(1)}, u32[]{:S(2)}, u32[]{:S(2)}) collective-permute-start(f32[2,2,128,128]{3,2,1,0:T(8,128)S(1)} %shift_sum.3.refs_0_), channel_id=1, source_target_pairs={{0,4},{1,2},{2,1},{3,7},{4,0},{5,6},{6,5},{7,3},{8,12},{9,10},{10,... | collective-permute-start | bytes 786440 | tf_op jit(solution)/shard_map/ppermute | solution.py:53
  33.3 0.6 %collective-permute-done.13.refs_2_ = f32[2,2,128,128]{3,2,1,0:T(8,128)S(1)} collective-permute-done((f32[2,2,128,128]{3,2,1,0:T(8,128)S(1)}, f32[2,2,128,128]{3,2,1,0:T(8,128)S(1)}, u32[]{:S(2)}, u32[]{:S(2)}) %collective-permute-start.13) | collective-permute-done | bytes 262176 | tf_op jit(solution)/shard_map/ppermute | solution.py:53
  33.9 1.1 %collective-permute-done.12.refs_1_ = f32[2,2,128,128]{3,2,1,0:T(8,128)S(1)} collective-permute-done((f32[2,2,128,128]{3,2,1,0:T(8,128)S(1)}, f32[2,2,128,128]{3,2,1,0:T(8,128)S(1)}, u32[]{:S(2)}, u32[]{:S(2)}) %collective-permute-start.12) | collective-permute-done | bytes 262176 | tf_op jit(solution)/shard_map/ppermute | solution.py:53
  35.0 1.3 %sandwich.7.own_ref = f32[2,2,128,128]{3,2,1,0:T(8,128)S(1)} custom-call(s32[2,8]{1,0:T(2,128)S(1)} %compare_select_fusion.1.index_ref, bf16[2,8,128,256]{3,2,1,0:T(8,128)(2,1)S(1)} %get-tuple-element.11.right_ref, bf16[2,256,1024]{2,1,0:T(8,128)(2,1)S(1)} %get-tuple-element.12.left_ref, f32[2,2,128,128]{3,2,1,0:T(8,128)S(1)} %get-tuple-element.16.refs_0_, ...), custom_call_target="tpu_custom_call" | custom-call | tf_op jit(solution)/shard_map/sandwich/pallas_call | solution.py:125
  36.4 2.6 %collective-permute-done.11.refs_2_ = f32[2,2,128,128]{3,2,1,0:T(8,128)S(1)} collective-permute-done((f32[2,2,128,128]{3,2,1,0:T(8,128)S(1)}, f32[2,2,128,128]{3,2,1,0:T(8,128)S(1)}, u32[]{:S(2)}, u32[]{:S(2)}) %collective-permute-start.11) | collective-permute-done | bytes 262176 | tf_op jit(solution)/shard_map/ppermute | solution.py:53
  39.0 0.8 %collective-permute-done.10.refs_1_ = f32[2,2,128,128]{3,2,1,0:T(8,128)S(1)} collective-permute-done((f32[2,2,128,128]{3,2,1,0:T(8,128)S(1)}, f32[2,2,128,128]{3,2,1,0:T(8,128)S(1)}, u32[]{:S(2)}, u32[]{:S(2)}) %collective-permute-start.10) | collective-permute-done | bytes 262176 | tf_op jit(solution)/shard_map/ppermute | solution.py:53
  39.9 1.3 %sandwich.6.sigma_ref = f32[2,2,128,128]{3,2,1,0:T(8,128)S(1)} custom-call(s32[2,8]{1,0:T(2,128)S(1)} %compare_select_fusion.1.index_ref, bf16[2,8,128,256]{3,2,1,0:T(8,128)(2,1)S(1)} %get-tuple-element.11.right_ref, bf16[2,256,1024]{2,1,0:T(8,128)(2,1)S(1)} %get-tuple-element.12.left_ref, f32[2,2,128,128]{3,2,1,0:T(8,128)S(1)} %shift_sum.3.refs_0_, ...), custom_call_target="tpu_custom_call" | custom-call | tf_op jit(solution)/shard_map/sandwich/pallas_call | solution.py:125
  41.2 3.0 %collective-permute-done.15.two_ref = f32[2,2,128,128]{3,2,1,0:T(8,128)S(1)} collective-permute-done((f32[2,2,128,128]{3,2,1,0:T(8,128)S(1)}, f32[2,2,128,128]{3,2,1,0:T(8,128)S(1)}, u32[]{:S(2)}, u32[]{:S(2)}) %collective-permute-start.15) | collective-permute-done | bytes 262176 | tf_op jit(solution)/shard_map/ppermute | solution.py:53
  44.2 1.5 %dyson.3 = f32[2,2,2,128,128]{4,3,2,1,0:T(8,128)} custom-call(f32[2,6]{1,0:T(2,128)S(1)} %select_reduce_fusion.weight_ref, f32[2,2,128,128]{3,2,1,0:T(8,128)S(1)} %sandwich.6.sigma_ref, f32[2,2,128,128]{3,2,1,0:T(8,128)S(1)} %sandwich.7.own_ref, f32[2,2,128,128]{3,2,1,0:T(8,128)S(1)} %collective-permute-done.14.one_ref, ...), custom_call_target="tpu_custom_call" | custom-call | tf_op jit(solution)/shard_map/dyson/pallas_call | solution.py:229
  (28 shorter events, 0.8 us)
Async XLA Ops:
  1.1 8.7 %collective-permute-start.1 = (f32[2,2,128,128]{3,2,1,0:T(8,128)S(1)}, f32[2,2,128,128]{3,2,1,0:T(8,128)S(1)}, u32[]{:S(2)}, u32[]{:S(2)}) collective-permute-start(f32[2,2,128,128]{3,2,1,0:T(8,128)S(1)} %get-tuple-element.13.own_ref.real_ref), channel_id=1, source_target_pairs={{0,1},{1,0},{2,3},{3,2},{4,8},{5,9},{6,10},{7,11},{8,4},{9,5},{10,... | collective-permute-start | bytes 786440 | tf_op jit(solution)/shard_map/ppermute | solution.py:53
  2.0 7.7 %collective-permute-start = (f32[2,2,128,128]{3,2,1,0:T(8,128)S(1)}, f32[2,2,128,128]{3,2,1,0:T(8,128)S(1)}, u32[]{:S(2)}, u32[]{:S(2)}) collective-permute-start(f32[2,2,128,128]{3,2,1,0:T(8,128)S(1)} %get-tuple-element.13.own_ref.real_ref), channel_id=1, source_target_pairs={{0,4},{1,5},{2,6},{3,7},{4,0},{5,1},{6,2},{7,3},{8,12},{9,13},{10,... | collective-permute-start | bytes 786440 | tf_op jit(solution)/shard_map/ppermute | solution.py:53
  2.7 8.8 %collective-permute-start.5 = (f32[2,2,128,128]{3,2,1,0:T(8,128)S(1)}, f32[2,2,128,128]{3,2,1,0:T(8,128)S(1)}, u32[]{:S(2)}, u32[]{:S(2)}) collective-permute-start(f32[2,2,128,128]{3,2,1,0:T(8,128)S(1)} %get-tuple-element.14.refs_0_.imag_ref), channel_id=1, source_target_pairs={{0,4},{1,2},{2,1},{3,7},{4,0},{5,6},{6,5},{7,3},{8,12},{9,10},{10,... | collective-permute-start | bytes 786440 | tf_op jit(solution)/shard_map/ppermute | solution.py:53
  4.3 7.9 %collective-permute-start.4 = (f32[2,2,128,128]{3,2,1,0:T(8,128)S(1)}, f32[2,2,128,128]{3,2,1,0:T(8,128)S(1)}, u32[]{:S(2)}, u32[]{:S(2)}) collective-permute-start(f32[2,2,128,128]{3,2,1,0:T(8,128)S(1)} %get-tuple-element.14.refs_0_.imag_ref), channel_id=1, source_target_pairs={{0,1},{1,0},{2,3},{3,2},{4,5},{5,4},{6,7},{7,6},{8,9},{9,8},{10,11... | collective-permute-start | bytes 786440 | tf_op jit(solution)/shard_map/ppermute | solution.py:53
  4.4 0.7 %copy-start.2 = (f32[4]{0:T(128)S(1)}, f32[4]{0:T(128)}, u32[]{:S(2)}) copy-start(f32[4]{0:T(128)} %param.9) | copy-start | bytes 52
  4.4 0.7 %copy-start.3 = (s32[4]{0:T(128)S(1)}, s32[4]{0:T(128)}, u32[]{:S(2)}) copy-start(s32[4]{0:T(128)} %param.8) | copy-start | bytes 52
  5.2 1.2 %copy-start = (f32[2,8,128,128]{3,2,1,0:T(8,128)S(1)}, f32[2,8,128,128]{3,2,1,0:T(8,128)}, u32[]{:S(2)}) copy-start(f32[2,8,128,128]{3,2,1,0:T(8,128)} %grad_ref.1) | copy-start | bytes 3145732
  6.4 0.7 %copy-start.1 = (s32[2,8]{1,0:T(2,128)S(1)}, s32[2,8]{1,0:T(2,128)}, u32[]{:S(2)}) copy-start(s32[2,8]{1,0:T(2,128)} %param.7) | copy-start | bytes 196
  9.9 7.4 %collective-permute-start.3 = (f32[2,2,128,128]{3,2,1,0:T(8,128)S(1)}, f32[2,2,128,128]{3,2,1,0:T(8,128)S(1)}, u32[]{:S(2)}, u32[]{:S(2)}) collective-permute-start(f32[2,2,128,128]{3,2,1,0:T(8,128)S(1)} %shift_sum.2.refs_0_), channel_id=1, source_target_pairs={{0,4},{1,2},{2,1},{3,7},{4,0},{5,6},{6,5},{7,3},{8,12},{9,10},{10,... | collective-permute-start | bytes 786440 | tf_op jit(solution)/shard_map/ppermute | solution.py:53
  11.6 7.1 %collective-permute-start.2 = (f32[2,2,128,128]{3,2,1,0:T(8,128)S(1)}, f32[2,2,128,128]{3,2,1,0:T(8,128)S(1)}, u32[]{:S(2)}, u32[]{:S(2)}) collective-permute-start(f32[2,2,128,128]{3,2,1,0:T(8,128)S(1)} %shift_sum.2.refs_0_), channel_id=1, source_target_pairs={{0,1},{1,0},{2,3},{3,2},{4,5},{5,4},{6,7},{7,6},{8,9},{9,8},{10,11... | collective-permute-start | bytes 786440 | tf_op jit(solution)/shard_map/ppermute | solution.py:53
  13.5 9.4 %collective-permute-start.7 = (f32[2,2,128,128]{3,2,1,0:T(8,128)S(1)}, f32[2,2,128,128]{3,2,1,0:T(8,128)S(1)}, u32[]{:S(2)}, u32[]{:S(2)}) collective-permute-start(f32[2,2,128,128]{3,2,1,0:T(8,128)S(1)} %sandwich.5.own_ref), channel_id=1, source_target_pairs={{0,1},{1,0},{2,3},{3,2},{4,8},{5,9},{6,10},{7,11},{8,4},{9,5},{10,... | collective-permute-start | bytes 786440 | tf_op jit(solution)/shard_map/ppermute | solution.py:53
  14.4 8.5 %collective-permute-start.6 = (f32[2,2,128,128]{3,2,1,0:T(8,128)S(1)}, f32[2,2,128,128]{3,2,1,0:T(8,128)S(1)}, u32[]{:S(2)}, u32[]{:S(2)}) collective-permute-start(f32[2,2,128,128]{3,2,1,0:T(8,128)S(1)} %sandwich.5.own_ref), channel_id=1, source_target_pairs={{0,4},{1,5},{2,6},{3,7},{4,0},{5,1},{6,2},{7,3},{8,12},{9,13},{10,... | collective-permute-start | bytes 786440 | tf_op jit(solution)/shard_map/ppermute | solution.py:53
  23.7 8.5 %collective-permute-start.9 = (f32[2,2,128,128]{3,2,1,0:T(8,128)S(1)}, f32[2,2,128,128]{3,2,1,0:T(8,128)S(1)}, u32[]{:S(2)}, u32[]{:S(2)}) collective-permute-start(f32[2,2,128,128]{3,2,1,0:T(8,128)S(1)} %get-tuple-element.15.own_ref), channel_id=1, source_target_pairs={{0,1},{1,0},{2,3},{3,2},{4,8},{5,9},{6,10},{7,11},{8,4},{9,5},{10,... | collective-permute-start | bytes 786440 | tf_op jit(solution)/shard_map/ppermute | solution.py:53
  24.7 7.5 %collective-permute-start.8 = (f32[2,2,128,128]{3,2,1,0:T(8,128)S(1)}, f32[2,2,128,128]{3,2,1,0:T(8,128)S(1)}, u32[]{:S(2)}, u32[]{:S(2)}) collective-permute-start(f32[2,2,128,128]{3,2,1,0:T(8,128)S(1)} %get-tuple-element.15.own_ref), channel_id=1, source_target_pairs={{0,4},{1,5},{2,6},{3,7},{4,0},{5,1},{6,2},{7,3},{8,12},{9,13},{10,... | collective-permute-start | bytes 786440 | tf_op jit(solution)/shard_map/ppermute | solution.py:53
  24.7 9.2 %collective-permute-start.13 = (f32[2,2,128,128]{3,2,1,0:T(8,128)S(1)}, f32[2,2,128,128]{3,2,1,0:T(8,128)S(1)}, u32[]{:S(2)}, u32[]{:S(2)}) collective-permute-start(f32[2,2,128,128]{3,2,1,0:T(8,128)S(1)} %get-tuple-element.16.refs_0_), channel_id=1, source_target_pairs={{0,4},{1,2},{2,1},{3,7},{4,0},{5,6},{6,5},{7,3},{8,12},{9,10},{10,... | collective-permute-start | bytes 786440 | tf_op jit(solution)/shard_map/ppermute | solution.py:53
  25.8 9.2 %collective-permute-start.12 = (f32[2,2,128,128]{3,2,1,0:T(8,128)S(1)}, f32[2,2,128,128]{3,2,1,0:T(8,128)S(1)}, u32[]{:S(2)}, u32[]{:S(2)}) collective-permute-start(f32[2,2,128,128]{3,2,1,0:T(8,128)S(1)} %get-tuple-element.16.refs_0_), channel_id=1, source_target_pairs={{0,1},{1,0},{2,3},{3,2},{4,5},{5,4},{6,7},{7,6},{8,9},{9,8},{10,11... | collective-permute-start | bytes 786440 | tf_op jit(solution)/shard_map/ppermute | solution.py:53
  32.4 6.6 %collective-permute-start.11 = (f32[2,2,128,128]{3,2,1,0:T(8,128)S(1)}, f32[2,2,128,128]{3,2,1,0:T(8,128)S(1)}, u32[]{:S(2)}, u32[]{:S(2)}) collective-permute-start(f32[2,2,128,128]{3,2,1,0:T(8,128)S(1)} %shift_sum.3.refs_0_), channel_id=1, source_target_pairs={{0,4},{1,2},{2,1},{3,7},{4,0},{5,6},{6,5},{7,3},{8,12},{9,10},{10,... | collective-permute-start | bytes 786440 | tf_op jit(solution)/shard_map/ppermute | solution.py:53
  33.3 6.6 %collective-permute-start.10 = (f32[2,2,128,128]{3,2,1,0:T(8,128)S(1)}, f32[2,2,128,128]{3,2,1,0:T(8,128)S(1)}, u32[]{:S(2)}, u32[]{:S(2)}) collective-permute-start(f32[2,2,128,128]{3,2,1,0:T(8,128)S(1)} %shift_sum.3.refs_0_), channel_id=1, source_target_pairs={{0,1},{1,0},{2,3},{3,2},{4,5},{5,4},{6,7},{7,6},{8,9},{9,8},{10,11... | collective-permute-start | bytes 786440 | tf_op jit(solution)/shard_map/ppermute | solution.py:53
  36.3 7.9 %collective-permute-start.15 = (f32[2,2,128,128]{3,2,1,0:T(8,128)S(1)}, f32[2,2,128,128]{3,2,1,0:T(8,128)S(1)}, u32[]{:S(2)}, u32[]{:S(2)}) collective-permute-start(f32[2,2,128,128]{3,2,1,0:T(8,128)S(1)} %sandwich.7.own_ref), channel_id=1, source_target_pairs={{0,1},{1,0},{2,3},{3,2},{4,8},{5,9},{6,10},{7,11},{8,4},{9,5},{10,... | collective-permute-start | bytes 786440 | tf_op jit(solution)/shard_map/ppermute | solution.py:53
  36.4 7.8 %collective-permute-start.14 = (f32[2,2,128,128]{3,2,1,0:T(8,128)S(1)}, f32[2,2,128,128]{3,2,1,0:T(8,128)S(1)}, u32[]{:S(2)}, u32[]{:S(2)}) collective-permute-start(f32[2,2,128,128]{3,2,1,0:T(8,128)S(1)} %sandwich.7.own_ref), channel_id=1, source_target_pairs={{0,4},{1,5},{2,6},{3,7},{4,0},{5,1},{6,2},{7,3},{8,12},{9,13},{10,... | collective-permute-start | bytes 786440 | tf_op jit(solution)/shard_map/ppermute | solution.py:53

commit v7 on v6

--- a/solution.py
+++ b/solution.py
@@ -32,7 +32,7 @@
                 to[axis] = there
             elif axis == "space" and sizes["energy"] % 2 == 0:
                 to["energy"] = energy ^ 1
-            elif axis == "energy" and count % 2 == 0:
+            elif axis == "energy" and sizes["space"] % 2 == 0:
                 to["space"] = space ^ 1
             pairs.append((energy * sizes["space"] + space, to["energy"] * sizes["space"] + to["space"]))
     return pairs
@@ -68,11 +68,11 @@
     for a in range(atoms):
         for k in range(entries):
             high, low = split(grad_ref[a, k])
-            left_ref[a, :orb, k * orb : (k + 1) * orb] = high
-            left_ref[a, orb:, k * orb : (k + 1) * orb] = low
+            left_ref[a, k, :orb] = high
+            left_ref[a, k, orb:] = low
             high, low = split(grad_ref[a, k].T)
-            right_ref[a, k, :, :orb] = high
-            right_ref[a, k, :, orb:] = low
+            right_ref[a, k, 0] = high
+            right_ref[a, k, 1] = low
 
 
 def prepare(grad_h):
@@ -80,8 +80,8 @@
     return pl.pallas_call(
         prepare_kernel,
         out_shape=(
-            at_hand((atoms, entries, orb, 2 * orb), jnp.bfloat16),
-            at_hand((atoms, 2 * orb, entries * orb), jnp.bfloat16),
+            at_hand((atoms, entries, 2, orb, orb), jnp.bfloat16),
+            at_hand((atoms, entries, 2 * orb, orb), jnp.bfloat16),
         ),
         in_specs=[VMEM],
         out_specs=(VMEM, VMEM),
@@ -103,7 +103,7 @@
             rest_ref[at, e * orb : (e + 1) * orb] = low
     for a in range(atoms):
         for k in range(entries):
-            weight = right_ref[a, k]
+            weight = jnp.concatenate([right_ref[a, k, 0], right_ref[a, k, 1]], axis=1)
             n = places[a, k]
             both = dot(jnp.concatenate([green_ref[n], rest_ref[n]], axis=1), jnp.concatenate([weight, weight], axis=0))
             high, low = split(both[:, :orb] + both[:, orb:])
@@ -112,8 +112,9 @@
                 low_ref[a, e, k * orb : (k + 1) * orb] = low[e * orb : (e + 1) * orb]
     for a in range(atoms):
         highs, lows = (jnp.concatenate([ref[a, e] for e in range(energies)], axis=1) for ref in (high_ref, low_ref))
-        main = dot(left_ref[a], highs)
-        total = main[:orb] + (main[orb:] + dot(left_ref[a, :orb], lows))
+        left = jnp.concatenate([left_ref[a, k] for k in range(entries)], axis=1)
+        main = dot(left, highs)
+        total = main[:orb] + (main[orb:] + dot(left[:orb], lows))
         for e in range(energies):
             out_ref[e, a] = total[:, e * orb : (e + 1) * orb]
 

time: 46.1 us -> 46.1 us (level)
  no operation moved by 1% of the time
where the time goes in v7:
time: 46.1 us; the launch traced here: 45.7 us
  waiting for transfers between devices  23.4 us (51%)
  starting transfers between devices  10.5 us (23%)
  Pallas kernels  9.25 us (20%)
  local copies, waits for them, and re-layouts  2.09 us (5%)
    ppermute x16, waiting for transfers between devices, trade(): got.append(lax.ppermute(edge, AXES, swaps(axis, parity)))  23.4 us
    ppermute x16, starting transfers between devices, trade(): got.append(lax.ppermute(edge, AXES, swaps(axis, parity)))  10.5 us
    pallas_call x4, Pallas kernels, sandwich(): pl.pallas_call(sandwich_kernel, out_shape=at_hand(own.shape), in_specs=[V...  5.12 us
    pallas_call x2, Pallas kernels, dyson(): pl.pallas_call(dyson_kernel, out_shape=out_shape, in_specs=[VMEM] * 7, ou...  2.28 us
    unnamed x8, local copies, waits for them, and re-layouts  2.07 us
    pallas_call x1, Pallas kernels, parts(): pl.pallas_call(parts_kernel, out_shape=(at_hand(shape), at_hand(shape)),...  1.04 us
  transfers between devices with their start and end apart: 16, of which 11 were waited for; matrix products, arithmetic and copies ran while one was open for 1% of the time, Pallas kernels for 13%

profile of v7, /device:TPU:12, one launch (start us, length us, event | category | flops | bytes accessed | tf_op | source)
XLA Modules:
  0.0 45.7 jit_solution(7131208034760806797)
XLA Ops:
  0.0 1.0 %parts.1 = (f32[2,2,128,128]{3,2,1,0:T(8,128)S(1)}, f32[2,2,128,128]{3,2,1,0:T(8,128)S(1)}) custom-call(f32[2,2,2,128,128]{4,3,2,1,0:T(8,128)} %green_ref.1), custom_call_target="tpu_custom_call" | custom-call | tf_op jit(solution)/shard_map/parts/pallas_call | solution.py:152
  1.1 0.9 %collective-permute-start.1 = (f32[2,2,128,128]{3,2,1,0:T(8,128)S(1)}, f32[2,2,128,128]{3,2,1,0:T(8,128)S(1)}, u32[]{:S(2)}, u32[]{:S(2)}) collective-permute-start(f32[2,2,128,128]{3,2,1,0:T(8,128)S(1)} %get-tuple-element.13.own_ref.real_ref), channel_id=1, source_target_pairs={{0,1},{1,0},{2,3},{3,2},{4,8},{5,9},{6,10},{7,11},{8,4},{9,5},{10,... | collective-permute-start | bytes 786440 | tf_op jit(solution)/shard_map/ppermute | solution.py:53
  2.0 0.7 %collective-permute-start = (f32[2,2,128,128]{3,2,1,0:T(8,128)S(1)}, f32[2,2,128,128]{3,2,1,0:T(8,128)S(1)}, u32[]{:S(2)}, u32[]{:S(2)}) collective-permute-start(f32[2,2,128,128]{3,2,1,0:T(8,128)S(1)} %get-tuple-element.13.own_ref.real_ref), channel_id=1, source_target_pairs={{0,4},{1,5},{2,6},{3,7},{4,0},{5,1},{6,2},{7,3},{8,12},{9,13},{10,... | collective-permute-start | bytes 786440 | tf_op jit(solution)/shard_map/ppermute | solution.py:53
  2.7 1.6 %collective-permute-start.5 = (f32[2,2,128,128]{3,2,1,0:T(8,128)S(1)}, f32[2,2,128,128]{3,2,1,0:T(8,128)S(1)}, u32[]{:S(2)}, u32[]{:S(2)}) collective-permute-start(f32[2,2,128,128]{3,2,1,0:T(8,128)S(1)} %get-tuple-element.14.refs_0_.imag_ref), channel_id=1, source_target_pairs={{0,4},{1,2},{2,1},{3,7},{4,0},{5,6},{6,5},{7,3},{8,12},{9,10},{10,... | collective-permute-start | bytes 786440 | tf_op jit(solution)/shard_map/ppermute | solution.py:53
  4.5 0.6 %copy-done.2 = f32[4]{0:T(128)S(1)} copy-done((f32[4]{0:T(128)S(1)}, f32[4]{0:T(128)}, u32[]{:S(2)}) %copy-start.2) | copy-done | bytes 40
  5.2 1.2 %copy-done = f32[2,8,128,128]{3,2,1,0:T(8,128)S(1)} copy-done((f32[2,8,128,128]{3,2,1,0:T(8,128)S(1)}, f32[2,8,128,128]{3,2,1,0:T(8,128)}, u32[]{:S(2)}) %copy-start) | copy-done | bytes 1048600
  6.4 0.4 prepare.1
  6.8 0.3 copy-done.1
  7.1 2.6 %collective-permute-done.1.two_ref = f32[2,2,128,128]{3,2,1,0:T(8,128)S(1)} collective-permute-done((f32[2,2,128,128]{3,2,1,0:T(8,128)S(1)}, f32[2,2,128,128]{3,2,1,0:T(8,128)S(1)}, u32[]{:S(2)}, u32[]{:S(2)}) %collective-permute-start.1) | collective-permute-done | bytes 262176 | tf_op jit(solution)/shard_map/ppermute | solution.py:53
  9.9 1.6 %collective-permute-start.3 = (f32[2,2,128,128]{3,2,1,0:T(8,128)S(1)}, f32[2,2,128,128]{3,2,1,0:T(8,128)S(1)}, u32[]{:S(2)}, u32[]{:S(2)}) collective-permute-start(f32[2,2,128,128]{3,2,1,0:T(8,128)S(1)} %shift_sum.2.refs_0_), channel_id=1, source_target_pairs={{0,4},{1,2},{2,1},{3,7},{4,0},{5,6},{6,5},{7,3},{8,12},{9,10},{10,... | collective-permute-start | bytes 786440 | tf_op jit(solution)/shard_map/ppermute | solution.py:53
  11.6 0.7 %collective-permute-done.4.refs_1_ = f32[2,2,128,128]{3,2,1,0:T(8,128)S(1)} collective-permute-done((f32[2,2,128,128]{3,2,1,0:T(8,128)S(1)}, f32[2,2,128,128]{3,2,1,0:T(8,128)S(1)}, u32[]{:S(2)}, u32[]{:S(2)}) %collective-permute-start.4) | collective-permute-done | bytes 262176 | tf_op jit(solution)/shard_map/ppermute | solution.py:53
  12.2 1.3 %sandwich.5.own_ref = f32[2,2,128,128]{3,2,1,0:T(8,128)S(1)} custom-call(s32[2,8]{1,0:T(2,128)S(1)} %compare_select_fusion.1.index_ref, bf16[2,8,2,128,128]{4,3,2,1,0:T(8,128)(2,1)S(1)} %get-tuple-element.11.right_ref, bf16[2,8,256,128]{3,2,1,0:T(8,128)(2,1)S(1)} %get-tuple-element.12.left_ref, f32[2,2,128,128]{3,2,1,0:T(8,128)S(1)} %get-tuple-element.14.refs_0_.imag_ref, ...), custom_call_target="tpu_custom_call" | custom-call | tf_op jit(solution)/shard_map/sandwich/pallas_call | solution.py:126
  13.5 0.9 %collective-permute-start.7 = (f32[2,2,128,128]{3,2,1,0:T(8,128)S(1)}, f32[2,2,128,128]{3,2,1,0:T(8,128)S(1)}, u32[]{:S(2)}, u32[]{:S(2)}) collective-permute-start(f32[2,2,128,128]{3,2,1,0:T(8,128)S(1)} %sandwich.5.own_ref), channel_id=1, source_target_pairs={{0,1},{1,0},{2,3},{3,2},{4,8},{5,9},{6,10},{7,11},{8,4},{9,5},{10,... | collective-permute-start | bytes 786440 | tf_op jit(solution)/shard_map/ppermute | solution.py:53
  14.4 0.7 %collective-permute-start.6 = (f32[2,2,128,128]{3,2,1,0:T(8,128)S(1)}, f32[2,2,128,128]{3,2,1,0:T(8,128)S(1)}, u32[]{:S(2)}, u32[]{:S(2)}) collective-permute-start(f32[2,2,128,128]{3,2,1,0:T(8,128)S(1)} %sandwich.5.own_ref), channel_id=1, source_target_pairs={{0,4},{1,5},{2,6},{3,7},{4,0},{5,1},{6,2},{7,3},{8,12},{9,13},{10,... | collective-permute-start | bytes 786440 | tf_op jit(solution)/shard_map/ppermute | solution.py:53
  15.1 2.2 %collective-permute-done.3.refs_2_ = f32[2,2,128,128]{3,2,1,0:T(8,128)S(1)} collective-permute-done((f32[2,2,128,128]{3,2,1,0:T(8,128)S(1)}, f32[2,2,128,128]{3,2,1,0:T(8,128)S(1)}, u32[]{:S(2)}, u32[]{:S(2)}) %collective-permute-start.3) | collective-permute-done | bytes 262176 | tf_op jit(solution)/shard_map/ppermute | solution.py:53
  17.3 1.3 %collective-permute-done.2.refs_1_ = f32[2,2,128,128]{3,2,1,0:T(8,128)S(1)} collective-permute-done((f32[2,2,128,128]{3,2,1,0:T(8,128)S(1)}, f32[2,2,128,128]{3,2,1,0:T(8,128)S(1)}, u32[]{:S(2)}, u32[]{:S(2)}) %collective-permute-start.2) | collective-permute-done | bytes 262176 | tf_op jit(solution)/shard_map/ppermute | solution.py:53
  18.6 1.3 %sandwich.4.sigma_ref = f32[2,2,128,128]{3,2,1,0:T(8,128)S(1)} custom-call(s32[2,8]{1,0:T(2,128)S(1)} %compare_select_fusion.1.index_ref, bf16[2,8,2,128,128]{4,3,2,1,0:T(8,128)(2,1)S(1)} %get-tuple-element.11.right_ref, bf16[2,8,256,128]{3,2,1,0:T(8,128)(2,1)S(1)} %get-tuple-element.12.left_ref, f32[2,2,128,128]{3,2,1,0:T(8,128)S(1)} %shift_sum.2.refs_0_, ...), custom_call_target="tpu_custom_call" | custom-call | tf_op jit(solution)/shard_map/sandwich/pallas_call | solution.py:126
  19.9 3.0 %collective-permute-done.7.two_ref = f32[2,2,128,128]{3,2,1,0:T(8,128)S(1)} collective-permute-done((f32[2,2,128,128]{3,2,1,0:T(8,128)S(1)}, f32[2,2,128,128]{3,2,1,0:T(8,128)S(1)}, u32[]{:S(2)}, u32[]{:S(2)}) %collective-permute-start.7) | collective-permute-done | bytes 262176 | tf_op jit(solution)/shard_map/ppermute | solution.py:53
  22.9 0.8 %dyson.2 = (f32[2,2,128,128]{3,2,1,0:T(8,128)S(1)}, f32[2,2,128,128]{3,2,1,0:T(8,128)S(1)}) custom-call(f32[2,6]{1,0:T(2,128)S(1)} %select_reduce_fusion.weight_ref, f32[2,2,128,128]{3,2,1,0:T(8,128)S(1)} %sandwich.4.sigma_ref, f32[2,2,128,128]{3,2,1,0:T(8,128)S(1)} %sandwich.5.own_ref, f32[2,2,128,128]{3,2,1,0:T(8,128)S(1)} %collective-permute-done.6.one_ref, ...), custom_call_target="tpu_custom_call" | custom-call | tf_op jit(solution)/shard_map/dyson/pallas_call | solution.py:230
  23.7 1.0 %collective-permute-start.9 = (f32[2,2,128,128]{3,2,1,0:T(8,128)S(1)}, f32[2,2,128,128]{3,2,1,0:T(8,128)S(1)}, u32[]{:S(2)}, u32[]{:S(2)}) collective-permute-start(f32[2,2,128,128]{3,2,1,0:T(8,128)S(1)} %get-tuple-element.15.own_ref), channel_id=1, source_target_pairs={{0,1},{1,0},{2,3},{3,2},{4,8},{5,9},{6,10},{7,11},{8,4},{9,5},{10,... | collective-permute-start | bytes 786440 | tf_op jit(solution)/shard_map/ppermute | solution.py:53
  24.7 1.1 %collective-permute-start.13 = (f32[2,2,128,128]{3,2,1,0:T(8,128)S(1)}, f32[2,2,128,128]{3,2,1,0:T(8,128)S(1)}, u32[]{:S(2)}, u32[]{:S(2)}) collective-permute-start(f32[2,2,128,128]{3,2,1,0:T(8,128)S(1)} %get-tuple-element.16.refs_0_), channel_id=1, source_target_pairs={{0,4},{1,2},{2,1},{3,7},{4,0},{5,6},{6,5},{7,3},{8,12},{9,10},{10,... | collective-permute-start | bytes 786440 | tf_op jit(solution)/shard_map/ppermute | solution.py:53
  25.8 0.9 %collective-permute-start.12 = (f32[2,2,128,128]{3,2,1,0:T(8,128)S(1)}, f32[2,2,128,128]{3,2,1,0:T(8,128)S(1)}, u32[]{:S(2)}, u32[]{:S(2)}) collective-permute-start(f32[2,2,128,128]{3,2,1,0:T(8,128)S(1)} %get-tuple-element.16.refs_0_), channel_id=1, source_target_pairs={{0,1},{1,0},{2,3},{3,2},{4,5},{5,4},{6,7},{7,6},{8,9},{9,8},{10,11... | collective-permute-start | bytes 786440 | tf_op jit(solution)/shard_map/ppermute | solution.py:53
  26.7 5.5 %collective-permute-done.9.two_ref = f32[2,2,128,128]{3,2,1,0:T(8,128)S(1)} collective-permute-done((f32[2,2,128,128]{3,2,1,0:T(8,128)S(1)}, f32[2,2,128,128]{3,2,1,0:T(8,128)S(1)}, u32[]{:S(2)}, u32[]{:S(2)}) %collective-permute-start.9) | collective-permute-done | bytes 262176 | tf_op jit(solution)/shard_map/ppermute | solution.py:53
  32.4 0.9 %collective-permute-start.11 = (f32[2,2,128,128]{3,2,1,0:T(8,128)S(1)}, f32[2,2,128,128]{3,2,1,0:T(8,128)S(1)}, u32[]{:S(2)}, u32[]{:S(2)}) collective-permute-start(f32[2,2,128,128]{3,2,1,0:T(8,128)S(1)} %shift_sum.3.refs_0_), channel_id=1, source_target_pairs={{0,4},{1,2},{2,1},{3,7},{4,0},{5,6},{6,5},{7,3},{8,12},{9,10},{10,... | collective-permute-start | bytes 786440 | tf_op jit(solution)/shard_map/ppermute | solution.py:53
  33.3 0.6 %collective-permute-done.13.refs_2_ = f32[2,2,128,128]{3,2,1,0:T(8,128)S(1)} collective-permute-done((f32[2,2,128,128]{3,2,1,0:T(8,128)S(1)}, f32[2,2,128,128]{3,2,1,0:T(8,128)S(1)}, u32[]{:S(2)}, u32[]{:S(2)}) %collective-permute-start.13) | collective-permute-done | bytes 262176 | tf_op jit(solution)/shard_map/ppermute | solution.py:53
  33.9 1.1 %collective-permute-done.12.refs_1_ = f32[2,2,128,128]{3,2,1,0:T(8,128)S(1)} collective-permute-done((f32[2,2,128,128]{3,2,1,0:T(8,128)S(1)}, f32[2,2,128,128]{3,2,1,0:T(8,128)S(1)}, u32[]{:S(2)}, u32[]{:S(2)}) %collective-permute-start.12) | collective-permute-done | bytes 262176 | tf_op jit(solution)/shard_map/ppermute | solution.py:53
  35.0 1.3 %sandwich.7.own_ref = f32[2,2,128,128]{3,2,1,0:T(8,128)S(1)} custom-call(s32[2,8]{1,0:T(2,128)S(1)} %compare_select_fusion.1.index_ref, bf16[2,8,2,128,128]{4,3,2,1,0:T(8,128)(2,1)S(1)} %get-tuple-element.11.right_ref, bf16[2,8,256,128]{3,2,1,0:T(8,128)(2,1)S(1)} %get-tuple-element.12.left_ref, f32[2,2,128,128]{3,2,1,0:T(8,128)S(1)} %get-tuple-element.16.refs_0_, ...), custom_call_target="tpu_custom_call" | custom-call | tf_op jit(solution)/shard_map/sandwich/pallas_call | solution.py:126
  36.5 2.6 %collective-permute-done.11.refs_2_ = f32[2,2,128,128]{3,2,1,0:T(8,128)S(1)} collective-permute-done((f32[2,2,128,128]{3,2,1,0:T(8,128)S(1)}, f32[2,2,128,128]{3,2,1,0:T(8,128)S(1)}, u32[]{:S(2)}, u32[]{:S(2)}) %collective-permute-start.11) | collective-permute-done | bytes 262176 | tf_op jit(solution)/shard_map/ppermute | solution.py:53
  39.1 0.8 %collective-permute-done.10.refs_1_ = f32[2,2,128,128]{3,2,1,0:T(8,128)S(1)} collective-permute-done((f32[2,2,128,128]{3,2,1,0:T(8,128)S(1)}, f32[2,2,128,128]{3,2,1,0:T(8,128)S(1)}, u32[]{:S(2)}, u32[]{:S(2)}) %collective-permute-start.10) | collective-permute-done | bytes 262176 | tf_op jit(solution)/shard_map/ppermute | solution.py:53
  39.9 1.3 %sandwich.6.sigma_ref = f32[2,2,128,128]{3,2,1,0:T(8,128)S(1)} custom-call(s32[2,8]{1,0:T(2,128)S(1)} %compare_select_fusion.1.index_ref, bf16[2,8,2,128,128]{4,3,2,1,0:T(8,128)(2,1)S(1)} %get-tuple-element.11.right_ref, bf16[2,8,256,128]{3,2,1,0:T(8,128)(2,1)S(1)} %get-tuple-element.12.left_ref, f32[2,2,128,128]{3,2,1,0:T(8,128)S(1)} %shift_sum.3.refs_0_, ...), custom_call_target="tpu_custom_call" | custom-call | tf_op jit(solution)/shard_map/sandwich/pallas_call | solution.py:126
  41.2 3.0 %collective-permute-done.15.two_ref = f32[2,2,128,128]{3,2,1,0:T(8,128)S(1)} collective-permute-done((f32[2,2,128,128]{3,2,1,0:T(8,128)S(1)}, f32[2,2,128,128]{3,2,1,0:T(8,128)S(1)}, u32[]{:S(2)}, u32[]{:S(2)}) %collective-permute-start.15) | collective-permute-done | bytes 262176 | tf_op jit(solution)/shard_map/ppermute | solution.py:53
  44.2 1.5 %dyson.3 = f32[2,2,2,128,128]{4,3,2,1,0:T(8,128)} custom-call(f32[2,6]{1,0:T(2,128)S(1)} %select_reduce_fusion.weight_ref, f32[2,2,128,128]{3,2,1,0:T(8,128)S(1)} %sandwich.6.sigma_ref, f32[2,2,128,128]{3,2,1,0:T(8,128)S(1)} %sandwich.7.own_ref, f32[2,2,128,128]{3,2,1,0:T(8,128)S(1)} %collective-permute-done.14.one_ref, ...), custom_call_target="tpu_custom_call" | custom-call | tf_op jit(solution)/shard_map/dyson/pallas_call | solution.py:230
  (28 shorter events, 0.9 us)
Async XLA Ops:
  1.1 8.7 %collective-permute-start.1 = (f32[2,2,128,128]{3,2,1,0:T(8,128)S(1)}, f32[2,2,128,128]{3,2,1,0:T(8,128)S(1)}, u32[]{:S(2)}, u32[]{:S(2)}) collective-permute-start(f32[2,2,128,128]{3,2,1,0:T(8,128)S(1)} %get-tuple-element.13.own_ref.real_ref), channel_id=1, source_target_pairs={{0,1},{1,0},{2,3},{3,2},{4,8},{5,9},{6,10},{7,11},{8,4},{9,5},{10,... | collective-permute-start | bytes 786440 | tf_op jit(solution)/shard_map/ppermute | solution.py:53
  2.0 7.7 %collective-permute-start = (f32[2,2,128,128]{3,2,1,0:T(8,128)S(1)}, f32[2,2,128,128]{3,2,1,0:T(8,128)S(1)}, u32[]{:S(2)}, u32[]{:S(2)}) collective-permute-start(f32[2,2,128,128]{3,2,1,0:T(8,128)S(1)} %get-tuple-element.13.own_ref.real_ref), channel_id=1, source_target_pairs={{0,4},{1,5},{2,6},{3,7},{4,0},{5,1},{6,2},{7,3},{8,12},{9,13},{10,... | collective-permute-start | bytes 786440 | tf_op jit(solution)/shard_map/ppermute | solution.py:53
  2.7 8.8 %collective-permute-start.5 = (f32[2,2,128,128]{3,2,1,0:T(8,128)S(1)}, f32[2,2,128,128]{3,2,1,0:T(8,128)S(1)}, u32[]{:S(2)}, u32[]{:S(2)}) collective-permute-start(f32[2,2,128,128]{3,2,1,0:T(8,128)S(1)} %get-tuple-element.14.refs_0_.imag_ref), channel_id=1, source_target_pairs={{0,4},{1,2},{2,1},{3,7},{4,0},{5,6},{6,5},{7,3},{8,12},{9,10},{10,... | collective-permute-start | bytes 786440 | tf_op jit(solution)/shard_map/ppermute | solution.py:53
  4.3 7.9 %collective-permute-start.4 = (f32[2,2,128,128]{3,2,1,0:T(8,128)S(1)}, f32[2,2,128,128]{3,2,1,0:T(8,128)S(1)}, u32[]{:S(2)}, u32[]{:S(2)}) collective-permute-start(f32[2,2,128,128]{3,2,1,0:T(8,128)S(1)} %get-tuple-element.14.refs_0_.imag_ref), channel_id=1, source_target_pairs={{0,1},{1,0},{2,3},{3,2},{4,5},{5,4},{6,7},{7,6},{8,9},{9,8},{10,11... | collective-permute-start | bytes 786440 | tf_op jit(solution)/shard_map/ppermute | solution.py:53
  4.4 0.7 %copy-start.2 = (f32[4]{0:T(128)S(1)}, f32[4]{0:T(128)}, u32[]{:S(2)}) copy-start(f32[4]{0:T(128)} %param.9) | copy-start | bytes 52
  4.4 0.7 %copy-start.3 = (s32[4]{0:T(128)S(1)}, s32[4]{0:T(128)}, u32[]{:S(2)}) copy-start(s32[4]{0:T(128)} %param.8) | copy-start | bytes 52
  5.2 1.2 %copy-start = (f32[2,8,128,128]{3,2,1,0:T(8,128)S(1)}, f32[2,8,128,128]{3,2,1,0:T(8,128)}, u32[]{:S(2)}) copy-start(f32[2,8,128,128]{3,2,1,0:T(8,128)} %grad_ref.1) | copy-start | bytes 3145732
  6.4 0.7 %copy-start.1 = (s32[2,8]{1,0:T(2,128)S(1)}, s32[2,8]{1,0:T(2,128)}, u32[]{:S(2)}) copy-start(s32[2,8]{1,0:T(2,128)} %param.7) | copy-start | bytes 196
  9.9 7.4 %collective-permute-start.3 = (f32[2,2,128,128]{3,2,1,0:T(8,128)S(1)}, f32[2,2,128,128]{3,2,1,0:T(8,128)S(1)}, u32[]{:S(2)}, u32[]{:S(2)}) collective-permute-start(f32[2,2,128,128]{3,2,1,0:T(8,128)S(1)} %shift_sum.2.refs_0_), channel_id=1, source_target_pairs={{0,4},{1,2},{2,1},{3,7},{4,0},{5,6},{6,5},{7,3},{8,12},{9,10},{10,... | collective-permute-start | bytes 786440 | tf_op jit(solution)/shard_map/ppermute | solution.py:53
  11.6 7.1 %collective-permute-start.2 = (f32[2,2,128,128]{3,2,1,0:T(8,128)S(1)}, f32[2,2,128,128]{3,2,1,0:T(8,128)S(1)}, u32[]{:S(2)}, u32[]{:S(2)}) collective-permute-start(f32[2,2,128,128]{3,2,1,0:T(8,128)S(1)} %shift_sum.2.refs_0_), channel_id=1, source_target_pairs={{0,1},{1,0},{2,3},{3,2},{4,5},{5,4},{6,7},{7,6},{8,9},{9,8},{10,11... | collective-permute-start | bytes 786440 | tf_op jit(solution)/shard_map/ppermute | solution.py:53
  13.5 9.4 %collective-permute-start.7 = (f32[2,2,128,128]{3,2,1,0:T(8,128)S(1)}, f32[2,2,128,128]{3,2,1,0:T(8,128)S(1)}, u32[]{:S(2)}, u32[]{:S(2)}) collective-permute-start(f32[2,2,128,128]{3,2,1,0:T(8,128)S(1)} %sandwich.5.own_ref), channel_id=1, source_target_pairs={{0,1},{1,0},{2,3},{3,2},{4,8},{5,9},{6,10},{7,11},{8,4},{9,5},{10,... | collective-permute-start | bytes 786440 | tf_op jit(solution)/shard_map/ppermute | solution.py:53
  14.4 8.5 %collective-permute-start.6 = (f32[2,2,128,128]{3,2,1,0:T(8,128)S(1)}, f32[2,2,128,128]{3,2,1,0:T(8,128)S(1)}, u32[]{:S(2)}, u32[]{:S(2)}) collective-permute-start(f32[2,2,128,128]{3,2,1,0:T(8,128)S(1)} %sandwich.5.own_ref), channel_id=1, source_target_pairs={{0,4},{1,5},{2,6},{3,7},{4,0},{5,1},{6,2},{7,3},{8,12},{9,13},{10,... | collective-permute-start | bytes 786440 | tf_op jit(solution)/shard_map/ppermute | solution.py:53
  23.7 8.5 %collective-permute-start.9 = (f32[2,2,128,128]{3,2,1,0:T(8,128)S(1)}, f32[2,2,128,128]{3,2,1,0:T(8,128)S(1)}, u32[]{:S(2)}, u32[]{:S(2)}) collective-permute-start(f32[2,2,128,128]{3,2,1,0:T(8,128)S(1)} %get-tuple-element.15.own_ref), channel_id=1, source_target_pairs={{0,1},{1,0},{2,3},{3,2},{4,8},{5,9},{6,10},{7,11},{8,4},{9,5},{10,... | collective-permute-start | bytes 786440 | tf_op jit(solution)/shard_map/ppermute | solution.py:53
  24.7 7.5 %collective-permute-start.8 = (f32[2,2,128,128]{3,2,1,0:T(8,128)S(1)}, f32[2,2,128,128]{3,2,1,0:T(8,128)S(1)}, u32[]{:S(2)}, u32[]{:S(2)}) collective-permute-start(f32[2,2,128,128]{3,2,1,0:T(8,128)S(1)} %get-tuple-element.15.own_ref), channel_id=1, source_target_pairs={{0,4},{1,5},{2,6},{3,7},{4,0},{5,1},{6,2},{7,3},{8,12},{9,13},{10,... | collective-permute-start | bytes 786440 | tf_op jit(solution)/shard_map/ppermute | solution.py:53
  24.7 9.2 %collective-permute-start.13 = (f32[2,2,128,128]{3,2,1,0:T(8,128)S(1)}, f32[2,2,128,128]{3,2,1,0:T(8,128)S(1)}, u32[]{:S(2)}, u32[]{:S(2)}) collective-permute-start(f32[2,2,128,128]{3,2,1,0:T(8,128)S(1)} %get-tuple-element.16.refs_0_), channel_id=1, source_target_pairs={{0,4},{1,2},{2,1},{3,7},{4,0},{5,6},{6,5},{7,3},{8,12},{9,10},{10,... | collective-permute-start | bytes 786440 | tf_op jit(solution)/shard_map/ppermute | solution.py:53
  25.8 9.2 %collective-permute-start.12 = (f32[2,2,128,128]{3,2,1,0:T(8,128)S(1)}, f32[2,2,128,128]{3,2,1,0:T(8,128)S(1)}, u32[]{:S(2)}, u32[]{:S(2)}) collective-permute-start(f32[2,2,128,128]{3,2,1,0:T(8,128)S(1)} %get-tuple-element.16.refs_0_), channel_id=1, source_target_pairs={{0,1},{1,0},{2,3},{3,2},{4,5},{5,4},{6,7},{7,6},{8,9},{9,8},{10,11... | collective-permute-start | bytes 786440 | tf_op jit(solution)/shard_map/ppermute | solution.py:53
  32.4 6.7 %collective-permute-start.11 = (f32[2,2,128,128]{3,2,1,0:T(8,128)S(1)}, f32[2,2,128,128]{3,2,1,0:T(8,128)S(1)}, u32[]{:S(2)}, u32[]{:S(2)}) collective-permute-start(f32[2,2,128,128]{3,2,1,0:T(8,128)S(1)} %shift_sum.3.refs_0_), channel_id=1, source_target_pairs={{0,4},{1,2},{2,1},{3,7},{4,0},{5,6},{6,5},{7,3},{8,12},{9,10},{10,... | collective-permute-start | bytes 786440 | tf_op jit(solution)/shard_map/ppermute | solution.py:53
  33.3 6.6 %collective-permute-start.10 = (f32[2,2,128,128]{3,2,1,0:T(8,128)S(1)}, f32[2,2,128,128]{3,2,1,0:T(8,128)S(1)}, u32[]{:S(2)}, u32[]{:S(2)}) collective-permute-start(f32[2,2,128,128]{3,2,1,0:T(8,128)S(1)} %shift_sum.3.refs_0_), channel_id=1, source_target_pairs={{0,1},{1,0},{2,3},{3,2},{4,5},{5,4},{6,7},{7,6},{8,9},{9,8},{10,11... | collective-permute-start | bytes 786440 | tf_op jit(solution)/shard_map/ppermute | solution.py:53
  36.3 7.9 %collective-permute-start.15 = (f32[2,2,128,128]{3,2,1,0:T(8,128)S(1)}, f32[2,2,128,128]{3,2,1,0:T(8,128)S(1)}, u32[]{:S(2)}, u32[]{:S(2)}) collective-permute-start(f32[2,2,128,128]{3,2,1,0:T(8,128)S(1)} %sandwich.7.own_ref), channel_id=1, source_target_pairs={{0,1},{1,0},{2,3},{3,2},{4,8},{5,9},{6,10},{7,11},{8,4},{9,5},{10,... | collective-permute-start | bytes 786440 | tf_op jit(solution)/shard_map/ppermute | solution.py:53
  36.4 7.8 %collective-permute-start.14 = (f32[2,2,128,128]{3,2,1,0:T(8,128)S(1)}, f32[2,2,128,128]{3,2,1,0:T(8,128)S(1)}, u32[]{:S(2)}, u32[]{:S(2)}) collective-permute-start(f32[2,2,128,128]{3,2,1,0:T(8,128)S(1)} %sandwich.7.own_ref), channel_id=1, source_target_pairs={{0,4},{1,5},{2,6},{3,7},{4,0},{5,1},{6,2},{7,3},{8,12},{9,13},{10,... | collective-permute-start | bytes 786440 | tf_op jit(solution)/shard_map/ppermute | solution.py:53
